TPU v7x, 32 devices: a whole 2x2x4 slice. The times are simulated.
32 devices in a mesh: groups: 2 (over x), seq: 16 (over z, y, core).
Axes of the slice: x: 2, y: 2, z: 4, core: 2. Of those that a mesh axis runs over, the one named last changes fastest.
Arguments:
- queries: bfloat16 [4096, 2048], P(('groups', 'seq')), parts along dimension 0, may hold values from -6 to 6
- keys: bfloat16 [4096, 2048], P(('groups', 'seq')), parts along dimension 0, may hold values from -6 to 6
- values: bfloat16 [4096, 2048], P(('groups', 'seq')), parts along dimension 0, may hold values from -6 to 6
- gain_q: float32 [128], replicated, may hold values from 0.5 to 1.5
- gain_k: float32 [128], replicated, may hold values from 0.5 to 1.5
- w_latent: bfloat16 [2048, 512], replicated, may hold values from -0.125 to 0.125
- w_temporal: bfloat16 [3, 512, 512], replicated, may hold values from -0.15625 to 0.15625
- w_decode: bfloat16 [512, 512], replicated, may hold values from -0.25 to 0.25
Outputs:
- attention: bfloat16 [4096, 2048], P(('groups', 'seq')), parts along dimension 0
- decoded: bfloat16 [4096, 512], P(('groups', 'seq')), parts along dimension 0
There are 2 independent parts, one for each index of `groups`. A program takes and returns all parts, laid end to end along the dimension named above; an argument that names none is the same for every part. Nothing has to cross between parts.
All inputs are finite; a program needn't handle non-finite values.
Results may differ from a plain program's by a relative error of at most 0.012.
The roundings to bfloat16 on the way count: a program that leaves them out, or rounds other values in their place, can miss the bound.
Values may be sent and summed in bfloat16 or wider, within the bound.
No kernel may reach another device: no remote copies, remote signals or barrier semaphores. Data moves between devices by JAX's collectives and lax.ppermute only.
A program may use at most 128 MiB of HBM per device.

v0:
```python
import math

import jax
import jax.numpy as jnp
from jax import lax
from jax.sharding import PartitionSpec as P

HEADS = 16
HD = 128


def passed_along(shard, axis, by):
    peers = lax.axis_size(axis)
    pairs = [(i, i + by) for i in range(peers) if 0 <= i + by < peers]
    return lax.ppermute(shard, axis, pairs)


def head_norm(x, gain):
    rows = x.shape[0]
    x = x.astype(jnp.float32).reshape(rows, HEADS, HD)
    x = x * lax.rsqrt(jnp.mean(x * x, axis=-1, keepdims=True) + 1e-06) * gain
    return x.astype(jnp.bfloat16).reshape(rows, HEADS * HD)


def attend(q_head, k_head, v_head):
    count = q_head.shape[0]
    block = 512
    scale = 1.0 / math.sqrt(HD)

    def one_block(qb):
        scores = jnp.dot(qb, k_head.T, preferred_element_type=jnp.float32) * scale
        top = jnp.max(scores, axis=-1, keepdims=True)
        expo = jnp.exp(scores - top)
        total = jnp.sum(expo, axis=-1, keepdims=True)
        out = jnp.dot(expo.astype(jnp.bfloat16), v_head, preferred_element_type=jnp.float32)
        return (out / total).astype(jnp.bfloat16)

    outs = lax.map(one_block, q_head.reshape(count // block, block, HD))
    return outs.reshape(count, HD)


def body(queries, keys, values, gain_q, gain_k, w_latent, w_temporal, w_decode):
    devices = lax.axis_size("seq")
    copies = devices // HEADS
    rows = queries.shape[0]
    q_norm = head_norm(queries, gain_q)
    k_norm = head_norm(keys, gain_k)

    def spread(x):
        wide = jnp.broadcast_to(x.reshape(rows, HEADS, 1, HD), (rows, HEADS, copies, HD))
        return wide.reshape(rows, devices * HD)

    stacked = jnp.stack([spread(q_norm), spread(k_norm), spread(values)])
    got = lax.all_to_all(stacked, "seq", split_axis=2, concat_axis=1, tiled=True)
    share = lax.axis_index("seq") % copies
    span = rows * HEADS
    q_head = lax.dynamic_slice_in_dim(got[0], share * span, span, 0)
    out = attend(q_head, got[1], got[2])
    places = (jnp.arange(copies, dtype=jnp.int32) == share)[:, None, None]
    placed = jnp.where(places, out[None], jnp.zeros_like(out)[None]).reshape(devices * rows, HD)
    back = lax.all_to_all(placed, "seq", split_axis=0, concat_axis=1, tiled=True)
    back = back.reshape(rows, HEADS, copies, HD).astype(jnp.float32)
    attention = jnp.sum(back, axis=2).astype(jnp.bfloat16).reshape(rows, HEADS * HD)
    latent = jnp.dot(attention, w_latent, preferred_element_type=jnp.float32).astype(jnp.bfloat16)
    earlier_one = passed_along(latent, "seq", 1)
    earlier_two = passed_along(latent, "seq", 2)
    state = jnp.dot(latent, w_temporal[0], preferred_element_type=jnp.float32)
    state = state + jnp.dot(earlier_one, w_temporal[1], preferred_element_type=jnp.float32)
    state = state + jnp.dot(earlier_two, w_temporal[2], preferred_element_type=jnp.float32)
    decoded = jnp.dot(
        jax.nn.silu(state).astype(jnp.bfloat16), w_decode, preferred_element_type=jnp.float32
    )
    return (attention, decoded.astype(jnp.bfloat16))


def solution(mesh):
    in_specs = (
        P(("groups", "seq"), None),
        P(("groups", "seq"), None),
        P(("groups", "seq"), None),
        P(),
        P(),
        P(),
        P(),
        P(),
    )
    out_specs = (P(("groups", "seq"), None), P(("groups", "seq"), None))
    return jax.shard_map(body, mesh=mesh, in_specs=in_specs, out_specs=out_specs, check_vma=False)
```

profile of v0, /device:TPU:8, one launch (start us, length us, event | category | flops | bytes accessed | tf_op | source)
XLA Modules:
  0.0 128.0 jit_solution(3480380868804211531)
XLA Ops:
  0.6 0.0 copy-start
  0.6 1.3 %fusion.23 = f32[16,8,16,128]{3,1,2,0:T(8,128)S(1)} fusion(bf16[128,2048]{1,0:T(8,128)(2,1)} %param.10), kind=kLoop, calls=%fused_computation.25 | loop fusion | flops 524288 | bytes 1572864
  1.9 0.2 copy.42
  2.1 0.3 reduce_sum.28
  2.5 0.1 copy.32
  2.5 0.1 copy.33
  2.7 0.0 copy-start.5
  2.7 0.0 copy-start.6
  2.7 1.2 fusion.26
  3.9 0.2 copy.44
  4.1 0.3 reduce_sum.32
  4.4 0.0 copy-start.1
  4.4 0.0 copy-start.2
  4.4 0.1 copy.34
  4.5 0.1 copy.35
  4.6 0.0 copy-done.5
  4.6 0.0 copy-done.6
  4.7 0.3 mul.74
  5.0 0.3 mul.83
  5.3 0.1 copy-done.1
  5.5 0.2 copy-done.2
  5.6 0.0 copy-start.4
  5.6 1.1 fusion.29
  6.7 0.0 copy-done.4
  6.7 1.3 %pad_maximum_fusion = bf16[3,128,2048]{2,1,0:T(8,128)(2,1)} fusion(bf16[1,128,2048]{2,1,0:T(8,128)(2,1)S(1)} %bitcast.82, bf16[1,128,2048]{2,1,0:T(8,128)(2,1)S(1)} %get-tuple-element.51, bf16[1,128,2048]{2,1,0:T(8,128)(2,1)S(1)} %get-tuple-element.52), kind=kLoop, calls=%fused_computation.16 | loop fusion | flops 1572864 | bytes 3145728 | tf_op jit(solution)/shard_map/stack | solution.py:53
  8.1 4.1 %copy.36 = bf16[3,128,2048]{1,0,2:T(4,128)(2,1)} copy(bf16[3,128,2048]{2,1,0:T(8,128)(2,1)} %pad_maximum_fusion) | data formatting | bytes 3145728 | tf_op jit(solution)/shard_map/stack | solution.py:53
  12.2 6.3 %all-to-all-start = ((bf16[3,128,2048]{1,0,2:T(4,128)(2,1)}), bf16[3,128,2048]{1,0,2:T(4,128)(2,1)}, u32[]{:S(2)}, u32[]{:S(2)}) async-start(bf16[3,128,2048]{1,0,2:T(4,128)(2,1)} %copy.36), calls=%async_computation | async-start | bytes 4194304 | tf_op jit(solution)/shard_map/all_to_all | solution.py:54
  18.5 45.9 %all-to-all-done = bf16[3,128,2048]{1,0,2:T(4,128)(2,1)} async-done(((bf16[3,128,2048]{1,0,2:T(4,128)(2,1)}), bf16[3,128,2048]{1,0,2:T(4,128)(2,1)}, u32[]{:S(2)}, u32[]{:S(2)}) %all-to-all-start) | async-done | bytes 1572896 | tf_op jit(solution)/shard_map/all_to_all | solution.py:54
  64.4 7.3 %fusion.44 = (bf16[1,16,128,128]{2,0,3,1:T(2,128)(2,1)}, bf16[1,16,128,128]{2,0,3,1:T(2,128)(2,1)}, bf16[1,16,128,128]{2,0,3,1:T(2,128)(2,1)}) fusion(bf16[3,16,128,128]{2,0,3,1:T(4,128)(2,1)} %bitcast.8), kind=kLoop, calls=%fused_computation.47 | loop fusion | bytes 3145728 | tf_op jit(solution)/shard_map/slice | solution.py:58
  71.6 2.4 %copy.38 = bf16[1,16,128,128]{3,2,1,0:T(8,128)(2,1)S(1)} copy(bf16[1,16,128,128]{2,0,3,1:T(2,128)(2,1)} %get-tuple-element.49) | data formatting | bytes 1048576 | tf_op jit(solution)/shard_map/slice | solution.py:58
  74.0 3.5 %copy.39 = bf16[1,16,128,128]{3,2,1,0:T(8,128)(2,1)} copy(bf16[1,16,128,128]{2,0,3,1:T(2,128)(2,1)} %get-tuple-element.48) | data formatting | bytes 1048576 | tf_op jit(solution)/shard_map/slice | solution.py:58
  77.6 2.4 %copy.37 = bf16[1,16,128,128]{3,2,1,0:T(8,128)(2,1)S(1)} copy(bf16[1,16,128,128]{2,0,3,1:T(2,128)(2,1)} %get-tuple-element.50) | data formatting | bytes 1048576 | tf_op jit(solution)/shard_map/slice | solution.py:57
  80.0 13.4 %while.10 = (s32[]{:T(128)}, bf16[4,512,128]{2,1,0:T(8,128)(2,1)}, bf16[4,512,128]{2,1,0:T(8,128)(2,1)S(1)}, bf16[2048,128]{1,0:T(8,128)(2,1)S(1)}, bf16[2048,128]{1,0:T(8,128)(2,1)}, /*index=5*/s32[]{:T(128)}) while((s32[]{:T(128)}, bf16[4,512,128]{2,1,0:T(8,128)(2,1)}, bf16[4,512,128]{2,1,0:T(8,128)(2,1)S(1)}, ...), condition=%wide.region_5.6_spmd, body=%wide.region_2.5_spmd.sunk | while | flops 545389568 | bytes 16001637 | solution.py:38
  80.0 0.8 multiply_reduce_fusion.2
  80.8 0.0 copy-start.3
  80.8 0.8 fusion.61
  81.6 0.2 copy-done.3
  81.8 1.5 %fusion.62 = bf16[4,512,128]{2,1,0:T(8,128)(2,1)} fusion(bf16[4,512,128]{2,1,0:T(8,128)(2,1)} %get-tuple-element.95, s32[]{:T(128)} %get-tuple-element.94, bf16[2048,128]{1,0:T(8,128)(2,1)S(1)} %copy-done.3, f32[512,2048]{1,0:T(8,128)S(1)} %get-tuple-element.86, f32[512]{0:T(512)S(1)} %get-tuple-element.87, f32[512]{0:T(512)S(1)} %fusion.61), kind=kOutput, calls=%fused_computation.10.clone.1 | convolution fusion | flops 271712256 | bytes 4854272 | tf_op jit(solution)/shard_map/while/body/eval_jaxpr/dot_general | solution.py:35
  83.3 0.8 multiply_reduce_fusion.2
  84.1 0.8 fusion.61
  84.9 0.2 copy-done.3
  85.1 1.5 %fusion.62 = bf16[4,512,128]{2,1,0:T(8,128)(2,1)} fusion(bf16[4,512,128]{2,1,0:T(8,128)(2,1)} %get-tuple-element.95, s32[]{:T(128)} %get-tuple-element.94, bf16[2048,128]{1,0:T(8,128)(2,1)S(1)} %copy-done.3, f32[512,2048]{1,0:T(8,128)S(1)} %get-tuple-element.86, f32[512]{0:T(512)S(1)} %get-tuple-element.87, f32[512]{0:T(512)S(1)} %fusion.61), kind=kOutput, calls=%fused_computation.10.clone.1 | convolution fusion | flops 271712256 | bytes 4854272 | tf_op jit(solution)/shard_map/while/body/eval_jaxpr/dot_general | solution.py:35
  86.6 0.8 multiply_reduce_fusion.2
  87.4 0.8 fusion.61
  88.2 0.2 copy-done.3
  88.5 1.5 %fusion.62 = bf16[4,512,128]{2,1,0:T(8,128)(2,1)} fusion(bf16[4,512,128]{2,1,0:T(8,128)(2,1)} %get-tuple-element.95, s32[]{:T(128)} %get-tuple-element.94, bf16[2048,128]{1,0:T(8,128)(2,1)S(1)} %copy-done.3, f32[512,2048]{1,0:T(8,128)S(1)} %get-tuple-element.86, f32[512]{0:T(512)S(1)} %get-tuple-element.87, f32[512]{0:T(512)S(1)} %fusion.61), kind=kOutput, calls=%fused_computation.10.clone.1 | convolution fusion | flops 271712256 | bytes 4854272 | tf_op jit(solution)/shard_map/while/body/eval_jaxpr/dot_general | solution.py:35
  90.0 0.8 multiply_reduce_fusion.2
  90.8 0.8 fusion.61
  91.6 0.2 copy-done.3
  91.8 1.5 %fusion.62 = bf16[4,512,128]{2,1,0:T(8,128)(2,1)} fusion(bf16[4,512,128]{2,1,0:T(8,128)(2,1)} %get-tuple-element.95, s32[]{:T(128)} %get-tuple-element.94, bf16[2048,128]{1,0:T(8,128)(2,1)S(1)} %copy-done.3, f32[512,2048]{1,0:T(8,128)S(1)} %get-tuple-element.86, f32[512]{0:T(512)S(1)} %get-tuple-element.87, f32[512]{0:T(512)S(1)} %fusion.61), kind=kOutput, calls=%fused_computation.10.clone.1 | convolution fusion | flops 271712256 | bytes 4854272 | tf_op jit(solution)/shard_map/while/body/eval_jaxpr/dot_general | solution.py:35
  93.3 20.2 %all_to_all.25 = bf16[16,128,128]{2,1,0:T(8,128)(2,1)S(1)} all-to-all(bf16[16,128,128]{2,1,0:T(8,128)(2,1)} %bitcast.13), channel_id=1, replica_groups=mesh['groups'=2,'seq'=16] {'seq'}, dimensions={0} | all-to-all | bytes 1048576 | tf_op jit(solution)/shard_map/all_to_all | solution.py:61
  113.5 0.3 copy.40
  113.8 0.0 copy-done
  113.8 0.5 convolution_convert_fusion.1
  114.3 0.0 copy-start.7
  114.3 2.7 %collective-permute-start = (bf16[128,512]{1,0:T(8,128)(2,1)S(1)}, bf16[128,512]{1,0:T(8,128)(2,1)S(1)}, u32[]{:S(2)}, u32[]{:S(2)}) collective-permute-start(bf16[128,512]{1,0:T(8,128)(2,1)S(1)} %convolution_convert_fusion.1), channel_id=1, source_target_pairs={{0,1},{1,2},{2,3},{3,4},{4,5},{5,6},{6,7},{7,8},{8,9},{9,10},{10,1... | collective-permute-start | bytes 393224 | tf_op jit(solution)/shard_map/ppermute | solution.py:15
  117.0 2.8 %collective-permute-start.1 = (bf16[128,512]{1,0:T(8,128)(2,1)S(1)}, bf16[128,512]{1,0:T(8,128)(2,1)S(1)}, u32[]{:S(2)}, u32[]{:S(2)}) collective-permute-start(bf16[128,512]{1,0:T(8,128)(2,1)S(1)} %convolution_convert_fusion.1), channel_id=1, source_target_pairs={{0,2},{1,3},{2,4},{3,5},{4,6},{5,7},{6,8},{7,9},{8,10},{9,11},{10,... | collective-permute-start | bytes 393224 | tf_op jit(solution)/shard_map/ppermute | solution.py:15
  119.8 1.0 copy.41
  120.8 1.3 fusion.33
  122.1 0.0 collective-permute-done
  122.1 1.3 convolution_add_fusion.1
  123.4 2.5 %collective-permute-done.1 = bf16[128,512]{1,0:T(8,128)(2,1)S(1)} collective-permute-done((bf16[128,512]{1,0:T(8,128)(2,1)S(1)}, bf16[128,512]{1,0:T(8,128)(2,1)S(1)}, u32[]{:S(2)}, u32[]{:S(2)}) %collective-permute-start.1) | collective-permute-done | bytes 131104 | tf_op jit(solution)/shard_map/ppermute | solution.py:15
  125.9 0.0 copy-done.7
  125.9 2.1 %convolution_convert_fusion = bf16[128,512]{1,0:T(8,128)(2,1)} fusion(bf16[512,512]{1,0:T(8,128)(2,1)S(1)} %copy-done.7, f32[128,512]{1,0:T(8,128)S(1)} %convolution_add_fusion.1, bf16[128,512]{1,0:T(8,128)(2,1)S(1)} %collective-permute-done.1, bf16[3,512,512]{2,1,0:T(8,128)(2,1)} %param.16), kind=kOutput, calls=%fused_computation.23 | convolution fusion | flops 134676480 | bytes 1572864 | tf_op jit(solution)/shard_map/dot_general | solution.py:70
  (8 shorter events, 0.0 us)
Async XLA Ops:
  0.6 113.1 %copy-start = (bf16[2048,512]{1,0:T(8,128)(2,1)S(1)}, bf16[2048,512]{1,0:T(8,128)(2,1)}, u32[]{:S(2)}) copy-start(bf16[2048,512]{1,0:T(8,128)(2,1)} %param.15) | copy-start | bytes 6291460
  2.7 1.9 %copy-start.5 = (f32[128]{0:T(128)S(1)}, f32[128]{0:T(128)}, u32[]{:S(2)}) copy-start(f32[128]{0:T(128)} %param.14) | copy-start | bytes 1540
  2.7 2.0 %copy-start.6 = (f32[128]{0:T(128)S(1)}, f32[128]{0:T(128)}, u32[]{:S(2)}) copy-start(f32[128]{0:T(128)} %param.13) | copy-start | bytes 1540
  4.4 1.0 copy-start.1
  4.4 1.2 copy-start.2
  5.6 1.1 copy-start.4
  12.2 52.2 %all-to-all-start = ((bf16[3,128,2048]{1,0,2:T(4,128)(2,1)}), bf16[3,128,2048]{1,0,2:T(4,128)(2,1)}, u32[]{:S(2)}, u32[]{:S(2)}) async-start(bf16[3,128,2048]{1,0,2:T(4,128)(2,1)} %copy.36), calls=%async_computation | async-start | bytes 4194304 | tf_op jit(solution)/shard_map/all_to_all | solution.py:54
  80.8 1.0 copy-start.3
  84.1 1.0 copy-start.3
  87.4 1.0 copy-start.3
  90.8 1.0 copy-start.3
  114.3 11.6 %copy-start.7 = (bf16[512,512]{1,0:T(8,128)(2,1)S(1)}, bf16[512,512]{1,0:T(8,128)(2,1)}, u32[]{:S(2)}) copy-start(bf16[512,512]{1,0:T(8,128)(2,1)} %param.17) | copy-start | bytes 1572868
  114.3 7.8 %collective-permute-start = (bf16[128,512]{1,0:T(8,128)(2,1)S(1)}, bf16[128,512]{1,0:T(8,128)(2,1)S(1)}, u32[]{:S(2)}, u32[]{:S(2)}) collective-permute-start(bf16[128,512]{1,0:T(8,128)(2,1)S(1)} %convolution_convert_fusion.1), channel_id=1, source_target_pairs={{0,1},{1,2},{2,3},{3,4},{4,5},{5,6},{6,7},{7,8},{8,9},{9,10},{10,1... | collective-permute-start | bytes 393224 | tf_op jit(solution)/shard_map/ppermute | solution.py:15
  117.0 8.9 %collective-permute-start.1 = (bf16[128,512]{1,0:T(8,128)(2,1)S(1)}, bf16[128,512]{1,0:T(8,128)(2,1)S(1)}, u32[]{:S(2)}, u32[]{:S(2)}) collective-permute-start(bf16[128,512]{1,0:T(8,128)(2,1)S(1)} %convolution_convert_fusion.1), channel_id=1, source_target_pairs={{0,2},{1,3},{2,4},{3,5},{4,6},{5,7},{6,8},{7,9},{8,10},{9,11},{10,... | collective-permute-start | bytes 393224 | tf_op jit(solution)/shard_map/ppermute | solution.py:15
where the time goes:
time: 129 us; the launch traced here: 128 us
  waiting for transfers between devices  48.4 us (38%)
  local copies, waits for them, and re-layouts  23.6 us (18%)
  blocking collectives  20.2 us (16%)
  matrix products  14.3 us (11%)
  starting transfers between devices  11.8 us (9%)
  other arithmetic  8.86 us (7%)
    all_to_all x1, waiting for transfers between devices, body(): lax.all_to_all(stacked, 'seq', split_axis=2, concat_axis=1, tiled=True)  45.9 us
    all_to_all x1, blocking collectives, body(): lax.all_to_all(placed, 'seq', split_axis=0, concat_axis=1, tiled=True)  20.2 us
    slice x3, local copies, waits for them, and re-layouts, body(): out = attend(q_head, got[1], got[2])  13.2 us
    all_to_all x1, starting transfers between devices, body(): lax.all_to_all(stacked, 'seq', split_axis=2, concat_axis=1, tiled=True)  6.3 us
    dot_general x4, matrix products, one_block(): jnp.dot(expo.astype(jnp.bfloat16), v_head, preferred_element_type=jnp.flo...  6 us
    ppermute x2, starting transfers between devices, passed_along(): return lax.ppermute(shard, axis, pairs)  5.51 us
    another operation x1, local copies, waits for them, and re-layouts, body(): stacked = jnp.stack([spread(q_norm), spread(k_norm), spread(values)])  4.14 us
    reduce_sum x4, other arithmetic, one_block(): total = jnp.sum(expo, axis=-1, keepdims=True)  3.27 us
  transfers between devices with their start and end apart: 3, of which 2 were waited for; matrix products, arithmetic and copies ran while one was open for 3% of the time, Pallas kernels for 0%

commit v1 on v0

v1 whole, which is shorter than its diff:
```python
import math

import jax
import jax.numpy as jnp
from jax import lax
from jax.experimental import pallas as pl
from jax.experimental.pallas import tpu as pltpu
from jax.sharding import PartitionSpec as P

HEADS = 16
HD = 128
EPS = 1e-06


def passed_along(shard, axis, by):
    peers = lax.axis_size(axis)
    pairs = [(i, i + by) for i in range(peers) if 0 <= i + by < peers]
    return lax.ppermute(shard, axis, pairs)


def _norm(x, gain):
    x = x.astype(jnp.float32)
    x = x * lax.rsqrt(jnp.mean(x * x, axis=-1, keepdims=True) + EPS) * gain
    return x.astype(jnp.bfloat16)


def _attn_kernel(share_ref, q_ref, k_ref, v_ref, gq_ref, gk_ref, o_ref, kn_ref):
    @pl.when(pl.program_id(0) == 0)
    def _():
        k = k_ref[...]
        k = k.reshape(k.shape[0] * k.shape[1], HD)
        kn_ref[...] = _norm(k, gk_ref[...])

    q = q_ref[...]
    q = q.reshape(q.shape[0] * q.shape[1], HD)
    qn = _norm(q, gq_ref[...])
    kn = kn_ref[...]
    v = v_ref[...]
    v = v.reshape(v.shape[0] * v.shape[1], HD)
    s = lax.dot_general(qn, kn, (((1,), (1,)), ((), ())), preferred_element_type=jnp.float32)
    s = s * (1.0 / math.sqrt(HD))
    m = jnp.max(s, axis=-1, keepdims=True)
    e = jnp.exp(s - m)
    total = jnp.sum(e, axis=-1, keepdims=True)
    out = jnp.dot(e.astype(jnp.bfloat16), v, preferred_element_type=jnp.float32)
    out = (out / total).astype(jnp.bfloat16)
    o_ref[...] = out.reshape(o_ref.shape)


def attend(got, share, span_blocks, gain_q, gain_k):
    src, _, rows, _ = got.shape
    qb = max(1, 512 // rows)
    qb = min(qb, span_blocks)
    steps = span_blocks // qb
    tokens = src * rows
    return pl.pallas_call(
        _attn_kernel,
        out_shape=jax.ShapeDtypeStruct((span_blocks, rows, HD), jnp.bfloat16),
        grid_spec=pltpu.PrefetchScalarGridSpec(
            num_scalar_prefetch=1,
            grid=(steps,),
            in_specs=[
                pl.BlockSpec((qb, None, rows, HD), lambda i, sh: (sh[0] * steps + i, 0, 0, 0)),
                pl.BlockSpec((src, None, rows, HD), lambda i, sh: (0, 1, 0, 0)),
                pl.BlockSpec((src, None, rows, HD), lambda i, sh: (0, 2, 0, 0)),
                pl.BlockSpec((1, HD), lambda i, sh: (0, 0)),
                pl.BlockSpec((1, HD), lambda i, sh: (0, 0)),
            ],
            out_specs=pl.BlockSpec((qb, rows, HD), lambda i, sh: (i, 0, 0)),
            scratch_shapes=[pltpu.VMEM((tokens, HD), jnp.bfloat16)],
        ),
        compiler_params=pltpu.CompilerParams(
            dimension_semantics=("arbitrary",), vmem_limit_bytes=48 * 1024 * 1024
        ),
    )(share, got, got, got, gain_q.reshape(1, HD), gain_k.reshape(1, HD))


def body(queries, keys, values, gain_q, gain_k, w_latent, w_temporal, w_decode):
    devices = lax.axis_size("seq")
    copies = devices // HEADS
    rows = queries.shape[0]

    def head_major(x):
        x = jnp.transpose(x.reshape(rows, HEADS, HD), (1, 0, 2))
        if copies > 1:
            x = jnp.broadcast_to(x[:, None], (HEADS, copies, rows, HD))
        return x.reshape(devices, rows, HD)

    stacked = jnp.stack([head_major(queries), head_major(keys), head_major(values)], axis=1)
    got = lax.all_to_all(stacked, "seq", split_axis=0, concat_axis=0, tiled=True)
    share = lax.axis_index("seq") % copies
    span_blocks = devices // copies
    out = attend(got, jnp.reshape(share, (1,)).astype(jnp.int32), span_blocks, gain_q, gain_k)
    if copies > 1:
        placed = jnp.zeros((copies, span_blocks, rows, HD), jnp.bfloat16)
        placed = lax.dynamic_update_index_in_dim(placed, out, share, 0)
        out = placed.reshape(devices, rows, HD)
    back = lax.all_to_all(out, "seq", split_axis=0, concat_axis=0, tiled=True)
    if copies > 1:
        back = jnp.sum(back.reshape(HEADS, copies, rows, HD).astype(jnp.float32), axis=1)
        back = back.astype(jnp.bfloat16)
    attention = jnp.transpose(back.reshape(HEADS, rows, HD), (1, 0, 2)).reshape(rows, HEADS * HD)
    latent = jnp.dot(attention, w_latent, preferred_element_type=jnp.float32).astype(jnp.bfloat16)
    earlier_one = passed_along(latent, "seq", 1)
    earlier_two = passed_along(latent, "seq", 2)
    state = jnp.dot(latent, w_temporal[0], preferred_element_type=jnp.float32)
    state = state + jnp.dot(earlier_one, w_temporal[1], preferred_element_type=jnp.float32)
    state = state + jnp.dot(earlier_two, w_temporal[2], preferred_element_type=jnp.float32)
    decoded = jnp.dot(
        jax.nn.silu(state).astype(jnp.bfloat16), w_decode, preferred_element_type=jnp.float32
    )
    return (attention, decoded.astype(jnp.bfloat16))


def solution(mesh):
    in_specs = (
        P(("groups", "seq"), None),
        P(("groups", "seq"), None),
        P(("groups", "seq"), None),
        P(),
        P(),
        P(),
        P(),
        P(),
    )
    out_specs = (P(("groups", "seq"), None), P(("groups", "seq"), None))
    return jax.shard_map(body, mesh=mesh, in_specs=in_specs, out_specs=out_specs, check_vma=False)
```

time: 129 us -> 96.9 us (0.75)
  waiting for transfers between devices: 48.4 us -> 5.02 us
  blocking collectives: 20.2 us -> 60.6 us
  local copies, waits for them, and re-layouts: 23.6 us -> 7.71 us
  Pallas kernels: 0 us -> 12.7 us
  matrix products: 14.3 us -> 3.07 us
  other arithmetic: 8.86 us -> 1.36 us
  starting transfers between devices: 11.8 us -> 5.23 us
    all_to_all x1 -> x0, waiting for transfers between devices: 45.9 us -> none  [body(): lax.all_to_all(stacked, 'seq', split_axis=2, concat_axis=1, tiled=True)]
    all_to_all x1 -> x2, blocking collectives: 20.2 us -> 60.6 us  [the longest x1 42.2 us: body(): lax.all_to_all(stacked, 'seq', split_axis=0, concat_axis=0, tiled=True)]
    slice x4 -> x0, local copies, waits for them, and re-layouts: 15.6 us -> none  [the longest x3 13.2 us: body(): out = attend(q_head, got[1], got[2])]
    pallas_call x0 -> x1, Pallas kernels: none -> 12.7 us  [attend(): pl.pallas_call(_attn_kernel, out_shape=jax.ShapeDtypeStruct((span_blocks,...]
    dot_general x8 -> x0, matrix products: 9.14 us -> none  [the longest x4 6 us: one_block(): jnp.dot(expo.astype(jnp.bfloat16), v_head, preferred_element_type=jnp.flo...]
    all_to_all x1 -> x0, starting transfers between devices: 6.3 us -> none  [body(): lax.all_to_all(stacked, 'seq', split_axis=2, concat_axis=1, tiled=True)]
    another operation x1 -> x0, local copies, waits for them, and re-layouts: 4.14 us -> none  [body(): stacked = jnp.stack([spread(q_norm), spread(k_norm), spread(values)])]
    reduce_sum x6 -> x0, other arithmetic: 3.96 us -> none  [the longest x4 3.27 us: one_block(): total = jnp.sum(expo, axis=-1, keepdims=True)]
  transfers between devices with their start and end apart: 3 -> 2, of which waited for: 2 -> 1; matrix products, arithmetic and copies ran while one was open for 3% -> 0% of each run, Pallas kernels for 0% -> 0%
where the time goes in v1:
time: 96.9 us; the launch traced here: 96.5 us
  blocking collectives  60.6 us (63%)
  Pallas kernels  12.7 us (13%)
  local copies, waits for them, and re-layouts  7.71 us (8%)
  starting transfers between devices  5.23 us (5%)
  waiting for transfers between devices  5.02 us (5%)
  matrix products  3.07 us (3%)
  other arithmetic  1.36 us (1%)
    all_to_all x1, blocking collectives, body(): lax.all_to_all(stacked, 'seq', split_axis=0, concat_axis=0, tiled=True)  42.2 us
    all_to_all x1, blocking collectives, body(): back = lax.all_to_all(out, 'seq', split_axis=0, concat_axis=0, tiled=True)  18.4 us
    pallas_call x1, Pallas kernels, attend(): pl.pallas_call(_attn_kernel, out_shape=jax.ShapeDtypeStruct((span_blocks,...  12.7 us
    ppermute x2, starting transfers between devices, passed_along(): return lax.ppermute(shard, axis, pairs)  5.23 us
    unnamed x14, local copies, waits for them, and re-layouts  5.12 us
    ppermute x2, waiting for transfers between devices, passed_along(): return lax.ppermute(shard, axis, pairs)  5.02 us
    reshape x3, local copies, waits for them, and re-layouts, head_major(): x = jnp.transpose(x.reshape(rows, HEADS, HD), (1, 0, 2))  2.31 us
    dot_general x1, matrix products, body(): jnp.dot(jax.nn.silu(state).astype(jnp.bfloat16), w_decode, preferred_elem...  2.14 us
  transfers between devices with their start and end apart: 2, of which 1 were waited for; matrix products, arithmetic and copies ran while one was open for 0% of the time, Pallas kernels for 0%

profile of v1, /device:TPU:8, one launch (start us, length us, event | category | flops | bytes accessed | tf_op | source)
XLA Modules:
  0.0 96.5 jit_solution(7805883970269070678)
XLA Ops:
  0.6 0.0 copy-start
  0.6 1.5 %copy.10 = bf16[128,2048]{0,1:T(8,128)(2,1)S(1)} copy(bf16[128,2048]{1,0:T(8,128)(2,1)} %param.8) | data formatting | bytes 1048576 | tf_op args[0]
  2.1 0.3 copy.11
  2.4 1.3 %copy.12 = bf16[128,2048]{0,1:T(8,128)(2,1)S(1)} copy(bf16[128,2048]{1,0:T(8,128)(2,1)} %param.9) | data formatting | bytes 1048576 | tf_op args[1]
  3.7 1.0 %copy.13 = bf16[128,16,128]{2,0,1:T(8,128)(2,1)} copy(bf16[128,16,128]{0,2,1:T(8,128)(2,1)S(1)} %bitcast.41) | data formatting | bytes 1048576 | tf_op jit(solution)/shard_map/reshape | solution.py:84
  4.7 1.3 %copy.14 = bf16[128,2048]{0,1:T(8,128)(2,1)S(1)} copy(bf16[128,2048]{1,0:T(8,128)(2,1)} %param.10) | data formatting | bytes 1048576 | tf_op args[2]
  6.0 1.0 %copy.15 = bf16[128,16,128]{2,0,1:T(8,128)(2,1)} copy(bf16[128,16,128]{0,2,1:T(8,128)(2,1)S(1)} %bitcast.42) | data formatting | bytes 1048576 | tf_op jit(solution)/shard_map/reshape | solution.py:84
  7.1 1.4 %pad_maximum_fusion = bf16[16,3,128,128]{3,2,1,0:T(8,128)(2,1)S(1)} fusion(bf16[16,1,128,128]{3,2,1,0:T(8,128)(2,1)} %bitcast.45, bf16[16,1,128,128]{3,2,1,0:T(8,128)(2,1)} %bitcast.44, bf16[16,1,128,128]{3,2,1,0:T(8,128)(2,1)S(1)} %bitcast.43), kind=kLoop, calls=%fused_computation | loop fusion | flops 1572864 | bytes 3145728 | tf_op jit(solution)/shard_map/stack | solution.py:89
  8.4 0.0 copy-start.1
  8.4 0.0 copy-start.2
  8.5 42.2 %all_to_all.10.q_ref.k_ref.v_ref = bf16[16,3,128,128]{3,2,1,0:T(8,128)(2,1)S(1)} all-to-all(bf16[16,3,128,128]{3,2,1,0:T(8,128)(2,1)S(1)} %pad_maximum_fusion), channel_id=1, replica_groups=mesh['groups'=2,'seq'=16] {'seq'}, dimensions={0} | all-to-all | bytes 3145728 | tf_op jit(solution)/shard_map/all_to_all | solution.py:90
  50.7 0.0 copy-done.1
  50.7 0.0 copy-done.2
  50.7 12.7 %shard_map.95 = bf16[16,128,128]{2,1,0:T(8,128)(2,1)S(1)} custom-call(s32[1]{0:T(128)} %constant.17.clone.1.share_ref, bf16[16,3,128,128]{3,2,1,0:T(8,128)(2,1)S(1)} %all_to_all.10.q_ref.k_ref.v_ref, bf16[16,3,128,128]{3,2,1,0:T(8,128)(2,1)S(1)} %all_to_all.10.q_ref.k_ref.v_ref, bf16[16,3,128,128]{3,2,1,0:T(8,128)(2,1)S(1)} %all_to_all.10.q_ref.k_ref.v_ref, ...), custom_call_target="tpu_custom_call" | custom-call | tf_op jit(solution)/shard_map/pallas_call | solution.py:56
  63.4 18.4 %all_to_all.11 = bf16[16,128,128]{2,1,0:T(8,128)(2,1)S(1)} all-to-all(bf16[16,128,128]{2,1,0:T(8,128)(2,1)S(1)} %shard_map.95), channel_id=1, replica_groups=mesh['groups'=2,'seq'=16] {'seq'}, dimensions={0} | all-to-all | bytes 1048576 | tf_op jit(solution)/shard_map/all_to_all | solution.py:98
  81.8 0.3 copy.16
  82.1 1.0 %copy.17 = bf16[128,2048]{1,0:T(8,128)(2,1)} copy(bf16[128,2048]{0,1:T(8,128)(2,1)S(1)} %bitcast.37) | data formatting | bytes 1048576
  83.1 0.0 copy-done
  83.1 0.0 copy-start.3
  83.1 0.5 convolution_convert_fusion.1
  83.6 0.0 copy-start.4
  83.6 3.3 %collective-permute-start.1 = (bf16[128,512]{1,0:T(8,128)(2,1)S(1)}, bf16[128,512]{1,0:T(8,128)(2,1)S(1)}, u32[]{:S(2)}, u32[]{:S(2)}) collective-permute-start(bf16[128,512]{1,0:T(8,128)(2,1)S(1)} %convolution_convert_fusion.1), channel_id=1, source_target_pairs={{0,2},{1,3},{2,4},{3,5},{4,6},{5,7},{6,8},{7,9},{8,10},{9,11},{10,... | collective-permute-start | bytes 393224 | tf_op jit(solution)/shard_map/ppermute | solution.py:18
  86.9 1.9 %collective-permute-start = (bf16[128,512]{1,0:T(8,128)(2,1)S(1)}, bf16[128,512]{1,0:T(8,128)(2,1)S(1)}, u32[]{:S(2)}, u32[]{:S(2)}) collective-permute-start(bf16[128,512]{1,0:T(8,128)(2,1)S(1)} %convolution_convert_fusion.1), channel_id=1, source_target_pairs={{0,1},{1,2},{2,3},{3,4},{4,5},{5,6},{6,7},{7,8},{8,9},{9,10},{10,1... | collective-permute-start | bytes 393224 | tf_op jit(solution)/shard_map/ppermute | solution.py:18
  88.8 0.0 copy-done.3
  88.9 0.2 fusion.2
  89.1 5.0 %collective-permute-done = bf16[128,512]{1,0:T(8,128)(2,1)S(1)} collective-permute-done((bf16[128,512]{1,0:T(8,128)(2,1)S(1)}, bf16[128,512]{1,0:T(8,128)(2,1)S(1)}, u32[]{:S(2)}, u32[]{:S(2)}) %collective-permute-start) | collective-permute-done | bytes 131104 | tf_op jit(solution)/shard_map/ppermute | solution.py:18
  94.1 0.2 convolution_add_fusion.1
  94.3 0.0 collective-permute-done.1
  94.4 0.0 copy-done.4
  94.4 2.1 %convolution_convert_fusion = bf16[128,512]{1,0:T(8,128)(2,1)} fusion(bf16[512,512]{1,0:T(8,128)(2,1)S(1)} %copy-done.4, f32[128,512]{1,0:T(8,128)S(1)} %convolution_add_fusion.1, bf16[128,512]{1,0:T(8,128)(2,1)S(1)} %collective-permute-done.1, bf16[3,512,512]{2,1,0:T(8,128)(2,1)} %param.14), kind=kOutput, calls=%fused_computation.3 | convolution fusion | flops 134676480 | bytes 1572864 | tf_op jit(solution)/shard_map/dot_general | solution.py:109
Async XLA Ops:
  0.6 82.5 %copy-start = (bf16[2048,512]{1,0:T(8,128)(2,1)S(1)}, bf16[2048,512]{1,0:T(8,128)(2,1)}, u32[]{:S(2)}) copy-start(bf16[2048,512]{1,0:T(8,128)(2,1)} %param.13) | copy-start | bytes 6291460
  8.4 42.2 %copy-start.1 = (f32[128]{0:T(128)S(1)}, f32[128]{0:T(128)}, u32[]{:S(2)}) copy-start(f32[128]{0:T(128)} %param.11) | copy-start | bytes 1540
  8.4 42.2 %copy-start.2 = (f32[128]{0:T(128)S(1)}, f32[128]{0:T(128)}, u32[]{:S(2)}) copy-start(f32[128]{0:T(128)} %param.12) | copy-start | bytes 1540
  83.1 5.7 %copy-start.3 = (bf16[3,512,512]{2,1,0:T(8,128)(2,1)S(1)}, bf16[3,512,512]{2,1,0:T(8,128)(2,1)}, u32[]{:S(2)}) copy-start(bf16[3,512,512]{2,1,0:T(8,128)(2,1)} %param.14) | copy-start | bytes 4718596
  83.6 10.8 %copy-start.4 = (bf16[512,512]{1,0:T(8,128)(2,1)S(1)}, bf16[512,512]{1,0:T(8,128)(2,1)}, u32[]{:S(2)}) copy-start(bf16[512,512]{1,0:T(8,128)(2,1)} %param.15) | copy-start | bytes 1572868
  83.6 10.7 %collective-permute-start.1 = (bf16[128,512]{1,0:T(8,128)(2,1)S(1)}, bf16[128,512]{1,0:T(8,128)(2,1)S(1)}, u32[]{:S(2)}, u32[]{:S(2)}) collective-permute-start(bf16[128,512]{1,0:T(8,128)(2,1)S(1)} %convolution_convert_fusion.1), channel_id=1, source_target_pairs={{0,2},{1,3},{2,4},{3,5},{4,6},{5,7},{6,8},{7,9},{8,10},{9,11},{10,... | collective-permute-start | bytes 393224 | tf_op jit(solution)/shard_map/ppermute | solution.py:18
  86.9 7.2 %collective-permute-start = (bf16[128,512]{1,0:T(8,128)(2,1)S(1)}, bf16[128,512]{1,0:T(8,128)(2,1)S(1)}, u32[]{:S(2)}, u32[]{:S(2)}) collective-permute-start(bf16[128,512]{1,0:T(8,128)(2,1)S(1)} %convolution_convert_fusion.1), channel_id=1, source_target_pairs={{0,1},{1,2},{2,3},{3,4},{4,5},{5,6},{6,7},{7,8},{8,9},{9,10},{10,1... | collective-permute-start | bytes 393224 | tf_op jit(solution)/shard_map/ppermute | solution.py:18

commit v2 on v1

--- a/solution.py
+++ b/solution.py
@@ -75,18 +75,34 @@
     )(share, got, got, got, gain_q.reshape(1, HD), gain_k.reshape(1, HD))
 
 
+def _pack_kernel(q_ref, k_ref, v_ref, o_ref):
+    group = q_ref.shape[1] // HD
+    copies = o_ref.shape[0] // group
+    for i in range(group):
+        for c in range(copies):
+            for j, ref in enumerate((q_ref, k_ref, v_ref)):
+                o_ref[i * copies + c, j] = ref[:, i * HD:(i + 1) * HD]
+
+
+def pack(queries, keys, values, copies):
+    rows = queries.shape[0]
+    group = 4
+    spec = pl.BlockSpec((rows, group * HD), lambda g: (0, g))
+    return pl.pallas_call(
+        _pack_kernel,
+        out_shape=jax.ShapeDtypeStruct((HEADS * copies, 3, rows, HD), jnp.bfloat16),
+        grid=(HEADS // group,),
+        in_specs=[spec, spec, spec],
+        out_specs=pl.BlockSpec((group * copies, 3, rows, HD), lambda g: (g, 0, 0, 0)),
+    )(queries, keys, values)
+
+
 def body(queries, keys, values, gain_q, gain_k, w_latent, w_temporal, w_decode):
     devices = lax.axis_size("seq")
     copies = devices // HEADS
     rows = queries.shape[0]
 
-    def head_major(x):
-        x = jnp.transpose(x.reshape(rows, HEADS, HD), (1, 0, 2))
-        if copies > 1:
-            x = jnp.broadcast_to(x[:, None], (HEADS, copies, rows, HD))
-        return x.reshape(devices, rows, HD)
-
-    stacked = jnp.stack([head_major(queries), head_major(keys), head_major(values)], axis=1)
+    stacked = pack(queries, keys, values, copies)
     got = lax.all_to_all(stacked, "seq", split_axis=0, concat_axis=0, tiled=True)
     share = lax.axis_index("seq") % copies
     span_blocks = devices // copies

time: 96.9 us -> 93.3 us (0.963)
  local copies, waits for them, and re-layouts: 7.71 us -> 1.32 us
  Pallas kernels: 12.7 us -> 16.6 us
  other arithmetic: 1.36 us -> 0 us
    unnamed x14 -> x11, local copies, waits for them, and re-layouts: 5.12 us -> 1.04 us
    pallas_call x0 -> x1, Pallas kernels: none -> 3.89 us  [pack(): pl.pallas_call(_pack_kernel, out_shape=jax.ShapeDtypeStruct((HEADS * copi...]
    reshape x3 -> x0, local copies, waits for them, and re-layouts: 2.31 us -> none  [head_major(): x = jnp.transpose(x.reshape(rows, HEADS, HD), (1, 0, 2))]
    another operation x1 -> x0, other arithmetic: 1.36 us -> none  [body(): jnp.stack([head_major(queries), head_major(keys), head_major(values)], ax...]
where the time goes in v2:
time: 93.3 us; the launch traced here: 92.9 us
  blocking collectives  61 us (65%)
  Pallas kernels  16.6 us (18%)
  starting transfers between devices  5.23 us (6%)
  waiting for transfers between devices  5.02 us (5%)
  matrix products  3.07 us (3%)
  local copies, waits for them, and re-layouts  1.32 us (1%)
    all_to_all x1, blocking collectives, body(): lax.all_to_all(stacked, 'seq', split_axis=0, concat_axis=0, tiled=True)  42.5 us
    all_to_all x1, blocking collectives, body(): back = lax.all_to_all(out, 'seq', split_axis=0, concat_axis=0, tiled=True)  18.4 us
    pallas_call x1, Pallas kernels, attend(): pl.pallas_call(_attn_kernel, out_shape=jax.ShapeDtypeStruct((span_blocks,...  12.7 us
    ppermute x2, starting transfers between devices, passed_along(): return lax.ppermute(shard, axis, pairs)  5.23 us
    ppermute x2, waiting for transfers between devices, passed_along(): return lax.ppermute(shard, axis, pairs)  5.02 us
    pallas_call x1, Pallas kernels, pack(): pl.pallas_call(_pack_kernel, out_shape=jax.ShapeDtypeStruct((HEADS * copi...  3.89 us
    dot_general x1, matrix products, body(): jnp.dot(jax.nn.silu(state).astype(jnp.bfloat16), w_decode, preferred_elem...  2.14 us
  transfers between devices with their start and end apart: 2, of which 1 were waited for; matrix products, arithmetic and copies ran while one was open for 0% of the time, Pallas kernels for 0%

profile of v2, /device:TPU:8, one launch (start us, length us, event | category | flops | bytes accessed | tf_op | source)
XLA Modules:
  0.0 92.9 jit_solution(17766926070234483399)
XLA Ops:
  0.6 0.0 copy-start
  0.6 3.9 %shard_map.95 = bf16[16,3,128,128]{3,2,1,0:T(8,128)(2,1)} custom-call(bf16[128,2048]{1,0:T(8,128)(2,1)} %q_ref.1, bf16[128,2048]{1,0:T(8,128)(2,1)} %k_ref.1, bf16[128,2048]{1,0:T(8,128)(2,1)} %v_ref.1), custom_call_target="tpu_custom_call" | custom-call | tf_op jit(solution)/shard_map/pallas_call | solution.py:91
  4.5 0.0 copy-start.1
  4.5 0.0 copy-start.2
  4.5 42.5 %all_to_all.10.q_ref.k_ref.v_ref = bf16[16,3,128,128]{3,2,1,0:T(8,128)(2,1)S(1)} all-to-all(bf16[16,3,128,128]{3,2,1,0:T(8,128)(2,1)} %shard_map.95), channel_id=1, replica_groups=mesh['groups'=2,'seq'=16] {'seq'}, dimensions={0} | all-to-all | bytes 3145728 | tf_op jit(solution)/shard_map/all_to_all | solution.py:106
  47.1 0.0 copy-done.1
  47.1 0.0 copy-done.2
  47.1 12.7 %shard_map.96 = bf16[16,128,128]{2,1,0:T(8,128)(2,1)S(1)} custom-call(s32[1]{0:T(128)} %constant.17.clone.1.share_ref, bf16[16,3,128,128]{3,2,1,0:T(8,128)(2,1)S(1)} %all_to_all.10.q_ref.k_ref.v_ref, bf16[16,3,128,128]{3,2,1,0:T(8,128)(2,1)S(1)} %all_to_all.10.q_ref.k_ref.v_ref, bf16[16,3,128,128]{3,2,1,0:T(8,128)(2,1)S(1)} %all_to_all.10.q_ref.k_ref.v_ref, ...), custom_call_target="tpu_custom_call" | custom-call | tf_op jit(solution)/shard_map/pallas_call | solution.py:56
  59.8 18.4 %all_to_all.11 = bf16[16,128,128]{2,1,0:T(8,128)(2,1)S(1)} all-to-all(bf16[16,128,128]{2,1,0:T(8,128)(2,1)S(1)} %shard_map.96), channel_id=1, replica_groups=mesh['groups'=2,'seq'=16] {'seq'}, dimensions={0} | all-to-all | bytes 1048576 | tf_op jit(solution)/shard_map/all_to_all | solution.py:114
  78.2 0.3 copy.10
  78.5 1.0 %copy.11 = bf16[128,2048]{1,0:T(8,128)(2,1)} copy(bf16[128,2048]{0,1:T(8,128)(2,1)S(1)} %bitcast.25) | data formatting | bytes 1048576
  79.5 0.0 copy-done
  79.5 0.0 copy-start.3
  79.5 0.5 convolution_convert_fusion.1
  80.0 0.0 copy-start.4
  80.0 3.3 %collective-permute-start.1 = (bf16[128,512]{1,0:T(8,128)(2,1)S(1)}, bf16[128,512]{1,0:T(8,128)(2,1)S(1)}, u32[]{:S(2)}, u32[]{:S(2)}) collective-permute-start(bf16[128,512]{1,0:T(8,128)(2,1)S(1)} %convolution_convert_fusion.1), channel_id=1, source_target_pairs={{0,2},{1,3},{2,4},{3,5},{4,6},{5,7},{6,8},{7,9},{8,10},{9,11},{10,... | collective-permute-start | bytes 393224 | tf_op jit(solution)/shard_map/ppermute | solution.py:18
  83.3 1.9 %collective-permute-start = (bf16[128,512]{1,0:T(8,128)(2,1)S(1)}, bf16[128,512]{1,0:T(8,128)(2,1)S(1)}, u32[]{:S(2)}, u32[]{:S(2)}) collective-permute-start(bf16[128,512]{1,0:T(8,128)(2,1)S(1)} %convolution_convert_fusion.1), channel_id=1, source_target_pairs={{0,1},{1,2},{2,3},{3,4},{4,5},{5,6},{6,7},{7,8},{8,9},{9,10},{10,1... | collective-permute-start | bytes 393224 | tf_op jit(solution)/shard_map/ppermute | solution.py:18
  85.3 0.0 copy-done.3
  85.3 0.2 fusion.2
  85.5 5.0 %collective-permute-done = bf16[128,512]{1,0:T(8,128)(2,1)S(1)} collective-permute-done((bf16[128,512]{1,0:T(8,128)(2,1)S(1)}, bf16[128,512]{1,0:T(8,128)(2,1)S(1)}, u32[]{:S(2)}, u32[]{:S(2)}) %collective-permute-start) | collective-permute-done | bytes 131104 | tf_op jit(solution)/shard_map/ppermute | solution.py:18
  90.5 0.2 convolution_add_fusion.1
  90.8 0.0 collective-permute-done.1
  90.8 0.0 copy-done.4
  90.8 2.1 %convolution_convert_fusion = bf16[128,512]{1,0:T(8,128)(2,1)} fusion(bf16[512,512]{1,0:T(8,128)(2,1)S(1)} %copy-done.4, f32[128,512]{1,0:T(8,128)S(1)} %convolution_add_fusion.1, bf16[128,512]{1,0:T(8,128)(2,1)S(1)} %collective-permute-done.1, bf16[3,512,512]{2,1,0:T(8,128)(2,1)} %param.14), kind=kOutput, calls=%fused_computation.2 | convolution fusion | flops 134676480 | bytes 1572864 | tf_op jit(solution)/shard_map/dot_general | solution.py:125
Async XLA Ops:
  0.6 78.9 %copy-start = (bf16[2048,512]{1,0:T(8,128)(2,1)S(1)}, bf16[2048,512]{1,0:T(8,128)(2,1)}, u32[]{:S(2)}) copy-start(bf16[2048,512]{1,0:T(8,128)(2,1)} %param.13) | copy-start | bytes 6291460
  4.5 42.5 %copy-start.1 = (f32[128]{0:T(128)S(1)}, f32[128]{0:T(128)}, u32[]{:S(2)}) copy-start(f32[128]{0:T(128)} %param.11) | copy-start | bytes 1540
  4.5 42.5 %copy-start.2 = (f32[128]{0:T(128)S(1)}, f32[128]{0:T(128)}, u32[]{:S(2)}) copy-start(f32[128]{0:T(128)} %param.12) | copy-start | bytes 1540
  79.5 5.7 %copy-start.3 = (bf16[3,512,512]{2,1,0:T(8,128)(2,1)S(1)}, bf16[3,512,512]{2,1,0:T(8,128)(2,1)}, u32[]{:S(2)}) copy-start(bf16[3,512,512]{2,1,0:T(8,128)(2,1)} %param.14) | copy-start | bytes 4718596
  80.0 10.8 %copy-start.4 = (bf16[512,512]{1,0:T(8,128)(2,1)S(1)}, bf16[512,512]{1,0:T(8,128)(2,1)}, u32[]{:S(2)}) copy-start(bf16[512,512]{1,0:T(8,128)(2,1)} %param.15) | copy-start | bytes 1572868
  80.0 10.7 %collective-permute-start.1 = (bf16[128,512]{1,0:T(8,128)(2,1)S(1)}, bf16[128,512]{1,0:T(8,128)(2,1)S(1)}, u32[]{:S(2)}, u32[]{:S(2)}) collective-permute-start(bf16[128,512]{1,0:T(8,128)(2,1)S(1)} %convolution_convert_fusion.1), channel_id=1, source_target_pairs={{0,2},{1,3},{2,4},{3,5},{4,6},{5,7},{6,8},{7,9},{8,10},{9,11},{10,... | collective-permute-start | bytes 393224 | tf_op jit(solution)/shard_map/ppermute | solution.py:18
  83.3 7.2 %collective-permute-start = (bf16[128,512]{1,0:T(8,128)(2,1)S(1)}, bf16[128,512]{1,0:T(8,128)(2,1)S(1)}, u32[]{:S(2)}, u32[]{:S(2)}) collective-permute-start(bf16[128,512]{1,0:T(8,128)(2,1)S(1)} %convolution_convert_fusion.1), channel_id=1, source_target_pairs={{0,1},{1,2},{2,3},{3,4},{4,5},{5,6},{6,7},{7,8},{8,9},{9,10},{10,1... | collective-permute-start | bytes 393224 | tf_op jit(solution)/shard_map/ppermute | solution.py:18

commit v3 on v2

--- a/solution.py
+++ b/solution.py
@@ -47,9 +47,9 @@
     o_ref[...] = out.reshape(o_ref.shape)
 
 
-def attend(got, share, span_blocks, gain_q, gain_k):
+def attend(got, share, span_blocks, gain_q, gain_k, qb_rows=256):
     src, _, rows, _ = got.shape
-    qb = max(1, 512 // rows)
+    qb = max(1, qb_rows // rows)
     qb = min(qb, span_blocks)
     steps = span_blocks // qb
     tokens = src * rows
@@ -86,7 +86,7 @@
 
 def pack(queries, keys, values, copies):
     rows = queries.shape[0]
-    group = 4
+    group = 8
     spec = pl.BlockSpec((rows, group * HD), lambda g: (0, g))
     return pl.pallas_call(
         _pack_kernel,

time: 93.3 us -> 89.7 us (0.961)
  Pallas kernels: 16.6 us -> 13 us
    pallas_call x1, Pallas kernels: 12.7 us -> 10.5 us  [attend(): pl.pallas_call(_attn_kernel, out_shape=jax.ShapeDtypeStruct((span_blocks,...]
    pallas_call x1, Pallas kernels: 3.89 us -> 2.56 us  [pack(): pl.pallas_call(_pack_kernel, out_shape=jax.ShapeDtypeStruct((HEADS * copi...]
  transfers between devices with their start and end apart: 2 -> 2, of which waited for: 1 -> 1; matrix products, arithmetic and copies ran while one was open for 0% -> 1% of each run, Pallas kernels for 0% -> 0%
where the time goes in v3:
time: 89.7 us; the launch traced here: 89.3 us
  blocking collectives  61 us (68%)
  Pallas kernels  13 us (14%)
  starting transfers between devices  5.23 us (6%)
  waiting for transfers between devices  5.01 us (6%)
  matrix products  3.07 us (3%)
  local copies, waits for them, and re-layouts  1.32 us (1%)
    all_to_all x1, blocking collectives, body(): lax.all_to_all(stacked, 'seq', split_axis=0, concat_axis=0, tiled=True)  42.5 us
    all_to_all x1, blocking collectives, body(): back = lax.all_to_all(out, 'seq', split_axis=0, concat_axis=0, tiled=True)  18.4 us
    pallas_call x1, Pallas kernels, attend(): pl.pallas_call(_attn_kernel, out_shape=jax.ShapeDtypeStruct((span_blocks,...  10.5 us
    ppermute x2, starting transfers between devices, passed_along(): return lax.ppermute(shard, axis, pairs)  5.23 us
    ppermute x2, waiting for transfers between devices, passed_along(): return lax.ppermute(shard, axis, pairs)  5.01 us
    pallas_call x1, Pallas kernels, pack(): pl.pallas_call(_pack_kernel, out_shape=jax.ShapeDtypeStruct((HEADS * copi...  2.56 us
    dot_general x1, matrix products, body(): jnp.dot(jax.nn.silu(state).astype(jnp.bfloat16), w_decode, preferred_elem...  2.14 us
  transfers between devices with their start and end apart: 2, of which 1 were waited for; matrix products, arithmetic and copies ran while one was open for 1% of the time, Pallas kernels for 0%

profile of v3, /device:TPU:8, one launch (start us, length us, event | category | flops | bytes accessed | tf_op | source)
XLA Modules:
  0.0 89.3 jit_solution(1502408349556119120)
XLA Ops:
  0.6 0.0 copy-start
  0.6 2.6 %shard_map.95 = bf16[16,3,128,128]{3,2,1,0:T(8,128)(2,1)} custom-call(bf16[128,2048]{1,0:T(8,128)(2,1)} %q_ref.1, bf16[128,2048]{1,0:T(8,128)(2,1)} %k_ref.1, bf16[128,2048]{1,0:T(8,128)(2,1)} %v_ref.1), custom_call_target="tpu_custom_call" | custom-call | tf_op jit(solution)/shard_map/pallas_call | solution.py:91
  3.2 0.0 copy-start.1
  3.2 0.0 copy-start.2
  3.2 42.5 %all_to_all.10.q_ref.k_ref.v_ref = bf16[16,3,128,128]{3,2,1,0:T(8,128)(2,1)S(1)} all-to-all(bf16[16,3,128,128]{3,2,1,0:T(8,128)(2,1)} %shard_map.95), channel_id=1, replica_groups=mesh['groups'=2,'seq'=16] {'seq'}, dimensions={0} | all-to-all | bytes 3145728 | tf_op jit(solution)/shard_map/all_to_all | solution.py:106
  45.8 0.0 copy-done.1
  45.8 0.0 copy-done.2
  45.8 10.5 %shard_map.96 = bf16[16,128,128]{2,1,0:T(8,128)(2,1)S(1)} custom-call(s32[1]{0:T(128)} %constant.17.clone.1.share_ref, bf16[16,3,128,128]{3,2,1,0:T(8,128)(2,1)S(1)} %all_to_all.10.q_ref.k_ref.v_ref, bf16[16,3,128,128]{3,2,1,0:T(8,128)(2,1)S(1)} %all_to_all.10.q_ref.k_ref.v_ref, bf16[16,3,128,128]{3,2,1,0:T(8,128)(2,1)S(1)} %all_to_all.10.q_ref.k_ref.v_ref, ...), custom_call_target="tpu_custom_call" | custom-call | tf_op jit(solution)/shard_map/pallas_call | solution.py:56
  56.2 18.4 %all_to_all.11 = bf16[16,128,128]{2,1,0:T(8,128)(2,1)S(1)} all-to-all(bf16[16,128,128]{2,1,0:T(8,128)(2,1)S(1)} %shard_map.96), channel_id=1, replica_groups=mesh['groups'=2,'seq'=16] {'seq'}, dimensions={0} | all-to-all | bytes 1048576 | tf_op jit(solution)/shard_map/all_to_all | solution.py:114
  74.7 0.3 copy.10
  74.9 1.0 %copy.11 = bf16[128,2048]{1,0:T(8,128)(2,1)} copy(bf16[128,2048]{0,1:T(8,128)(2,1)S(1)} %bitcast.25) | data formatting | bytes 1048576
  76.0 0.0 copy-done
  76.0 0.0 copy-start.3
  76.0 0.5 convolution_convert_fusion.1
  76.4 0.0 copy-start.4
  76.4 3.3 %collective-permute-start.1 = (bf16[128,512]{1,0:T(8,128)(2,1)S(1)}, bf16[128,512]{1,0:T(8,128)(2,1)S(1)}, u32[]{:S(2)}, u32[]{:S(2)}) collective-permute-start(bf16[128,512]{1,0:T(8,128)(2,1)S(1)} %convolution_convert_fusion.1), channel_id=1, source_target_pairs={{0,2},{1,3},{2,4},{3,5},{4,6},{5,7},{6,8},{7,9},{8,10},{9,11},{10,... | collective-permute-start | bytes 393224 | tf_op jit(solution)/shard_map/ppermute | solution.py:18
  79.8 1.9 %collective-permute-start = (bf16[128,512]{1,0:T(8,128)(2,1)S(1)}, bf16[128,512]{1,0:T(8,128)(2,1)S(1)}, u32[]{:S(2)}, u32[]{:S(2)}) collective-permute-start(bf16[128,512]{1,0:T(8,128)(2,1)S(1)} %convolution_convert_fusion.1), channel_id=1, source_target_pairs={{0,1},{1,2},{2,3},{3,4},{4,5},{5,6},{6,7},{7,8},{8,9},{9,10},{10,1... | collective-permute-start | bytes 393224 | tf_op jit(solution)/shard_map/ppermute | solution.py:18
  81.7 0.0 copy-done.3
  81.7 0.2 fusion.2
  81.9 5.0 %collective-permute-done = bf16[128,512]{1,0:T(8,128)(2,1)S(1)} collective-permute-done((bf16[128,512]{1,0:T(8,128)(2,1)S(1)}, bf16[128,512]{1,0:T(8,128)(2,1)S(1)}, u32[]{:S(2)}, u32[]{:S(2)}) %collective-permute-start) | collective-permute-done | bytes 131104 | tf_op jit(solution)/shard_map/ppermute | solution.py:18
  86.9 0.2 convolution_add_fusion.1
  87.2 0.0 collective-permute-done.1
  87.2 0.0 copy-done.4
  87.2 2.1 %convolution_convert_fusion = bf16[128,512]{1,0:T(8,128)(2,1)} fusion(bf16[512,512]{1,0:T(8,128)(2,1)S(1)} %copy-done.4, f32[128,512]{1,0:T(8,128)S(1)} %convolution_add_fusion.1, bf16[128,512]{1,0:T(8,128)(2,1)S(1)} %collective-permute-done.1, bf16[3,512,512]{2,1,0:T(8,128)(2,1)} %param.14), kind=kOutput, calls=%fused_computation.2 | convolution fusion | flops 134676480 | bytes 1572864 | tf_op jit(solution)/shard_map/dot_general | solution.py:125
Async XLA Ops:
  0.6 75.3 %copy-start = (bf16[2048,512]{1,0:T(8,128)(2,1)S(1)}, bf16[2048,512]{1,0:T(8,128)(2,1)}, u32[]{:S(2)}) copy-start(bf16[2048,512]{1,0:T(8,128)(2,1)} %param.13) | copy-start | bytes 6291460
  3.2 42.5 %copy-start.1 = (f32[128]{0:T(128)S(1)}, f32[128]{0:T(128)}, u32[]{:S(2)}) copy-start(f32[128]{0:T(128)} %param.11) | copy-start | bytes 1540
  3.2 42.5 %copy-start.2 = (f32[128]{0:T(128)S(1)}, f32[128]{0:T(128)}, u32[]{:S(2)}) copy-start(f32[128]{0:T(128)} %param.12) | copy-start | bytes 1540
  76.0 5.7 %copy-start.3 = (bf16[3,512,512]{2,1,0:T(8,128)(2,1)S(1)}, bf16[3,512,512]{2,1,0:T(8,128)(2,1)}, u32[]{:S(2)}) copy-start(bf16[3,512,512]{2,1,0:T(8,128)(2,1)} %param.14) | copy-start | bytes 4718596
  76.4 10.8 %copy-start.4 = (bf16[512,512]{1,0:T(8,128)(2,1)S(1)}, bf16[512,512]{1,0:T(8,128)(2,1)}, u32[]{:S(2)}) copy-start(bf16[512,512]{1,0:T(8,128)(2,1)} %param.15) | copy-start | bytes 1572868
  76.4 10.7 %collective-permute-start.1 = (bf16[128,512]{1,0:T(8,128)(2,1)S(1)}, bf16[128,512]{1,0:T(8,128)(2,1)S(1)}, u32[]{:S(2)}, u32[]{:S(2)}) collective-permute-start(bf16[128,512]{1,0:T(8,128)(2,1)S(1)} %convolution_convert_fusion.1), channel_id=1, source_target_pairs={{0,2},{1,3},{2,4},{3,5},{4,6},{5,7},{6,8},{7,9},{8,10},{9,11},{10,... | collective-permute-start | bytes 393224 | tf_op jit(solution)/shard_map/ppermute | solution.py:18
  79.8 7.2 %collective-permute-start = (bf16[128,512]{1,0:T(8,128)(2,1)S(1)}, bf16[128,512]{1,0:T(8,128)(2,1)S(1)}, u32[]{:S(2)}, u32[]{:S(2)}) collective-permute-start(bf16[128,512]{1,0:T(8,128)(2,1)S(1)} %convolution_convert_fusion.1), channel_id=1, source_target_pairs={{0,1},{1,2},{2,3},{3,4},{4,5},{5,6},{6,7},{7,8},{8,9},{9,10},{10,1... | collective-permute-start | bytes 393224 | tf_op jit(solution)/shard_map/ppermute | solution.py:18

commit v4 on v3

--- a/solution.py
+++ b/solution.py
@@ -38,9 +38,9 @@
     v = v_ref[...]
     v = v.reshape(v.shape[0] * v.shape[1], HD)
     s = lax.dot_general(qn, kn, (((1,), (1,)), ((), ())), preferred_element_type=jnp.float32)
-    s = s * (1.0 / math.sqrt(HD))
+    c = math.log2(math.e) / math.sqrt(HD)
     m = jnp.max(s, axis=-1, keepdims=True)
-    e = jnp.exp(s - m)
+    e = jnp.exp2(s * c - m * c)
     total = jnp.sum(e, axis=-1, keepdims=True)
     out = jnp.dot(e.astype(jnp.bfloat16), v, preferred_element_type=jnp.float32)
     out = (out / total).astype(jnp.bfloat16)
@@ -97,6 +97,36 @@
     )(queries, keys, values)
 
 
+def _latent_kernel(b_ref, w_ref, z_ref):
+    acc = jnp.zeros(z_ref.shape, jnp.float32)
+    for h in range(b_ref.shape[0]):
+        acc = acc + jnp.dot(b_ref[h], w_ref[h * HD:(h + 1) * HD, :], preferred_element_type=jnp.float32)
+    z_ref[...] = acc.astype(z_ref.dtype)
+
+
+def latent_of(back, w_latent):
+    heads, rows, _ = back.shape
+    return pl.pallas_call(
+        _latent_kernel,
+        out_shape=jax.ShapeDtypeStruct((rows, w_latent.shape[1]), jnp.bfloat16),
+    )(back, w_latent)
+
+
+def _decode_kernel(z_ref, e1_ref, e2_ref, wt_ref, wd_ref, o_ref):
+    state = jnp.dot(z_ref[...], wt_ref[0], preferred_element_type=jnp.float32)
+    state = state + jnp.dot(e1_ref[...], wt_ref[1], preferred_element_type=jnp.float32)
+    state = state + jnp.dot(e2_ref[...], wt_ref[2], preferred_element_type=jnp.float32)
+    act = jax.nn.silu(state).astype(jnp.bfloat16)
+    o_ref[...] = jnp.dot(act, wd_ref[...], preferred_element_type=jnp.float32).astype(o_ref.dtype)
+
+
+def decode(latent, earlier_one, earlier_two, w_temporal, w_decode):
+    return pl.pallas_call(
+        _decode_kernel,
+        out_shape=jax.ShapeDtypeStruct((latent.shape[0], w_decode.shape[1]), jnp.bfloat16),
+    )(latent, earlier_one, earlier_two, w_temporal, w_decode)
+
+
 def body(queries, keys, values, gain_q, gain_k, w_latent, w_temporal, w_decode):
     devices = lax.axis_size("seq")
     copies = devices // HEADS
@@ -115,17 +145,13 @@
     if copies > 1:
         back = jnp.sum(back.reshape(HEADS, copies, rows, HD).astype(jnp.float32), axis=1)
         back = back.astype(jnp.bfloat16)
-    attention = jnp.transpose(back.reshape(HEADS, rows, HD), (1, 0, 2)).reshape(rows, HEADS * HD)
-    latent = jnp.dot(attention, w_latent, preferred_element_type=jnp.float32).astype(jnp.bfloat16)
+    back = back.reshape(HEADS, rows, HD)
+    latent = latent_of(back, w_latent)
     earlier_one = passed_along(latent, "seq", 1)
     earlier_two = passed_along(latent, "seq", 2)
-    state = jnp.dot(latent, w_temporal[0], preferred_element_type=jnp.float32)
-    state = state + jnp.dot(earlier_one, w_temporal[1], preferred_element_type=jnp.float32)
-    state = state + jnp.dot(earlier_two, w_temporal[2], preferred_element_type=jnp.float32)
-    decoded = jnp.dot(
-        jax.nn.silu(state).astype(jnp.bfloat16), w_decode, preferred_element_type=jnp.float32
-    )
-    return (attention, decoded.astype(jnp.bfloat16))
+    attention = jnp.transpose(back, (1, 0, 2)).reshape(rows, HEADS * HD)
+    decoded = decode(latent, earlier_one, earlier_two, w_temporal, w_decode)
+    return (attention, decoded)
 
 
 def solution(mesh):

time: 89.7 us -> 91.9 us (1.025)
  Pallas kernels: 13 us -> 18.6 us
  matrix products: 3.07 us -> 0 us
    pallas_call x0 -> x2, Pallas kernels: none -> 6.03 us  [the longest x1 3.14 us: latent_of(): pl.pallas_call(_latent_kernel, out_shape=jax.ShapeDtypeStruct((rows, w_la...]
    dot_general x4 -> x0, matrix products: 3.07 us -> none  [the longest x1 2.14 us: body(): jnp.dot(jax.nn.silu(state).astype(jnp.bfloat16), w_decode, preferred_elem...]
  transfers between devices with their start and end apart: 2 -> 2, of which waited for: 1 -> 2; matrix products, arithmetic and copies ran while one was open for 1% -> 1% of each run, Pallas kernels for 0% -> 0%
where the time goes in v4:
time: 91.9 us; the launch traced here: 91.6 us
  blocking collectives  61.1 us (66%)
  Pallas kernels  18.6 us (20%)
  starting transfers between devices  5.09 us (6%)
  waiting for transfers between devices  4.15 us (5%)
  local copies, waits for them, and re-layouts  1.96 us (2%)
    all_to_all x1, blocking collectives, body(): lax.all_to_all(stacked, 'seq', split_axis=0, concat_axis=0, tiled=True)  42.5 us
    all_to_all x1, blocking collectives, body(): back = lax.all_to_all(out, 'seq', split_axis=0, concat_axis=0, tiled=True)  18.5 us
    pallas_call x1, Pallas kernels, attend(): pl.pallas_call(_attn_kernel, out_shape=jax.ShapeDtypeStruct((span_blocks,...  10.2 us
    ppermute x2, starting transfers between devices, passed_along(): return lax.ppermute(shard, axis, pairs)  5.09 us
    ppermute x2, waiting for transfers between devices, passed_along(): return lax.ppermute(shard, axis, pairs)  4.15 us
    pallas_call x1, Pallas kernels, latent_of(): pl.pallas_call(_latent_kernel, out_shape=jax.ShapeDtypeStruct((rows, w_la...  3.14 us
    pallas_call x1, Pallas kernels, decode(): pl.pallas_call(_decode_kernel, out_shape=jax.ShapeDtypeStruct((latent.sha...  2.89 us
    pallas_call x1, Pallas kernels, pack(): pl.pallas_call(_pack_kernel, out_shape=jax.ShapeDtypeStruct((HEADS * copi...  2.42 us
  transfers between devices with their start and end apart: 2, of which 2 were waited for; matrix products, arithmetic and copies ran while one was open for 1% of the time, Pallas kernels for 0%

profile of v4, /device:TPU:8, one launch (start us, length us, event | category | flops | bytes accessed | tf_op | source)
XLA Modules:
  0.0 91.6 jit_solution(7496172641399225520)
XLA Ops:
  0.6 2.4 %shard_map.95 = bf16[16,3,128,128]{3,2,1,0:T(8,128)(2,1)} custom-call(bf16[128,2048]{1,0:T(8,128)(2,1)} %q_ref.1, bf16[128,2048]{1,0:T(8,128)(2,1)} %k_ref.1, bf16[128,2048]{1,0:T(8,128)(2,1)} %v_ref.1), custom_call_target="tpu_custom_call" | custom-call | tf_op jit(solution)/shard_map/pallas_call | solution.py:91
  3.0 0.0 copy-start
  3.1 0.0 copy-start.1
  3.1 42.5 %all_to_all.10.q_ref.k_ref.v_ref = bf16[16,3,128,128]{3,2,1,0:T(8,128)(2,1)S(1)} all-to-all(bf16[16,3,128,128]{3,2,1,0:T(8,128)(2,1)} %shard_map.95), channel_id=1, replica_groups=mesh['groups'=2,'seq'=16] {'seq'}, dimensions={0} | all-to-all | bytes 3145728 | tf_op jit(solution)/shard_map/all_to_all | solution.py:136
  45.6 0.0 copy-done
  45.6 0.0 copy-done.1
  45.6 10.2 %shard_map.96 = bf16[16,128,128]{2,1,0:T(8,128)(2,1)S(1)} custom-call(s32[1]{0:T(128)} %constant.15.clone.1.share_ref, bf16[16,3,128,128]{3,2,1,0:T(8,128)(2,1)S(1)} %all_to_all.10.q_ref.k_ref.v_ref, bf16[16,3,128,128]{3,2,1,0:T(8,128)(2,1)S(1)} %all_to_all.10.q_ref.k_ref.v_ref, bf16[16,3,128,128]{3,2,1,0:T(8,128)(2,1)S(1)} %all_to_all.10.q_ref.k_ref.v_ref, ...), custom_call_target="tpu_custom_call" | custom-call | tf_op jit(solution)/shard_map/pallas_call | solution.py:56
  55.8 18.5 %all_to_all.11.b_ref = bf16[16,128,128]{2,1,0:T(8,128)(2,1)} all-to-all(bf16[16,128,128]{2,1,0:T(8,128)(2,1)S(1)} %shard_map.96), channel_id=1, replica_groups=mesh['groups'=2,'seq'=16] {'seq'}, dimensions={0} | all-to-all | bytes 1048576 | tf_op jit(solution)/shard_map/all_to_all | solution.py:144
  74.3 0.0 copy-start.2
  74.3 3.1 %shard_map.97.z_ref = bf16[128,512]{1,0:T(8,128)(2,1)} custom-call(bf16[16,128,128]{2,1,0:T(8,128)(2,1)} %all_to_all.11.b_ref, bf16[2048,512]{1,0:T(8,128)(2,1)} %w_ref.1), custom_call_target="tpu_custom_call" | custom-call | tf_op jit(solution)/shard_map/pallas_call | solution.py:109
  77.5 3.2 %collective-permute-start.1 = (bf16[128,512]{1,0:T(8,128)(2,1)}, bf16[128,512]{1,0:T(8,128)(2,1)S(1)}, u32[]{:S(2)}, u32[]{:S(2)}) collective-permute-start(bf16[128,512]{1,0:T(8,128)(2,1)} %shard_map.97.z_ref), channel_id=1, source_target_pairs={{0,2},{1,3},{2,4},{3,5},{4,6},{5,7},{6,8},{7,9},{8,10},{9,11},{10,... | collective-permute-start | bytes 393224 | tf_op jit(solution)/shard_map/ppermute | solution.py:18
  80.6 1.9 %collective-permute-start = (bf16[128,512]{1,0:T(8,128)(2,1)}, bf16[128,512]{1,0:T(8,128)(2,1)S(1)}, u32[]{:S(2)}, u32[]{:S(2)}) collective-permute-start(bf16[128,512]{1,0:T(8,128)(2,1)} %shard_map.97.z_ref), channel_id=1, source_target_pairs={{0,1},{1,2},{2,3},{3,4},{4,5},{5,6},{6,7},{7,8},{8,9},{9,10},{10,1... | collective-permute-start | bytes 393224 | tf_op jit(solution)/shard_map/ppermute | solution.py:18
  82.6 0.0 copy-done.2
  82.6 0.3 copy.10
  82.9 1.0 %copy.11 = bf16[128,2048]{1,0:T(8,128)(2,1)} copy(bf16[128,2048]{0,1:T(8,128)(2,1)S(1)} %bitcast.7) | data formatting | bytes 1048576
  83.9 2.6 %collective-permute-done.1.e2_ref = bf16[128,512]{1,0:T(8,128)(2,1)S(1)} collective-permute-done((bf16[128,512]{1,0:T(8,128)(2,1)}, bf16[128,512]{1,0:T(8,128)(2,1)S(1)}, u32[]{:S(2)}, u32[]{:S(2)}) %collective-permute-start.1) | collective-permute-done | bytes 131104 | tf_op jit(solution)/shard_map/ppermute | solution.py:18
  86.5 0.0 copy-start.3
  86.5 1.5 %collective-permute-done.e1_ref = bf16[128,512]{1,0:T(8,128)(2,1)S(1)} collective-permute-done((bf16[128,512]{1,0:T(8,128)(2,1)}, bf16[128,512]{1,0:T(8,128)(2,1)S(1)}, u32[]{:S(2)}, u32[]{:S(2)}) %collective-permute-start) | collective-permute-done | bytes 131104 | tf_op jit(solution)/shard_map/ppermute | solution.py:18
  88.0 0.0 copy-done.3
  88.0 0.0 copy-start.4
  88.0 0.6 copy-done.4
  88.7 2.9 %shard_map.98 = bf16[128,512]{1,0:T(8,128)(2,1)} custom-call(bf16[128,512]{1,0:T(8,128)(2,1)} %shard_map.97.z_ref, bf16[128,512]{1,0:T(8,128)(2,1)} %copy-done.4, bf16[128,512]{1,0:T(8,128)(2,1)} %copy-done.3, bf16[3,512,512]{2,1,0:T(8,128)(2,1)} %wt_ref.1, bf16[512,512]{1,0:T(8,128)(2,1)} %wd_ref.1), custom_call_target="tpu_custom_call" | custom-call | tf_op jit(solution)/shard_map/pallas_call | solution.py:124
Async XLA Ops:
  3.0 42.5 %copy-start = (f32[128]{0:T(128)S(1)}, f32[128]{0:T(128)}, u32[]{:S(2)}) copy-start(f32[128]{0:T(128)} %param.11) | copy-start | bytes 1540
  3.1 42.5 %copy-start.1 = (f32[128]{0:T(128)S(1)}, f32[128]{0:T(128)}, u32[]{:S(2)}) copy-start(f32[128]{0:T(128)} %param.12) | copy-start | bytes 1540
  74.3 8.3 %copy-start.2 = (bf16[16,128,128]{2,1,0:T(8,128)(2,1)S(1)}, bf16[16,128,128]{2,1,0:T(8,128)(2,1)}, u32[]{:S(2)}) copy-start(bf16[16,128,128]{2,1,0:T(8,128)(2,1)} %all_to_all.11.b_ref) | copy-start | bytes 1572868
  77.5 9.0 %collective-permute-start.1 = (bf16[128,512]{1,0:T(8,128)(2,1)}, bf16[128,512]{1,0:T(8,128)(2,1)S(1)}, u32[]{:S(2)}, u32[]{:S(2)}) collective-permute-start(bf16[128,512]{1,0:T(8,128)(2,1)} %shard_map.97.z_ref), channel_id=1, source_target_pairs={{0,2},{1,3},{2,4},{3,5},{4,6},{5,7},{6,8},{7,9},{8,10},{9,11},{10,... | collective-permute-start | bytes 393224 | tf_op jit(solution)/shard_map/ppermute | solution.py:18
  80.6 7.4 %collective-permute-start = (bf16[128,512]{1,0:T(8,128)(2,1)}, bf16[128,512]{1,0:T(8,128)(2,1)S(1)}, u32[]{:S(2)}, u32[]{:S(2)}) collective-permute-start(bf16[128,512]{1,0:T(8,128)(2,1)} %shard_map.97.z_ref), channel_id=1, source_target_pairs={{0,1},{1,2},{2,3},{3,4},{4,5},{5,6},{6,7},{7,8},{8,9},{9,10},{10,1... | collective-permute-start | bytes 393224 | tf_op jit(solution)/shard_map/ppermute | solution.py:18
  86.5 1.5 %copy-start.3 = (bf16[128,512]{1,0:T(8,128)(2,1)}, bf16[128,512]{1,0:T(8,128)(2,1)S(1)}, u32[]{:S(2)}) copy-start(bf16[128,512]{1,0:T(8,128)(2,1)S(1)} %collective-permute-done.1.e2_ref) | copy-start | bytes 393220
  88.0 0.6 copy-start.4

commit v5 on v3

--- a/solution.py
+++ b/solution.py
@@ -24,33 +24,32 @@
     return x.astype(jnp.bfloat16)
 
 
-def _attn_kernel(share_ref, q_ref, k_ref, v_ref, gq_ref, gk_ref, o_ref, kn_ref):
+def _attn_kernel(share_ref, q_ref, k_ref, v_ref, gq_ref, gk_ref, o_ref, kn_ref, vt_ref):
     @pl.when(pl.program_id(0) == 0)
     def _():
         k = k_ref[...]
         k = k.reshape(k.shape[0] * k.shape[1], HD)
         kn_ref[...] = _norm(k, gk_ref[...])
+        v = v_ref[...]
+        vt_ref[...] = v.reshape(v.shape[0] * v.shape[1], HD).T
 
     q = q_ref[...]
     q = q.reshape(q.shape[0] * q.shape[1], HD)
-    qn = _norm(q, gq_ref[...])
-    kn = kn_ref[...]
-    v = v_ref[...]
-    v = v.reshape(v.shape[0] * v.shape[1], HD)
-    s = lax.dot_general(qn, kn, (((1,), (1,)), ((), ())), preferred_element_type=jnp.float32)
-    s = s * (1.0 / math.sqrt(HD))
-    m = jnp.max(s, axis=-1, keepdims=True)
-    e = jnp.exp(s - m)
-    total = jnp.sum(e, axis=-1, keepdims=True)
-    out = jnp.dot(e.astype(jnp.bfloat16), v, preferred_element_type=jnp.float32)
-    out = (out / total).astype(jnp.bfloat16)
+    qt = _norm(q, gq_ref[...]).T
+    st = jnp.dot(kn_ref[...], qt, preferred_element_type=jnp.float32)
+    c = math.log2(math.e) / math.sqrt(HD)
+    m = jnp.max(st, axis=0, keepdims=True)
+    e = jnp.exp2(st * c - m * c)
+    total = jnp.sum(e, axis=0, keepdims=True)
+    out_t = jnp.dot(vt_ref[...], e.astype(jnp.bfloat16), preferred_element_type=jnp.float32)
+    out = (out_t / total).T.astype(jnp.bfloat16)
     o_ref[...] = out.reshape(o_ref.shape)
 
 
-def attend(got, share, span_blocks, gain_q, gain_k, qb_rows=256):
+def attend(got, share, span_blocks, gain_q, gain_k):
     src, _, rows, _ = got.shape
-    qb = max(1, qb_rows // rows)
-    qb = min(qb, span_blocks)
+    tokens = src * rows
+    qb = max(1, min(span_blocks, (4 << 20) // (tokens * rows)))
     steps = span_blocks // qb
     tokens = src * rows
     return pl.pallas_call(
@@ -67,7 +66,7 @@
                 pl.BlockSpec((1, HD), lambda i, sh: (0, 0)),
             ],
             out_specs=pl.BlockSpec((qb, rows, HD), lambda i, sh: (i, 0, 0)),
-            scratch_shapes=[pltpu.VMEM((tokens, HD), jnp.bfloat16)],
+            scratch_shapes=[pltpu.VMEM((tokens, HD), jnp.bfloat16), pltpu.VMEM((HD, tokens), jnp.bfloat16)],
         ),
         compiler_params=pltpu.CompilerParams(
             dimension_semantics=("arbitrary",), vmem_limit_bytes=48 * 1024 * 1024

time: 89.7 us -> 85.2 us (0.950)
  Pallas kernels: 13 us -> 8.56 us
    pallas_call x1, Pallas kernels: 10.5 us -> 6 us  [attend(): pl.pallas_call(_attn_kernel, out_shape=jax.ShapeDtypeStruct((span_blocks,...]
where the time goes in v5:
time: 85.2 us; the launch traced here: 84.9 us
  blocking collectives  61 us (72%)
  Pallas kernels  8.56 us (10%)
  starting transfers between devices  5.23 us (6%)
  waiting for transfers between devices  5.01 us (6%)
  matrix products  3.07 us (4%)
  local copies, waits for them, and re-layouts  1.32 us (2%)
    all_to_all x1, blocking collectives, body(): lax.all_to_all(stacked, 'seq', split_axis=0, concat_axis=0, tiled=True)  42.5 us
    all_to_all x1, blocking collectives, body(): back = lax.all_to_all(out, 'seq', split_axis=0, concat_axis=0, tiled=True)  18.4 us
    pallas_call x1, Pallas kernels, attend(): pl.pallas_call(_attn_kernel, out_shape=jax.ShapeDtypeStruct((span_blocks,...  6 us
    ppermute x2, starting transfers between devices, passed_along(): return lax.ppermute(shard, axis, pairs)  5.23 us
    ppermute x2, waiting for transfers between devices, passed_along(): return lax.ppermute(shard, axis, pairs)  5.01 us
    pallas_call x1, Pallas kernels, pack(): pl.pallas_call(_pack_kernel, out_shape=jax.ShapeDtypeStruct((HEADS * copi...  2.56 us
    dot_general x1, matrix products, body(): jnp.dot(jax.nn.silu(state).astype(jnp.bfloat16), w_decode, preferred_elem...  2.14 us
  transfers between devices with their start and end apart: 2, of which 1 were waited for; matrix products, arithmetic and copies ran while one was open for 1% of the time, Pallas kernels for 0%

profile of v5, /device:TPU:8, one launch (start us, length us, event | category | flops | bytes accessed | tf_op | source)
XLA Modules:
  0.0 84.9 jit_solution(2064929969382741590)
XLA Ops:
  0.6 0.0 copy-start
  0.6 2.6 %shard_map.95 = bf16[16,3,128,128]{3,2,1,0:T(8,128)(2,1)} custom-call(bf16[128,2048]{1,0:T(8,128)(2,1)} %q_ref.1, bf16[128,2048]{1,0:T(8,128)(2,1)} %k_ref.1, bf16[128,2048]{1,0:T(8,128)(2,1)} %v_ref.1), custom_call_target="tpu_custom_call" | custom-call | tf_op jit(solution)/shard_map/pallas_call | solution.py:90
  3.2 0.0 copy-start.1
  3.2 0.0 copy-start.2
  3.2 42.5 %all_to_all.10.q_ref.k_ref.v_ref = bf16[16,3,128,128]{3,2,1,0:T(8,128)(2,1)S(1)} all-to-all(bf16[16,3,128,128]{3,2,1,0:T(8,128)(2,1)} %shard_map.95), channel_id=1, replica_groups=mesh['groups'=2,'seq'=16] {'seq'}, dimensions={0} | all-to-all | bytes 3145728 | tf_op jit(solution)/shard_map/all_to_all | solution.py:105
  45.8 0.0 copy-done.1
  45.8 0.0 copy-done.2
  45.8 6.0 %shard_map.96 = bf16[16,128,128]{2,1,0:T(8,128)(2,1)S(1)} custom-call(s32[1]{0:T(128)} %constant.17.clone.1.share_ref, bf16[16,3,128,128]{3,2,1,0:T(8,128)(2,1)S(1)} %all_to_all.10.q_ref.k_ref.v_ref, bf16[16,3,128,128]{3,2,1,0:T(8,128)(2,1)S(1)} %all_to_all.10.q_ref.k_ref.v_ref, bf16[16,3,128,128]{3,2,1,0:T(8,128)(2,1)S(1)} %all_to_all.10.q_ref.k_ref.v_ref, ...), custom_call_target="tpu_custom_call" | custom-call | tf_op jit(solution)/shard_map/pallas_call | solution.py:55
  51.8 18.4 %all_to_all.11 = bf16[16,128,128]{2,1,0:T(8,128)(2,1)S(1)} all-to-all(bf16[16,128,128]{2,1,0:T(8,128)(2,1)S(1)} %shard_map.96), channel_id=1, replica_groups=mesh['groups'=2,'seq'=16] {'seq'}, dimensions={0} | all-to-all | bytes 1048576 | tf_op jit(solution)/shard_map/all_to_all | solution.py:113
  70.2 0.3 copy.10
  70.5 1.0 %copy.11 = bf16[128,2048]{1,0:T(8,128)(2,1)} copy(bf16[128,2048]{0,1:T(8,128)(2,1)S(1)} %bitcast.25) | data formatting | bytes 1048576
  71.5 0.0 copy-done
  71.5 0.0 copy-start.3
  71.5 0.5 convolution_convert_fusion.1
  72.0 0.0 copy-start.4
  72.0 3.3 %collective-permute-start.1 = (bf16[128,512]{1,0:T(8,128)(2,1)S(1)}, bf16[128,512]{1,0:T(8,128)(2,1)S(1)}, u32[]{:S(2)}, u32[]{:S(2)}) collective-permute-start(bf16[128,512]{1,0:T(8,128)(2,1)S(1)} %convolution_convert_fusion.1), channel_id=1, source_target_pairs={{0,2},{1,3},{2,4},{3,5},{4,6},{5,7},{6,8},{7,9},{8,10},{9,11},{10,... | collective-permute-start | bytes 393224 | tf_op jit(solution)/shard_map/ppermute | solution.py:18
  75.3 1.9 %collective-permute-start = (bf16[128,512]{1,0:T(8,128)(2,1)S(1)}, bf16[128,512]{1,0:T(8,128)(2,1)S(1)}, u32[]{:S(2)}, u32[]{:S(2)}) collective-permute-start(bf16[128,512]{1,0:T(8,128)(2,1)S(1)} %convolution_convert_fusion.1), channel_id=1, source_target_pairs={{0,1},{1,2},{2,3},{3,4},{4,5},{5,6},{6,7},{7,8},{8,9},{9,10},{10,1... | collective-permute-start | bytes 393224 | tf_op jit(solution)/shard_map/ppermute | solution.py:18
  77.2 0.0 copy-done.3
  77.2 0.2 fusion.2
  77.5 5.0 %collective-permute-done = bf16[128,512]{1,0:T(8,128)(2,1)S(1)} collective-permute-done((bf16[128,512]{1,0:T(8,128)(2,1)S(1)}, bf16[128,512]{1,0:T(8,128)(2,1)S(1)}, u32[]{:S(2)}, u32[]{:S(2)}) %collective-permute-start) | collective-permute-done | bytes 131104 | tf_op jit(solution)/shard_map/ppermute | solution.py:18
  82.5 0.2 convolution_add_fusion.1
  82.7 0.0 collective-permute-done.1
  82.7 0.0 copy-done.4
  82.7 2.1 %convolution_convert_fusion = bf16[128,512]{1,0:T(8,128)(2,1)} fusion(bf16[512,512]{1,0:T(8,128)(2,1)S(1)} %copy-done.4, f32[128,512]{1,0:T(8,128)S(1)} %convolution_add_fusion.1, bf16[128,512]{1,0:T(8,128)(2,1)S(1)} %collective-permute-done.1, bf16[3,512,512]{2,1,0:T(8,128)(2,1)} %param.14), kind=kOutput, calls=%fused_computation.2 | convolution fusion | flops 134676480 | bytes 1572864 | tf_op jit(solution)/shard_map/dot_general | solution.py:124
Async XLA Ops:
  0.6 70.9 %copy-start = (bf16[2048,512]{1,0:T(8,128)(2,1)S(1)}, bf16[2048,512]{1,0:T(8,128)(2,1)}, u32[]{:S(2)}) copy-start(bf16[2048,512]{1,0:T(8,128)(2,1)} %param.13) | copy-start | bytes 6291460
  3.2 42.5 %copy-start.1 = (f32[128]{0:T(128)S(1)}, f32[128]{0:T(128)}, u32[]{:S(2)}) copy-start(f32[128]{0:T(128)} %param.11) | copy-start | bytes 1540
  3.2 42.5 %copy-start.2 = (f32[128]{0:T(128)S(1)}, f32[128]{0:T(128)}, u32[]{:S(2)}) copy-start(f32[128]{0:T(128)} %param.12) | copy-start | bytes 1540
  71.5 5.7 %copy-start.3 = (bf16[3,512,512]{2,1,0:T(8,128)(2,1)S(1)}, bf16[3,512,512]{2,1,0:T(8,128)(2,1)}, u32[]{:S(2)}) copy-start(bf16[3,512,512]{2,1,0:T(8,128)(2,1)} %param.14) | copy-start | bytes 4718596
  72.0 10.8 %copy-start.4 = (bf16[512,512]{1,0:T(8,128)(2,1)S(1)}, bf16[512,512]{1,0:T(8,128)(2,1)}, u32[]{:S(2)}) copy-start(bf16[512,512]{1,0:T(8,128)(2,1)} %param.15) | copy-start | bytes 1572868
  72.0 10.7 %collective-permute-start.1 = (bf16[128,512]{1,0:T(8,128)(2,1)S(1)}, bf16[128,512]{1,0:T(8,128)(2,1)S(1)}, u32[]{:S(2)}, u32[]{:S(2)}) collective-permute-start(bf16[128,512]{1,0:T(8,128)(2,1)S(1)} %convolution_convert_fusion.1), channel_id=1, source_target_pairs={{0,2},{1,3},{2,4},{3,5},{4,6},{5,7},{6,8},{7,9},{8,10},{9,11},{10,... | collective-permute-start | bytes 393224 | tf_op jit(solution)/shard_map/ppermute | solution.py:18
  75.3 7.2 %collective-permute-start = (bf16[128,512]{1,0:T(8,128)(2,1)S(1)}, bf16[128,512]{1,0:T(8,128)(2,1)S(1)}, u32[]{:S(2)}, u32[]{:S(2)}) collective-permute-start(bf16[128,512]{1,0:T(8,128)(2,1)S(1)} %convolution_convert_fusion.1), channel_id=1, source_target_pairs={{0,1},{1,2},{2,3},{3,4},{4,5},{5,6},{6,7},{7,8},{8,9},{9,10},{10,1... | collective-permute-start | bytes 393224 | tf_op jit(solution)/shard_map/ppermute | solution.py:18

commit v6 on v5

--- a/solution.py
+++ b/solution.py
@@ -114,16 +114,18 @@
     if copies > 1:
         back = jnp.sum(back.reshape(HEADS, copies, rows, HD).astype(jnp.float32), axis=1)
         back = back.astype(jnp.bfloat16)
-    attention = jnp.transpose(back.reshape(HEADS, rows, HD), (1, 0, 2)).reshape(rows, HEADS * HD)
-    latent = jnp.dot(attention, w_latent, preferred_element_type=jnp.float32).astype(jnp.bfloat16)
+    back = back.reshape(HEADS, rows, HD)
+    latent = jnp.einsum(
+        "hrd,hdc->rc", back, w_latent.reshape(HEADS, HD, -1), preferred_element_type=jnp.float32
+    ).astype(jnp.bfloat16)
+    attention = jnp.transpose(back, (1, 0, 2)).reshape(rows, HEADS * HD)
     earlier_one = passed_along(latent, "seq", 1)
     earlier_two = passed_along(latent, "seq", 2)
     state = jnp.dot(latent, w_temporal[0], preferred_element_type=jnp.float32)
     state = state + jnp.dot(earlier_one, w_temporal[1], preferred_element_type=jnp.float32)
     state = state + jnp.dot(earlier_two, w_temporal[2], preferred_element_type=jnp.float32)
-    decoded = jnp.dot(
-        jax.nn.silu(state).astype(jnp.bfloat16), w_decode, preferred_element_type=jnp.float32
-    )
+    act = lax.optimization_barrier(jax.nn.silu(state).astype(jnp.bfloat16))
+    decoded = jnp.dot(act, w_decode, preferred_element_type=jnp.float32)
     return (attention, decoded.astype(jnp.bfloat16))
 
 

time: 85.2 us -> 85.2 us (level)
  waiting for transfers between devices: 5.01 us -> 2.67 us
  matrix products: 3.07 us -> 5.18 us
    ppermute x2, waiting for transfers between devices: 5.01 us -> 2.67 us  [passed_along(): return lax.ppermute(shard, axis, pairs)]
    dot_general x1, matrix products: 0.23 us -> 1.27 us  [body(): jnp.dot(earlier_one, w_temporal[1], preferred_element_type=jnp.float32)]
    dot_general x1, matrix products: 0.23 us -> 1.26 us  [body(): state = jnp.dot(latent, w_temporal[0], preferred_element_type=jnp.float32)]
    dot_general x2 -> x3, matrix products: 2.61 us -> 2.65 us  [the longest x1 1.32 us: body(): jnp.dot(earlier_two, w_temporal[2], preferred_element_type=jnp.float32)]
  transfers between devices with their start and end apart: 2 -> 2, of which waited for: 1 -> 1; matrix products, arithmetic and copies ran while one was open for 1% -> 5% of each run, Pallas kernels for 0% -> 0%
where the time goes in v6:
time: 85.2 us; the launch traced here: 84.5 us
  blocking collectives  61 us (72%)
  Pallas kernels  8.56 us (10%)
  matrix products  5.18 us (6%)
  starting transfers between devices  5.1 us (6%)
  waiting for transfers between devices  2.67 us (3%)
  local copies, waits for them, and re-layouts  1.32 us (2%)
    all_to_all x1, blocking collectives, body(): lax.all_to_all(stacked, 'seq', split_axis=0, concat_axis=0, tiled=True)  42.5 us
    all_to_all x1, blocking collectives, body(): back = lax.all_to_all(out, 'seq', split_axis=0, concat_axis=0, tiled=True)  18.4 us
    pallas_call x1, Pallas kernels, attend(): pl.pallas_call(_attn_kernel, out_shape=jax.ShapeDtypeStruct((span_blocks,...  5.99 us
    ppermute x2, starting transfers between devices, passed_along(): return lax.ppermute(shard, axis, pairs)  5.1 us
    ppermute x2, waiting for transfers between devices, passed_along(): return lax.ppermute(shard, axis, pairs)  2.67 us
    pallas_call x1, Pallas kernels, pack(): pl.pallas_call(_pack_kernel, out_shape=jax.ShapeDtypeStruct((HEADS * copi...  2.57 us
  transfers between devices with their start and end apart: 2, of which 1 were waited for; matrix products, arithmetic and copies ran while one was open for 5% of the time, Pallas kernels for 0%

profile of v6, /device:TPU:8, one launch (start us, length us, event | category | flops | bytes accessed | tf_op | source)
XLA Modules:
  0.0 84.5 jit_solution(7261916152365429104)
XLA Ops:
  0.6 0.0 copy-start
  0.6 2.6 %shard_map.95 = bf16[16,3,128,128]{3,2,1,0:T(8,128)(2,1)} custom-call(bf16[128,2048]{1,0:T(8,128)(2,1)} %q_ref.1, bf16[128,2048]{1,0:T(8,128)(2,1)} %k_ref.1, bf16[128,2048]{1,0:T(8,128)(2,1)} %v_ref.1), custom_call_target="tpu_custom_call" | custom-call | tf_op jit(solution)/shard_map/pallas_call | solution.py:90
  3.2 0.0 copy-start.1
  3.2 0.0 copy-start.2
  3.2 42.5 %all_to_all.10.q_ref.k_ref.v_ref = bf16[16,3,128,128]{3,2,1,0:T(8,128)(2,1)S(1)} all-to-all(bf16[16,3,128,128]{3,2,1,0:T(8,128)(2,1)} %shard_map.95), channel_id=1, replica_groups=mesh['groups'=2,'seq'=16] {'seq'}, dimensions={0} | all-to-all | bytes 3145728 | tf_op jit(solution)/shard_map/all_to_all | solution.py:105
  45.8 0.0 copy-done.1
  45.8 0.0 copy-done.2
  45.8 6.0 %shard_map.96 = bf16[16,128,128]{2,1,0:T(8,128)(2,1)S(1)} custom-call(s32[1]{0:T(128)} %constant.17.clone.1.share_ref, bf16[16,3,128,128]{3,2,1,0:T(8,128)(2,1)S(1)} %all_to_all.10.q_ref.k_ref.v_ref, bf16[16,3,128,128]{3,2,1,0:T(8,128)(2,1)S(1)} %all_to_all.10.q_ref.k_ref.v_ref, bf16[16,3,128,128]{3,2,1,0:T(8,128)(2,1)S(1)} %all_to_all.10.q_ref.k_ref.v_ref, ...), custom_call_target="tpu_custom_call" | custom-call | tf_op jit(solution)/shard_map/pallas_call | solution.py:55
  51.8 18.4 %all_to_all.11 = bf16[16,128,128]{2,1,0:T(8,128)(2,1)S(1)} all-to-all(bf16[16,128,128]{2,1,0:T(8,128)(2,1)S(1)} %shard_map.96), channel_id=1, replica_groups=mesh['groups'=2,'seq'=16] {'seq'}, dimensions={0} | all-to-all | bytes 1048576 | tf_op jit(solution)/shard_map/all_to_all | solution.py:113
  70.2 0.0 copy-done
  70.2 0.4 fusion
  70.6 3.2 %collective-permute-start.1 = (bf16[128,512]{1,0:T(8,128)(2,1)S(1)}, bf16[128,512]{1,0:T(8,128)(2,1)S(1)}, u32[]{:S(2)}, u32[]{:S(2)}) collective-permute-start(bf16[128,512]{1,0:T(8,128)(2,1)S(1)} %fusion), channel_id=1, source_target_pairs={{0,2},{1,3},{2,4},{3,5},{4,6},{5,7},{6,8},{7,9},{8,10},{9,11},{10,... | collective-permute-start | bytes 393224 | tf_op jit(solution)/shard_map/ppermute | solution.py:18
  73.8 1.9 %collective-permute-start = (bf16[128,512]{1,0:T(8,128)(2,1)S(1)}, bf16[128,512]{1,0:T(8,128)(2,1)S(1)}, u32[]{:S(2)}, u32[]{:S(2)}) collective-permute-start(bf16[128,512]{1,0:T(8,128)(2,1)S(1)} %fusion), channel_id=1, source_target_pairs={{0,1},{1,2},{2,3},{3,4},{4,5},{5,6},{6,7},{7,8},{8,9},{9,10},{10,1... | collective-permute-start | bytes 393224 | tf_op jit(solution)/shard_map/ppermute | solution.py:18
  75.8 0.3 copy.10
  76.1 1.0 %copy.11 = bf16[128,2048]{1,0:T(8,128)(2,1)} copy(bf16[128,2048]{0,1:T(8,128)(2,1)S(1)} %bitcast.31) | data formatting | bytes 1048576
  77.1 1.3 %fusion.3 = f32[128,512]{1,0:T(8,128)S(1)} fusion(bf16[128,512]{1,0:T(8,128)(2,1)S(1)} %fusion, bf16[3,512,512]{2,1,0:T(8,128)(2,1)} %param.14), kind=kOutput, calls=%fused_computation.7 | convolution fusion | flops 67108864 | bytes 917504 | tf_op jit(solution)/shard_map/dot_general | solution.py:124
  78.3 0.0 copy-start.3
  78.3 2.7 %collective-permute-done = bf16[128,512]{1,0:T(8,128)(2,1)S(1)} collective-permute-done((bf16[128,512]{1,0:T(8,128)(2,1)S(1)}, bf16[128,512]{1,0:T(8,128)(2,1)S(1)}, u32[]{:S(2)}, u32[]{:S(2)}) %collective-permute-start) | collective-permute-done | bytes 131104 | tf_op jit(solution)/shard_map/ppermute | solution.py:18
  81.0 1.3 %convolution_add_fusion.1 = f32[128,512]{1,0:T(8,128)S(1)} fusion(f32[128,512]{1,0:T(8,128)S(1)} %fusion.3, bf16[128,512]{1,0:T(8,128)(2,1)S(1)} %collective-permute-done, bf16[3,512,512]{2,1,0:T(8,128)(2,1)} %param.14), kind=kOutput, calls=%fused_computation.1 | convolution fusion | flops 67174400 | bytes 1179648 | tf_op jit(solution)/shard_map/dot_general | solution.py:125
  82.3 0.0 collective-permute-done.1
  82.3 1.3 %multiply_convert_fusion = bf16[128,512]{1,0:T(8,128)(2,1)S(1)} fusion(f32[128,512]{1,0:T(8,128)S(1)} %convolution_add_fusion.1, bf16[128,512]{1,0:T(8,128)(2,1)S(1)} %collective-permute-done.1, bf16[3,512,512]{2,1,0:T(8,128)(2,1)} %param.14), kind=kOutput, calls=%fused_computation.12 | convolution fusion | flops 67502080 | bytes 1048576 | tf_op jit(solution)/shard_map/dot_general | solution.py:126
  83.6 0.0 copy-done.3
  83.6 0.9 %convolution_convert_fusion = bf16[128,512]{1,0:T(8,128)(2,1)} fusion(bf16[128,512]{1,0:T(8,128)(2,1)S(1)} %multiply_convert_fusion, bf16[512,512]{1,0:T(8,128)(2,1)S(1)} %copy-done.3), kind=kOutput, calls=%fused_computation.3 | convolution fusion | flops 67174400 | bytes 786432 | tf_op jit(solution)/shard_map/dot_general | solution.py:128
Async XLA Ops:
  0.6 69.6 %copy-start = (bf16[2048,512]{1,0:T(8,128)(2,1)S(1)}, bf16[2048,512]{1,0:T(8,128)(2,1)}, u32[]{:S(2)}) copy-start(bf16[2048,512]{1,0:T(8,128)(2,1)} %param.13) | copy-start | bytes 6291460
  3.2 42.5 %copy-start.1 = (f32[128]{0:T(128)S(1)}, f32[128]{0:T(128)}, u32[]{:S(2)}) copy-start(f32[128]{0:T(128)} %param.11) | copy-start | bytes 1540
  3.2 42.5 %copy-start.2 = (f32[128]{0:T(128)S(1)}, f32[128]{0:T(128)}, u32[]{:S(2)}) copy-start(f32[128]{0:T(128)} %param.12) | copy-start | bytes 1540
  70.6 11.7 %collective-permute-start.1 = (bf16[128,512]{1,0:T(8,128)(2,1)S(1)}, bf16[128,512]{1,0:T(8,128)(2,1)S(1)}, u32[]{:S(2)}, u32[]{:S(2)}) collective-permute-start(bf16[128,512]{1,0:T(8,128)(2,1)S(1)} %fusion), channel_id=1, source_target_pairs={{0,2},{1,3},{2,4},{3,5},{4,6},{5,7},{6,8},{7,9},{8,10},{9,11},{10,... | collective-permute-start | bytes 393224 | tf_op jit(solution)/shard_map/ppermute | solution.py:18
  73.8 7.2 %collective-permute-start = (bf16[128,512]{1,0:T(8,128)(2,1)S(1)}, bf16[128,512]{1,0:T(8,128)(2,1)S(1)}, u32[]{:S(2)}, u32[]{:S(2)}) collective-permute-start(bf16[128,512]{1,0:T(8,128)(2,1)S(1)} %fusion), channel_id=1, source_target_pairs={{0,1},{1,2},{2,3},{3,4},{4,5},{5,6},{6,7},{7,8},{8,9},{9,10},{10,1... | collective-permute-start | bytes 393224 | tf_op jit(solution)/shard_map/ppermute | solution.py:18
  78.3 5.3 %copy-start.3 = (bf16[512,512]{1,0:T(8,128)(2,1)S(1)}, bf16[512,512]{1,0:T(8,128)(2,1)}, u32[]{:S(2)}) copy-start(bf16[512,512]{1,0:T(8,128)(2,1)} %param.15) | copy-start | bytes 1572868

commit v7 on v6

--- a/solution.py
+++ b/solution.py
@@ -96,6 +96,24 @@
     )(queries, keys, values)
 
 
+def _decode_kernel(z_ref, e1_ref, e2_ref, wt_ref, wd_ref, o_ref):
+    state = jnp.dot(z_ref[...], wt_ref[0], preferred_element_type=jnp.float32)
+    state = state + jnp.dot(e1_ref[...], wt_ref[1], preferred_element_type=jnp.float32)
+    state = state + jnp.dot(e2_ref[...], wt_ref[2], preferred_element_type=jnp.float32)
+    act = jax.nn.silu(state).astype(jnp.bfloat16)
+    o_ref[...] = jnp.dot(act, wd_ref[...], preferred_element_type=jnp.float32).astype(o_ref.dtype)
+
+
+def decode(latent, earlier_one, earlier_two, w_temporal, w_decode):
+    vmem = pl.BlockSpec(memory_space=pltpu.VMEM)
+    return pl.pallas_call(
+        _decode_kernel,
+        out_shape=jax.ShapeDtypeStruct((latent.shape[0], w_decode.shape[1]), jnp.bfloat16),
+        in_specs=[vmem] * 5,
+        out_specs=vmem,
+    )(latent, earlier_one, earlier_two, w_temporal, w_decode)
+
+
 def body(queries, keys, values, gain_q, gain_k, w_latent, w_temporal, w_decode):
     devices = lax.axis_size("seq")
     copies = devices // HEADS
@@ -121,12 +139,8 @@
     attention = jnp.transpose(back, (1, 0, 2)).reshape(rows, HEADS * HD)
     earlier_one = passed_along(latent, "seq", 1)
     earlier_two = passed_along(latent, "seq", 2)
-    state = jnp.dot(latent, w_temporal[0], preferred_element_type=jnp.float32)
-    state = state + jnp.dot(earlier_one, w_temporal[1], preferred_element_type=jnp.float32)
-    state = state + jnp.dot(earlier_two, w_temporal[2], preferred_element_type=jnp.float32)
-    act = lax.optimization_barrier(jax.nn.silu(state).astype(jnp.bfloat16))
-    decoded = jnp.dot(act, w_decode, preferred_element_type=jnp.float32)
-    return (attention, decoded.astype(jnp.bfloat16))
+    decoded = decode(latent, earlier_one, earlier_two, w_temporal, w_decode)
+    return (attention, decoded)
 
 
 def solution(mesh):

time: 85.2 us -> 84.9 us (level)
  matrix products: 5.18 us -> 0.44 us
  Pallas kernels: 8.56 us -> 11.4 us
  waiting for transfers between devices: 2.67 us -> 3.95 us
    dot_general x4 -> x0, matrix products: 4.75 us -> none  [the longest x1 1.32 us: body(): jnp.dot(earlier_two, w_temporal[2], preferred_element_type=jnp.float32)]
    pallas_call x0 -> x1, Pallas kernels: none -> 2.88 us  [decode(): pl.pallas_call(_decode_kernel, out_shape=jax.ShapeDtypeStruct((latent.sha...]
    ppermute x2, waiting for transfers between devices: 2.67 us -> 3.95 us  [passed_along(): return lax.ppermute(shard, axis, pairs)]
  transfers between devices with their start and end apart: 2 -> 2, of which waited for: 1 -> 2; matrix products, arithmetic and copies ran while one was open for 5% -> 2% of each run, Pallas kernels for 0% -> 0%
where the time goes in v7:
time: 84.9 us; the launch traced here: 84.6 us
  blocking collectives  61 us (72%)
  Pallas kernels  11.4 us (13%)
  starting transfers between devices  5.1 us (6%)
  waiting for transfers between devices  3.95 us (5%)
  local copies, waits for them, and re-layouts  1.98 us (2%)
    all_to_all x1, blocking collectives, body(): lax.all_to_all(stacked, 'seq', split_axis=0, concat_axis=0, tiled=True)  42.5 us
    all_to_all x1, blocking collectives, body(): back = lax.all_to_all(out, 'seq', split_axis=0, concat_axis=0, tiled=True)  18.4 us
    pallas_call x1, Pallas kernels, attend(): pl.pallas_call(_attn_kernel, out_shape=jax.ShapeDtypeStruct((span_blocks,...  6 us
    ppermute x2, starting transfers between devices, passed_along(): return lax.ppermute(shard, axis, pairs)  5.1 us
    ppermute x2, waiting for transfers between devices, passed_along(): return lax.ppermute(shard, axis, pairs)  3.95 us
    pallas_call x1, Pallas kernels, decode(): pl.pallas_call(_decode_kernel, out_shape=jax.ShapeDtypeStruct((latent.sha...  2.88 us
    pallas_call x1, Pallas kernels, pack(): pl.pallas_call(_pack_kernel, out_shape=jax.ShapeDtypeStruct((HEADS * copi...  2.56 us
  transfers between devices with their start and end apart: 2, of which 2 were waited for; matrix products, arithmetic and copies ran while one was open for 2% of the time, Pallas kernels for 0%

profile of v7, /device:TPU:8, one launch (start us, length us, event | category | flops | bytes accessed | tf_op | source)
XLA Modules:
  0.0 84.6 jit_solution(16006182675819882666)
XLA Ops:
  0.6 0.0 copy-start
  0.6 2.6 %shard_map.95 = bf16[16,3,128,128]{3,2,1,0:T(8,128)(2,1)} custom-call(bf16[128,2048]{1,0:T(8,128)(2,1)} %q_ref.1, bf16[128,2048]{1,0:T(8,128)(2,1)} %k_ref.1, bf16[128,2048]{1,0:T(8,128)(2,1)} %v_ref.1), custom_call_target="tpu_custom_call" | custom-call | tf_op jit(solution)/shard_map/pallas_call | solution.py:90
  3.2 0.0 copy-start.1
  3.2 0.0 copy-start.2
  3.2 42.5 %all_to_all.10.q_ref.k_ref.v_ref = bf16[16,3,128,128]{3,2,1,0:T(8,128)(2,1)S(1)} all-to-all(bf16[16,3,128,128]{3,2,1,0:T(8,128)(2,1)} %shard_map.95), channel_id=1, replica_groups=mesh['groups'=2,'seq'=16] {'seq'}, dimensions={0} | all-to-all | bytes 3145728 | tf_op jit(solution)/shard_map/all_to_all | solution.py:123
  45.7 0.0 copy-done.1
  45.8 0.0 copy-done.2
  45.8 6.0 %shard_map.96 = bf16[16,128,128]{2,1,0:T(8,128)(2,1)S(1)} custom-call(s32[1]{0:T(128)} %constant.15.clone.1.share_ref, bf16[16,3,128,128]{3,2,1,0:T(8,128)(2,1)S(1)} %all_to_all.10.q_ref.k_ref.v_ref, bf16[16,3,128,128]{3,2,1,0:T(8,128)(2,1)S(1)} %all_to_all.10.q_ref.k_ref.v_ref, bf16[16,3,128,128]{3,2,1,0:T(8,128)(2,1)S(1)} %all_to_all.10.q_ref.k_ref.v_ref, ...), custom_call_target="tpu_custom_call" | custom-call | tf_op jit(solution)/shard_map/pallas_call | solution.py:55
  51.8 18.4 %all_to_all.11 = bf16[16,128,128]{2,1,0:T(8,128)(2,1)S(1)} all-to-all(bf16[16,128,128]{2,1,0:T(8,128)(2,1)S(1)} %shard_map.96), channel_id=1, replica_groups=mesh['groups'=2,'seq'=16] {'seq'}, dimensions={0} | all-to-all | bytes 1048576 | tf_op jit(solution)/shard_map/all_to_all | solution.py:131
  70.2 0.0 copy-done
  70.2 0.4 fusion.z_ref
  70.6 0.0 copy-start.3
  70.6 3.2 %collective-permute-start.1 = (bf16[128,512]{1,0:T(8,128)(2,1)S(1)}, bf16[128,512]{1,0:T(8,128)(2,1)S(1)}, u32[]{:S(2)}, u32[]{:S(2)}) collective-permute-start(bf16[128,512]{1,0:T(8,128)(2,1)S(1)} %fusion.z_ref), channel_id=1, source_target_pairs={{0,2},{1,3},{2,4},{3,5},{4,6},{5,7},{6,8},{7,9},{8,10},{9,11},{10,... | collective-permute-start | bytes 393224 | tf_op jit(solution)/shard_map/ppermute | solution.py:18
  73.8 1.9 %collective-permute-start = (bf16[128,512]{1,0:T(8,128)(2,1)S(1)}, bf16[128,512]{1,0:T(8,128)(2,1)S(1)}, u32[]{:S(2)}, u32[]{:S(2)}) collective-permute-start(bf16[128,512]{1,0:T(8,128)(2,1)S(1)} %fusion.z_ref), channel_id=1, source_target_pairs={{0,1},{1,2},{2,3},{3,4},{4,5},{5,6},{6,7},{7,8},{8,9},{9,10},{10,1... | collective-permute-start | bytes 393224 | tf_op jit(solution)/shard_map/ppermute | solution.py:18
  75.8 0.3 copy.10
  76.0 1.0 %copy.11 = bf16[128,2048]{1,0:T(8,128)(2,1)} copy(bf16[128,2048]{0,1:T(8,128)(2,1)S(1)} %bitcast.15) | data formatting | bytes 1048576
  77.1 2.4 %collective-permute-done.1.e2_ref = bf16[128,512]{1,0:T(8,128)(2,1)S(1)} collective-permute-done((bf16[128,512]{1,0:T(8,128)(2,1)S(1)}, bf16[128,512]{1,0:T(8,128)(2,1)S(1)}, u32[]{:S(2)}, u32[]{:S(2)}) %collective-permute-start.1) | collective-permute-done | bytes 131104 | tf_op jit(solution)/shard_map/ppermute | solution.py:18
  79.5 0.0 copy-start.4
  79.5 1.5 %collective-permute-done.e1_ref = bf16[128,512]{1,0:T(8,128)(2,1)S(1)} collective-permute-done((bf16[128,512]{1,0:T(8,128)(2,1)S(1)}, bf16[128,512]{1,0:T(8,128)(2,1)S(1)}, u32[]{:S(2)}, u32[]{:S(2)}) %collective-permute-start) | collective-permute-done | bytes 131104 | tf_op jit(solution)/shard_map/ppermute | solution.py:18
  81.0 0.0 copy-done.3
  81.0 0.0 copy-done.4
  81.0 0.0 copy-start.5
  81.0 0.7 copy-done.5
  81.7 2.9 %shard_map.97 = bf16[128,512]{1,0:T(8,128)(2,1)} custom-call(bf16[128,512]{1,0:T(8,128)(2,1)} %copy-done.3, bf16[128,512]{1,0:T(8,128)(2,1)} %copy-done.5, bf16[128,512]{1,0:T(8,128)(2,1)} %copy-done.4, bf16[3,512,512]{2,1,0:T(8,128)(2,1)} %wt_ref.1, bf16[512,512]{1,0:T(8,128)(2,1)} %wd_ref.1), custom_call_target="tpu_custom_call" | custom-call | tf_op jit(solution)/shard_map/pallas_call | solution.py:109
Async XLA Ops:
  0.6 69.6 %copy-start = (bf16[2048,512]{1,0:T(8,128)(2,1)S(1)}, bf16[2048,512]{1,0:T(8,128)(2,1)}, u32[]{:S(2)}) copy-start(bf16[2048,512]{1,0:T(8,128)(2,1)} %param.13) | copy-start | bytes 6291460
  3.2 42.5 %copy-start.1 = (f32[128]{0:T(128)S(1)}, f32[128]{0:T(128)}, u32[]{:S(2)}) copy-start(f32[128]{0:T(128)} %param.11) | copy-start | bytes 1540
  3.2 42.5 %copy-start.2 = (f32[128]{0:T(128)S(1)}, f32[128]{0:T(128)}, u32[]{:S(2)}) copy-start(f32[128]{0:T(128)} %param.12) | copy-start | bytes 1540
  70.6 10.4 %copy-start.3 = (bf16[128,512]{1,0:T(8,128)(2,1)}, bf16[128,512]{1,0:T(8,128)(2,1)S(1)}, u32[]{:S(2)}) copy-start(bf16[128,512]{1,0:T(8,128)(2,1)S(1)} %fusion.z_ref) | copy-start | bytes 393220
  70.6 8.9 %collective-permute-start.1 = (bf16[128,512]{1,0:T(8,128)(2,1)S(1)}, bf16[128,512]{1,0:T(8,128)(2,1)S(1)}, u32[]{:S(2)}, u32[]{:S(2)}) collective-permute-start(bf16[128,512]{1,0:T(8,128)(2,1)S(1)} %fusion.z_ref), channel_id=1, source_target_pairs={{0,2},{1,3},{2,4},{3,5},{4,6},{5,7},{6,8},{7,9},{8,10},{9,11},{10,... | collective-permute-start | bytes 393224 | tf_op jit(solution)/shard_map/ppermute | solution.py:18
  73.8 7.2 %collective-permute-start = (bf16[128,512]{1,0:T(8,128)(2,1)S(1)}, bf16[128,512]{1,0:T(8,128)(2,1)S(1)}, u32[]{:S(2)}, u32[]{:S(2)}) collective-permute-start(bf16[128,512]{1,0:T(8,128)(2,1)S(1)} %fusion.z_ref), channel_id=1, source_target_pairs={{0,1},{1,2},{2,3},{3,4},{4,5},{5,6},{6,7},{7,8},{8,9},{9,10},{10,1... | collective-permute-start | bytes 393224 | tf_op jit(solution)/shard_map/ppermute | solution.py:18
  79.5 1.5 %copy-start.4 = (bf16[128,512]{1,0:T(8,128)(2,1)}, bf16[128,512]{1,0:T(8,128)(2,1)S(1)}, u32[]{:S(2)}) copy-start(bf16[128,512]{1,0:T(8,128)(2,1)S(1)} %collective-permute-done.1.e2_ref) | copy-start | bytes 393220
  81.0 0.7 copy-start.5

commit v8 on v6

--- a/solution.py
+++ b/solution.py
@@ -121,12 +121,11 @@
     attention = jnp.transpose(back, (1, 0, 2)).reshape(rows, HEADS * HD)
     earlier_one = passed_along(latent, "seq", 1)
     earlier_two = passed_along(latent, "seq", 2)
-    state = jnp.dot(latent, w_temporal[0], preferred_element_type=jnp.float32)
-    state = state + jnp.dot(earlier_one, w_temporal[1], preferred_element_type=jnp.float32)
-    state = state + jnp.dot(earlier_two, w_temporal[2], preferred_element_type=jnp.float32)
+    taps = jnp.concatenate([latent, earlier_one, earlier_two], axis=1)
+    state = jnp.dot(taps, w_temporal.reshape(-1, w_temporal.shape[2]), preferred_element_type=jnp.float32)
     act = lax.optimization_barrier(jax.nn.silu(state).astype(jnp.bfloat16))
-    decoded = jnp.dot(act, w_decode, preferred_element_type=jnp.float32)
-    return (attention, decoded.astype(jnp.bfloat16))
+    decoded = jnp.dot(act, w_decode, preferred_element_type=jnp.float32).astype(jnp.bfloat16)
+    return (attention, decoded)
 
 
 def solution(mesh):

time: 85.2 us -> 84.1 us (0.987)
  matrix products: 5.18 us -> 3.21 us
  waiting for transfers between devices: 2.67 us -> 3.95 us
    dot_general x4 -> x2, matrix products: 4.75 us -> 2.77 us  [the longest x1 1.88 us: body(): jnp.dot(taps, w_temporal.reshape(-1, w_temporal.shape[2]), preferred_elem...]
    ppermute x2, waiting for transfers between devices: 2.67 us -> 3.95 us  [passed_along(): return lax.ppermute(shard, axis, pairs)]
  transfers between devices with their start and end apart: 2 -> 2, of which waited for: 1 -> 2; matrix products, arithmetic and copies ran while one was open for 5% -> 2% of each run, Pallas kernels for 0% -> 0%
where the time goes in v8:
time: 84.1 us; the launch traced here: 83.8 us
  blocking collectives  61 us (73%)
  Pallas kernels  8.56 us (10%)
  starting transfers between devices  5.1 us (6%)
  waiting for transfers between devices  3.95 us (5%)
  matrix products  3.21 us (4%)
  local copies, waits for them, and re-layouts  1.31 us (2%)
    all_to_all x1, blocking collectives, body(): lax.all_to_all(stacked, 'seq', split_axis=0, concat_axis=0, tiled=True)  42.5 us
    all_to_all x1, blocking collectives, body(): back = lax.all_to_all(out, 'seq', split_axis=0, concat_axis=0, tiled=True)  18.4 us
    pallas_call x1, Pallas kernels, attend(): pl.pallas_call(_attn_kernel, out_shape=jax.ShapeDtypeStruct((span_blocks,...  5.99 us
    ppermute x2, starting transfers between devices, passed_along(): return lax.ppermute(shard, axis, pairs)  5.1 us
    ppermute x2, waiting for transfers between devices, passed_along(): return lax.ppermute(shard, axis, pairs)  3.95 us
    pallas_call x1, Pallas kernels, pack(): pl.pallas_call(_pack_kernel, out_shape=jax.ShapeDtypeStruct((HEADS * copi...  2.57 us
    dot_general x1, matrix products, body(): jnp.dot(taps, w_temporal.reshape(-1, w_temporal.shape[2]), preferred_elem...  1.88 us
  transfers between devices with their start and end apart: 2, of which 2 were waited for; matrix products, arithmetic and copies ran while one was open for 2% of the time, Pallas kernels for 0%

profile of v8, /device:TPU:8, one launch (start us, length us, event | category | flops | bytes accessed | tf_op | source)
XLA Modules:
  0.0 83.8 jit_solution(5654426003909956778)
XLA Ops:
  0.6 0.0 copy-start
  0.6 2.6 %shard_map.95 = bf16[16,3,128,128]{3,2,1,0:T(8,128)(2,1)} custom-call(bf16[128,2048]{1,0:T(8,128)(2,1)} %q_ref.1, bf16[128,2048]{1,0:T(8,128)(2,1)} %k_ref.1, bf16[128,2048]{1,0:T(8,128)(2,1)} %v_ref.1), custom_call_target="tpu_custom_call" | custom-call | tf_op jit(solution)/shard_map/pallas_call | solution.py:90
  3.2 0.0 copy-start.1
  3.2 0.0 copy-start.2
  3.2 42.5 %all_to_all.10.q_ref.k_ref.v_ref = bf16[16,3,128,128]{3,2,1,0:T(8,128)(2,1)S(1)} all-to-all(bf16[16,3,128,128]{3,2,1,0:T(8,128)(2,1)} %shard_map.95), channel_id=1, replica_groups=mesh['groups'=2,'seq'=16] {'seq'}, dimensions={0} | all-to-all | bytes 3145728 | tf_op jit(solution)/shard_map/all_to_all | solution.py:105
  45.8 0.0 copy-done.1
  45.8 0.0 copy-done.2
  45.8 6.0 %shard_map.96 = bf16[16,128,128]{2,1,0:T(8,128)(2,1)S(1)} custom-call(s32[1]{0:T(128)} %constant.17.clone.1.share_ref, bf16[16,3,128,128]{3,2,1,0:T(8,128)(2,1)S(1)} %all_to_all.10.q_ref.k_ref.v_ref, bf16[16,3,128,128]{3,2,1,0:T(8,128)(2,1)S(1)} %all_to_all.10.q_ref.k_ref.v_ref, bf16[16,3,128,128]{3,2,1,0:T(8,128)(2,1)S(1)} %all_to_all.10.q_ref.k_ref.v_ref, ...), custom_call_target="tpu_custom_call" | custom-call | tf_op jit(solution)/shard_map/pallas_call | solution.py:55
  51.8 18.4 %all_to_all.11 = bf16[16,128,128]{2,1,0:T(8,128)(2,1)S(1)} all-to-all(bf16[16,128,128]{2,1,0:T(8,128)(2,1)S(1)} %shard_map.96), channel_id=1, replica_groups=mesh['groups'=2,'seq'=16] {'seq'}, dimensions={0} | all-to-all | bytes 1048576 | tf_op jit(solution)/shard_map/all_to_all | solution.py:113
  70.2 0.0 copy-done
  70.2 0.4 fusion
  70.6 3.2 %collective-permute-start.1 = (bf16[128,512]{1,0:T(8,128)(2,1)S(1)}, bf16[128,512]{1,0:T(8,128)(2,1)S(1)}, u32[]{:S(2)}, u32[]{:S(2)}) collective-permute-start(bf16[128,512]{1,0:T(8,128)(2,1)S(1)} %fusion), channel_id=1, source_target_pairs={{0,2},{1,3},{2,4},{3,5},{4,6},{5,7},{6,8},{7,9},{8,10},{9,11},{10,... | collective-permute-start | bytes 393224 | tf_op jit(solution)/shard_map/ppermute | solution.py:18
  73.8 1.9 %collective-permute-start = (bf16[128,512]{1,0:T(8,128)(2,1)S(1)}, bf16[128,512]{1,0:T(8,128)(2,1)S(1)}, u32[]{:S(2)}, u32[]{:S(2)}) collective-permute-start(bf16[128,512]{1,0:T(8,128)(2,1)S(1)} %fusion), channel_id=1, source_target_pairs={{0,1},{1,2},{2,3},{3,4},{4,5},{5,6},{6,7},{7,8},{8,9},{9,10},{10,1... | collective-permute-start | bytes 393224 | tf_op jit(solution)/shard_map/ppermute | solution.py:18
  75.8 0.3 copy.10
  76.1 1.0 %copy.11 = bf16[128,2048]{1,0:T(8,128)(2,1)} copy(bf16[128,2048]{0,1:T(8,128)(2,1)S(1)} %bitcast.19) | data formatting | bytes 1048576
  77.1 2.4 %collective-permute-done.1 = bf16[128,512]{1,0:T(8,128)(2,1)S(1)} collective-permute-done((bf16[128,512]{1,0:T(8,128)(2,1)S(1)}, bf16[128,512]{1,0:T(8,128)(2,1)S(1)}, u32[]{:S(2)}, u32[]{:S(2)}) %collective-permute-start.1) | collective-permute-done | bytes 131104 | tf_op jit(solution)/shard_map/ppermute | solution.py:18
  79.5 1.5 %collective-permute-done = bf16[128,512]{1,0:T(8,128)(2,1)S(1)} collective-permute-done((bf16[128,512]{1,0:T(8,128)(2,1)S(1)}, bf16[128,512]{1,0:T(8,128)(2,1)S(1)}, u32[]{:S(2)}, u32[]{:S(2)}) %collective-permute-start) | collective-permute-done | bytes 131104 | tf_op jit(solution)/shard_map/ppermute | solution.py:18
  81.0 0.0 copy-start.3
  81.0 1.9 %multiply_convert_fusion = bf16[128,512]{1,0:T(8,128)(2,1)S(1)} fusion(bf16[1536,512]{1,0:T(8,128)(2,1)} %bitcast.20, bf16[128,512]{1,0:T(8,128)(2,1)S(1)} %collective-permute-done.1, bf16[128,512]{1,0:T(8,128)(2,1)S(1)} %collective-permute-done, bf16[128,512]{1,0:T(8,128)(2,1)S(1)} %fusion), kind=kOutput, calls=%fused_computation.9 | convolution fusion | flops 202833920 | bytes 2097152 | tf_op jit(solution)/shard_map/dot_general | solution.py:125
  82.9 0.0 copy-done.3
  82.9 0.9 %convolution_convert_fusion = bf16[128,512]{1,0:T(8,128)(2,1)} fusion(bf16[128,512]{1,0:T(8,128)(2,1)S(1)} %multiply_convert_fusion, bf16[512,512]{1,0:T(8,128)(2,1)S(1)} %copy-done.3), kind=kOutput, calls=%fused_computation.1 | convolution fusion | flops 67174400 | bytes 786432 | tf_op jit(solution)/shard_map/dot_general | solution.py:127
Async XLA Ops:
  0.6 69.6 %copy-start = (bf16[2048,512]{1,0:T(8,128)(2,1)S(1)}, bf16[2048,512]{1,0:T(8,128)(2,1)}, u32[]{:S(2)}) copy-start(bf16[2048,512]{1,0:T(8,128)(2,1)} %param.13) | copy-start | bytes 6291460
  3.2 42.5 %copy-start.1 = (f32[128]{0:T(128)S(1)}, f32[128]{0:T(128)}, u32[]{:S(2)}) copy-start(f32[128]{0:T(128)} %param.11) | copy-start | bytes 1540
  3.2 42.5 %copy-start.2 = (f32[128]{0:T(128)S(1)}, f32[128]{0:T(128)}, u32[]{:S(2)}) copy-start(f32[128]{0:T(128)} %param.12) | copy-start | bytes 1540
  70.6 8.8 %collective-permute-start.1 = (bf16[128,512]{1,0:T(8,128)(2,1)S(1)}, bf16[128,512]{1,0:T(8,128)(2,1)S(1)}, u32[]{:S(2)}, u32[]{:S(2)}) collective-permute-start(bf16[128,512]{1,0:T(8,128)(2,1)S(1)} %fusion), channel_id=1, source_target_pairs={{0,2},{1,3},{2,4},{3,5},{4,6},{5,7},{6,8},{7,9},{8,10},{9,11},{10,... | collective-permute-start | bytes 393224 | tf_op jit(solution)/shard_map/ppermute | solution.py:18
  73.8 7.2 %collective-permute-start = (bf16[128,512]{1,0:T(8,128)(2,1)S(1)}, bf16[128,512]{1,0:T(8,128)(2,1)S(1)}, u32[]{:S(2)}, u32[]{:S(2)}) collective-permute-start(bf16[128,512]{1,0:T(8,128)(2,1)S(1)} %fusion), channel_id=1, source_target_pairs={{0,1},{1,2},{2,3},{3,4},{4,5},{5,6},{6,7},{7,8},{8,9},{9,10},{10,1... | collective-permute-start | bytes 393224 | tf_op jit(solution)/shard_map/ppermute | solution.py:18
  81.0 1.9 %copy-start.3 = (bf16[512,512]{1,0:T(8,128)(2,1)S(1)}, bf16[512,512]{1,0:T(8,128)(2,1)}, u32[]{:S(2)}) copy-start(bf16[512,512]{1,0:T(8,128)(2,1)} %param.15) | copy-start | bytes 1572868

commit v9 on v8

--- a/solution.py
+++ b/solution.py
@@ -121,8 +121,10 @@
     attention = jnp.transpose(back, (1, 0, 2)).reshape(rows, HEADS * HD)
     earlier_one = passed_along(latent, "seq", 1)
     earlier_two = passed_along(latent, "seq", 2)
-    taps = jnp.concatenate([latent, earlier_one, earlier_two], axis=1)
-    state = jnp.dot(taps, w_temporal.reshape(-1, w_temporal.shape[2]), preferred_element_type=jnp.float32)
+    own = jnp.dot(latent, w_temporal[0], preferred_element_type=jnp.float32)
+    own = lax.optimization_barrier(own)
+    taps = jnp.concatenate([earlier_one, earlier_two], axis=1)
+    state = own + jnp.dot(taps, w_temporal[1:].reshape(-1, w_temporal.shape[2]), preferred_element_type=jnp.float32)
     act = lax.optimization_barrier(jax.nn.silu(state).astype(jnp.bfloat16))
     decoded = jnp.dot(act, w_decode, preferred_element_type=jnp.float32).astype(jnp.bfloat16)
     return (attention, decoded)

time: 84.1 us -> 86.4 us (1.027)
  blocking collectives: 61 us -> 42.5 us
  waiting for transfers between devices: 3.95 us -> 15 us
  starting transfers between devices: 5.1 us -> 10.4 us
  local copies, waits for them, and re-layouts: 1.31 us -> 3.57 us
  matrix products: 3.21 us -> 4.33 us
    all_to_all x1 -> x0, blocking collectives: 18.4 us -> none  [body(): back = lax.all_to_all(out, 'seq', split_axis=0, concat_axis=0, tiled=True)]
    all_to_all x0 -> x1, waiting for transfers between devices: none -> 11.4 us  [body(): back = lax.all_to_all(out, 'seq', split_axis=0, concat_axis=0, tiled=True)]
    all_to_all x0 -> x1, starting transfers between devices: none -> 4.99 us  [body(): back = lax.all_to_all(out, 'seq', split_axis=0, concat_axis=0, tiled=True)]
    slice x0 -> x1, local copies, waits for them, and re-layouts: none -> 2.26 us  [body(): w_temporal[1:].reshape(-1, w_temporal.shape[2])]
    dot_general x1 -> x2, matrix products: 1.88 us -> 2.99 us  [the longest x1 1.72 us: body(): jnp.dot(taps, w_temporal[1:].reshape(-1, w_temporal.shape[2]), preferred_...]
  transfers between devices with their start and end apart: 2 -> 3, of which waited for: 2 -> 2; matrix products, arithmetic and copies ran while one was open for 2% -> 6% of each run, Pallas kernels for 0% -> 0%
where the time goes in v9:
time: 86.4 us; the launch traced here: 85.9 us
  blocking collectives  42.5 us (49%)
  waiting for transfers between devices  15 us (17%)
  starting transfers between devices  10.4 us (12%)
  Pallas kernels  9.35 us (11%)
  matrix products  4.33 us (5%)
  local copies, waits for them, and re-layouts  3.57 us (4%)
    all_to_all x1, blocking collectives, body(): lax.all_to_all(stacked, 'seq', split_axis=0, concat_axis=0, tiled=True)  42.5 us
    all_to_all x1, waiting for transfers between devices, body(): back = lax.all_to_all(out, 'seq', split_axis=0, concat_axis=0, tiled=True)  11.4 us
    pallas_call x1, Pallas kernels, attend(): pl.pallas_call(_attn_kernel, out_shape=jax.ShapeDtypeStruct((span_blocks,...  6.79 us
    ppermute x2, starting transfers between devices, passed_along(): return lax.ppermute(shard, axis, pairs)  5.38 us
    all_to_all x1, starting transfers between devices, body(): back = lax.all_to_all(out, 'seq', split_axis=0, concat_axis=0, tiled=True)  4.99 us
    ppermute x2, waiting for transfers between devices, passed_along(): return lax.ppermute(shard, axis, pairs)  3.63 us
    pallas_call x1, Pallas kernels, pack(): pl.pallas_call(_pack_kernel, out_shape=jax.ShapeDtypeStruct((HEADS * copi...  2.56 us
    slice x1, local copies, waits for them, and re-layouts, body(): w_temporal[1:].reshape(-1, w_temporal.shape[2])  2.26 us
  transfers between devices with their start and end apart: 3, of which 2 were waited for; matrix products, arithmetic and copies ran while one was open for 6% of the time, Pallas kernels for 0%

profile of v9, /device:TPU:8, one launch (start us, length us, event | category | flops | bytes accessed | tf_op | source)
XLA Modules:
  0.0 85.9 jit_solution(13985588608549900456)
XLA Ops:
  0.6 0.0 copy-start
  0.6 2.6 %shard_map.95 = bf16[16,3,128,128]{3,2,1,0:T(8,128)(2,1)} custom-call(bf16[128,2048]{1,0:T(8,128)(2,1)} %q_ref.1, bf16[128,2048]{1,0:T(8,128)(2,1)} %k_ref.1, bf16[128,2048]{1,0:T(8,128)(2,1)} %v_ref.1), custom_call_target="tpu_custom_call" | custom-call | tf_op jit(solution)/shard_map/pallas_call | solution.py:90
  3.2 0.0 copy-start.1
  3.2 0.0 copy-start.2
  3.2 42.5 %all_to_all.10.q_ref.k_ref.v_ref = bf16[16,3,128,128]{3,2,1,0:T(8,128)(2,1)S(1)} all-to-all(bf16[16,3,128,128]{3,2,1,0:T(8,128)(2,1)} %shard_map.95), channel_id=1, replica_groups=mesh['groups'=2,'seq'=16] {'seq'}, dimensions={0} | all-to-all | bytes 3145728 | tf_op jit(solution)/shard_map/all_to_all | solution.py:105
  45.7 0.0 copy-done.1
  45.8 0.0 copy-done.2
  45.8 6.8 %shard_map.96 = bf16[16,128,128]{2,1,0:T(8,128)(2,1)} custom-call(s32[1]{0:T(128)} %constant.17.clone.1.share_ref, bf16[16,3,128,128]{3,2,1,0:T(8,128)(2,1)S(1)} %all_to_all.10.q_ref.k_ref.v_ref, bf16[16,3,128,128]{3,2,1,0:T(8,128)(2,1)S(1)} %all_to_all.10.q_ref.k_ref.v_ref, bf16[16,3,128,128]{3,2,1,0:T(8,128)(2,1)S(1)} %all_to_all.10.q_ref.k_ref.v_ref, ...), custom_call_target="tpu_custom_call" | custom-call | tf_op jit(solution)/shard_map/pallas_call | solution.py:55
  52.5 5.0 %all-to-all-start.1 = ((bf16[16,128,128]{2,1,0:T(8,128)(2,1)}), bf16[16,128,128]{2,1,0:T(8,128)(2,1)S(1)}, u32[]{:S(2)}, u32[]{:S(2)}) async-start(bf16[16,128,128]{2,1,0:T(8,128)(2,1)} %shard_map.96), calls=%async_computation.1 | async-start | bytes 1048576 | tf_op jit(solution)/shard_map/all_to_all | solution.py:113
  57.5 2.3 %slice.7 = bf16[2,512,512]{2,1,0:T(8,128)(2,1)} slice(bf16[3,512,512]{2,1,0:T(8,128)(2,1)} %param.14), slice={[1:3], [0:512], [0:512]} | slice | bytes 2097152 | tf_op jit(solution)/shard_map/slice | solution.py:127
  59.8 11.4 %all-to-all-done.1 = bf16[16,128,128]{2,1,0:T(8,128)(2,1)S(1)} async-done(((bf16[16,128,128]{2,1,0:T(8,128)(2,1)}), bf16[16,128,128]{2,1,0:T(8,128)(2,1)S(1)}, u32[]{:S(2)}, u32[]{:S(2)}) %all-to-all-start.1) | async-done | bytes 524320 | tf_op jit(solution)/shard_map/all_to_all | solution.py:113
  71.2 0.0 copy-done
  71.2 0.4 fusion
  71.6 2.5 %collective-permute-start = (bf16[128,512]{1,0:T(8,128)(2,1)S(1)}, bf16[128,512]{1,0:T(8,128)(2,1)}, u32[]{:S(2)}, u32[]{:S(2)}) collective-permute-start(bf16[128,512]{1,0:T(8,128)(2,1)S(1)} %fusion), channel_id=1, source_target_pairs={{0,1},{1,2},{2,3},{3,4},{4,5},{5,6},{6,7},{7,8},{8,9},{9,10},{10,1... | collective-permute-start | bytes 393224 | tf_op jit(solution)/shard_map/ppermute | solution.py:18
  74.2 2.8 %collective-permute-start.1 = (bf16[128,512]{1,0:T(8,128)(2,1)S(1)}, bf16[128,512]{1,0:T(8,128)(2,1)}, u32[]{:S(2)}, u32[]{:S(2)}) collective-permute-start(bf16[128,512]{1,0:T(8,128)(2,1)S(1)} %fusion), channel_id=1, source_target_pairs={{0,2},{1,3},{2,4},{3,5},{4,6},{5,7},{6,8},{7,9},{8,10},{9,11},{10,... | collective-permute-start | bytes 393224 | tf_op jit(solution)/shard_map/ppermute | solution.py:18
  77.0 1.3 %fusion.1 = f32[128,512]{1,0:T(8,128)S(1)} fusion(bf16[128,512]{1,0:T(8,128)(2,1)S(1)} %fusion, bf16[3,512,512]{2,1,0:T(8,128)(2,1)} %param.14), kind=kOutput, calls=%fused_computation.4 | convolution fusion | flops 67108864 | bytes 917504 | tf_op jit(solution)/shard_map/dot_general | solution.py:124
  78.3 0.3 copy.10
  78.6 0.0 copy-start.3
  78.6 1.0 %copy.11 = bf16[128,2048]{1,0:T(8,128)(2,1)} copy(bf16[128,2048]{0,1:T(8,128)(2,1)S(1)} %bitcast.23) | data formatting | bytes 1048576
  79.6 0.0 collective-permute-done
  79.6 3.6 %collective-permute-done.1 = bf16[128,512]{1,0:T(8,128)(2,1)} collective-permute-done((bf16[128,512]{1,0:T(8,128)(2,1)S(1)}, bf16[128,512]{1,0:T(8,128)(2,1)}, u32[]{:S(2)}, u32[]{:S(2)}) %collective-permute-start.1) | collective-permute-done | bytes 131104 | tf_op jit(solution)/shard_map/ppermute | solution.py:18
  83.2 1.7 %multiply_convert_fusion = bf16[128,512]{1,0:T(8,128)(2,1)S(1)} fusion(f32[128,512]{1,0:T(8,128)S(1)} %fusion.1, bf16[1024,512]{1,0:T(8,128)(2,1)} %bitcast.24, bf16[128,512]{1,0:T(8,128)(2,1)} %collective-permute-done.1, bf16[128,512]{1,0:T(8,128)(2,1)} %collective-permute-done), kind=kOutput, calls=%fused_computation.10 | convolution fusion | flops 135135232 | bytes 1703936 | tf_op jit(solution)/shard_map/dot_general | solution.py:127
  85.0 0.0 copy-done.3
  85.0 0.9 %convolution_convert_fusion = bf16[128,512]{1,0:T(8,128)(2,1)} fusion(bf16[128,512]{1,0:T(8,128)(2,1)S(1)} %multiply_convert_fusion, bf16[512,512]{1,0:T(8,128)(2,1)S(1)} %copy-done.3), kind=kOutput, calls=%fused_computation.2 | convolution fusion | flops 67174400 | bytes 786432 | tf_op jit(solution)/shard_map/dot_general | solution.py:129
Async XLA Ops:
  0.6 70.6 %copy-start = (bf16[2048,512]{1,0:T(8,128)(2,1)S(1)}, bf16[2048,512]{1,0:T(8,128)(2,1)}, u32[]{:S(2)}) copy-start(bf16[2048,512]{1,0:T(8,128)(2,1)} %param.13) | copy-start | bytes 6291460
  3.2 42.5 %copy-start.1 = (f32[128]{0:T(128)S(1)}, f32[128]{0:T(128)}, u32[]{:S(2)}) copy-start(f32[128]{0:T(128)} %param.11) | copy-start | bytes 1540
  3.2 42.5 %copy-start.2 = (f32[128]{0:T(128)S(1)}, f32[128]{0:T(128)}, u32[]{:S(2)}) copy-start(f32[128]{0:T(128)} %param.12) | copy-start | bytes 1540
  52.5 18.6 %all-to-all-start.1 = ((bf16[16,128,128]{2,1,0:T(8,128)(2,1)}), bf16[16,128,128]{2,1,0:T(8,128)(2,1)S(1)}, u32[]{:S(2)}, u32[]{:S(2)}) async-start(bf16[16,128,128]{2,1,0:T(8,128)(2,1)} %shard_map.96), calls=%async_computation.1 | async-start | bytes 1048576 | tf_op jit(solution)/shard_map/all_to_all | solution.py:113
  71.6 8.0 %collective-permute-start = (bf16[128,512]{1,0:T(8,128)(2,1)S(1)}, bf16[128,512]{1,0:T(8,128)(2,1)}, u32[]{:S(2)}, u32[]{:S(2)}) collective-permute-start(bf16[128,512]{1,0:T(8,128)(2,1)S(1)} %fusion), channel_id=1, source_target_pairs={{0,1},{1,2},{2,3},{3,4},{4,5},{5,6},{6,7},{7,8},{8,9},{9,10},{10,1... | collective-permute-start | bytes 393224 | tf_op jit(solution)/shard_map/ppermute | solution.py:18
  74.2 9.0 %collective-permute-start.1 = (bf16[128,512]{1,0:T(8,128)(2,1)S(1)}, bf16[128,512]{1,0:T(8,128)(2,1)}, u32[]{:S(2)}, u32[]{:S(2)}) collective-permute-start(bf16[128,512]{1,0:T(8,128)(2,1)S(1)} %fusion), channel_id=1, source_target_pairs={{0,2},{1,3},{2,4},{3,5},{4,6},{5,7},{6,8},{7,9},{8,10},{9,11},{10,... | collective-permute-start | bytes 393224 | tf_op jit(solution)/shard_map/ppermute | solution.py:18
  78.6 6.4 %copy-start.3 = (bf16[512,512]{1,0:T(8,128)(2,1)S(1)}, bf16[512,512]{1,0:T(8,128)(2,1)}, u32[]{:S(2)}) copy-start(bf16[512,512]{1,0:T(8,128)(2,1)} %param.15) | copy-start | bytes 1572868

commit v10 on v8

--- a/solution.py
+++ b/solution.py
@@ -96,6 +96,23 @@
     )(queries, keys, values)
 
 
+def _unpack_kernel(b_ref, o_ref):
+    for h in range(b_ref.shape[0]):
+        o_ref[:, h * HD:(h + 1) * HD] = b_ref[h]
+
+
+def unpack(back):
+    heads, rows, _ = back.shape
+    group = 8
+    return pl.pallas_call(
+        _unpack_kernel,
+        out_shape=jax.ShapeDtypeStruct((rows, heads * HD), back.dtype),
+        grid=(heads // group,),
+        in_specs=[pl.BlockSpec((group, rows, HD), lambda g: (g, 0, 0))],
+        out_specs=pl.BlockSpec((rows, group * HD), lambda g: (0, g)),
+    )(back)
+
+
 def body(queries, keys, values, gain_q, gain_k, w_latent, w_temporal, w_decode):
     devices = lax.axis_size("seq")
     copies = devices // HEADS
@@ -118,7 +135,7 @@
     latent = jnp.einsum(
         "hrd,hdc->rc", back, w_latent.reshape(HEADS, HD, -1), preferred_element_type=jnp.float32
     ).astype(jnp.bfloat16)
-    attention = jnp.transpose(back, (1, 0, 2)).reshape(rows, HEADS * HD)
+    attention = unpack(back)
     earlier_one = passed_along(latent, "seq", 1)
     earlier_two = passed_along(latent, "seq", 2)
     taps = jnp.concatenate([latent, earlier_one, earlier_two], axis=1)

time: 84.1 us -> 84.1 us (level)
  Pallas kernels: 8.56 us -> 10.4 us
  local copies, waits for them, and re-layouts: 1.31 us -> 0.02 us
    pallas_call x0 -> x1, Pallas kernels: none -> 1.82 us  [unpack(): pl.pallas_call(_unpack_kernel, out_shape=jax.ShapeDtypeStruct((rows, head...]
    unnamed x9 -> x10, local copies, waits for them, and re-layouts: 1.03 us -> 0.02 us
  transfers between devices with their start and end apart: 2 -> 2, of which waited for: 2 -> 2; matrix products, arithmetic and copies ran while one was open for 2% -> 0% of each run, Pallas kernels for 0% -> 2%
where the time goes in v10:
time: 84.1 us; the launch traced here: 83.8 us
  blocking collectives  61 us (73%)
  Pallas kernels  10.4 us (12%)
  starting transfers between devices  5.1 us (6%)
  waiting for transfers between devices  3.43 us (4%)
  matrix products  3.21 us (4%)
    all_to_all x1, blocking collectives, body(): lax.all_to_all(stacked, 'seq', split_axis=0, concat_axis=0, tiled=True)  42.5 us
    all_to_all x1, blocking collectives, body(): back = lax.all_to_all(out, 'seq', split_axis=0, concat_axis=0, tiled=True)  18.4 us
    pallas_call x1, Pallas kernels, attend(): pl.pallas_call(_attn_kernel, out_shape=jax.ShapeDtypeStruct((span_blocks,...  6 us
    ppermute x2, starting transfers between devices, passed_along(): return lax.ppermute(shard, axis, pairs)  5.1 us
    ppermute x2, waiting for transfers between devices, passed_along(): return lax.ppermute(shard, axis, pairs)  3.43 us
    pallas_call x1, Pallas kernels, pack(): pl.pallas_call(_pack_kernel, out_shape=jax.ShapeDtypeStruct((HEADS * copi...  2.56 us
    dot_general x1, matrix products, body(): jnp.dot(taps, w_temporal.reshape(-1, w_temporal.shape[2]), preferred_elem...  1.88 us
    pallas_call x1, Pallas kernels, unpack(): pl.pallas_call(_unpack_kernel, out_shape=jax.ShapeDtypeStruct((rows, head...  1.82 us
  transfers between devices with their start and end apart: 2, of which 2 were waited for; matrix products, arithmetic and copies ran while one was open for 0% of the time, Pallas kernels for 2%

profile of v10, /device:TPU:8, one launch (start us, length us, event | category | flops | bytes accessed | tf_op | source)
XLA Modules:
  0.0 83.8 jit_solution(2657334456329539706)
XLA Ops:
  0.6 0.0 copy-start
  0.6 2.6 %shard_map.95 = bf16[16,3,128,128]{3,2,1,0:T(8,128)(2,1)} custom-call(bf16[128,2048]{1,0:T(8,128)(2,1)} %q_ref.1, bf16[128,2048]{1,0:T(8,128)(2,1)} %k_ref.1, bf16[128,2048]{1,0:T(8,128)(2,1)} %v_ref.1), custom_call_target="tpu_custom_call" | custom-call | tf_op jit(solution)/shard_map/pallas_call | solution.py:90
  3.2 0.0 copy-start.1
  3.2 0.0 copy-start.2
  3.2 42.5 %all_to_all.10.q_ref.k_ref.v_ref = bf16[16,3,128,128]{3,2,1,0:T(8,128)(2,1)S(1)} all-to-all(bf16[16,3,128,128]{3,2,1,0:T(8,128)(2,1)} %shard_map.95), channel_id=1, replica_groups=mesh['groups'=2,'seq'=16] {'seq'}, dimensions={0} | all-to-all | bytes 3145728 | tf_op jit(solution)/shard_map/all_to_all | solution.py:122
  45.8 0.0 copy-done.1
  45.8 0.0 copy-done.2
  45.8 6.0 %shard_map.96 = bf16[16,128,128]{2,1,0:T(8,128)(2,1)S(1)} custom-call(s32[1]{0:T(128)} %constant.17.clone.1.share_ref, bf16[16,3,128,128]{3,2,1,0:T(8,128)(2,1)S(1)} %all_to_all.10.q_ref.k_ref.v_ref, bf16[16,3,128,128]{3,2,1,0:T(8,128)(2,1)S(1)} %all_to_all.10.q_ref.k_ref.v_ref, bf16[16,3,128,128]{3,2,1,0:T(8,128)(2,1)S(1)} %all_to_all.10.q_ref.k_ref.v_ref, ...), custom_call_target="tpu_custom_call" | custom-call | tf_op jit(solution)/shard_map/pallas_call | solution.py:55
  51.8 18.4 %all_to_all.11.b_ref = bf16[16,128,128]{2,1,0:T(8,128)(2,1)S(1)} all-to-all(bf16[16,128,128]{2,1,0:T(8,128)(2,1)S(1)} %shard_map.96), channel_id=1, replica_groups=mesh['groups'=2,'seq'=16] {'seq'}, dimensions={0} | all-to-all | bytes 1048576 | tf_op jit(solution)/shard_map/all_to_all | solution.py:130
  70.2 0.0 copy-done
  70.2 0.0 copy-start.3
  70.2 0.4 fusion
  70.6 3.2 %collective-permute-start.1 = (bf16[128,512]{1,0:T(8,128)(2,1)S(1)}, bf16[128,512]{1,0:T(8,128)(2,1)S(1)}, u32[]{:S(2)}, u32[]{:S(2)}) collective-permute-start(bf16[128,512]{1,0:T(8,128)(2,1)S(1)} %fusion), channel_id=1, source_target_pairs={{0,2},{1,3},{2,4},{3,5},{4,6},{5,7},{6,8},{7,9},{8,10},{9,11},{10,... | collective-permute-start | bytes 393224 | tf_op jit(solution)/shard_map/ppermute | solution.py:18
  73.8 1.9 %collective-permute-start = (bf16[128,512]{1,0:T(8,128)(2,1)S(1)}, bf16[128,512]{1,0:T(8,128)(2,1)S(1)}, u32[]{:S(2)}, u32[]{:S(2)}) collective-permute-start(bf16[128,512]{1,0:T(8,128)(2,1)S(1)} %fusion), channel_id=1, source_target_pairs={{0,1},{1,2},{2,3},{3,4},{4,5},{5,6},{6,7},{7,8},{8,9},{9,10},{10,1... | collective-permute-start | bytes 393224 | tf_op jit(solution)/shard_map/ppermute | solution.py:18
  75.8 0.0 copy-done.3
  75.8 1.8 %shard_map.97 = bf16[128,2048]{1,0:T(8,128)(2,1)} custom-call(bf16[16,128,128]{2,1,0:T(8,128)(2,1)} %copy-done.3), custom_call_target="tpu_custom_call" | custom-call | tf_op jit(solution)/shard_map/pallas_call | solution.py:107
  77.6 1.9 %collective-permute-done.1 = bf16[128,512]{1,0:T(8,128)(2,1)S(1)} collective-permute-done((bf16[128,512]{1,0:T(8,128)(2,1)S(1)}, bf16[128,512]{1,0:T(8,128)(2,1)S(1)}, u32[]{:S(2)}, u32[]{:S(2)}) %collective-permute-start.1) | collective-permute-done | bytes 131104 | tf_op jit(solution)/shard_map/ppermute | solution.py:18
  79.5 1.5 %collective-permute-done = bf16[128,512]{1,0:T(8,128)(2,1)S(1)} collective-permute-done((bf16[128,512]{1,0:T(8,128)(2,1)S(1)}, bf16[128,512]{1,0:T(8,128)(2,1)S(1)}, u32[]{:S(2)}, u32[]{:S(2)}) %collective-permute-start) | collective-permute-done | bytes 131104 | tf_op jit(solution)/shard_map/ppermute | solution.py:18
  81.0 0.0 copy-start.4
  81.0 1.9 %multiply_convert_fusion = bf16[128,512]{1,0:T(8,128)(2,1)S(1)} fusion(bf16[1536,512]{1,0:T(8,128)(2,1)} %bitcast.16, bf16[128,512]{1,0:T(8,128)(2,1)S(1)} %collective-permute-done.1, bf16[128,512]{1,0:T(8,128)(2,1)S(1)} %collective-permute-done, bf16[128,512]{1,0:T(8,128)(2,1)S(1)} %fusion), kind=kOutput, calls=%fused_computation.9 | convolution fusion | flops 202833920 | bytes 2097152 | tf_op jit(solution)/shard_map/dot_general | solution.py:142
  82.9 0.0 copy-done.4
  82.9 0.9 %convolution_convert_fusion = bf16[128,512]{1,0:T(8,128)(2,1)} fusion(bf16[128,512]{1,0:T(8,128)(2,1)S(1)} %multiply_convert_fusion, bf16[512,512]{1,0:T(8,128)(2,1)S(1)} %copy-done.4), kind=kOutput, calls=%fused_computation.1 | convolution fusion | flops 67174400 | bytes 786432 | tf_op jit(solution)/shard_map/dot_general | solution.py:144
Async XLA Ops:
  0.6 69.6 %copy-start = (bf16[2048,512]{1,0:T(8,128)(2,1)S(1)}, bf16[2048,512]{1,0:T(8,128)(2,1)}, u32[]{:S(2)}) copy-start(bf16[2048,512]{1,0:T(8,128)(2,1)} %param.13) | copy-start | bytes 6291460
  3.2 42.5 %copy-start.1 = (f32[128]{0:T(128)S(1)}, f32[128]{0:T(128)}, u32[]{:S(2)}) copy-start(f32[128]{0:T(128)} %param.11) | copy-start | bytes 1540
  3.2 42.5 %copy-start.2 = (f32[128]{0:T(128)S(1)}, f32[128]{0:T(128)}, u32[]{:S(2)}) copy-start(f32[128]{0:T(128)} %param.12) | copy-start | bytes 1540
  70.2 5.6 %copy-start.3 = (bf16[16,128,128]{2,1,0:T(8,128)(2,1)}, bf16[16,128,128]{2,1,0:T(8,128)(2,1)S(1)}, u32[]{:S(2)}) copy-start(bf16[16,128,128]{2,1,0:T(8,128)(2,1)S(1)} %all_to_all.11.b_ref) | copy-start | bytes 1572868
  70.6 8.9 %collective-permute-start.1 = (bf16[128,512]{1,0:T(8,128)(2,1)S(1)}, bf16[128,512]{1,0:T(8,128)(2,1)S(1)}, u32[]{:S(2)}, u32[]{:S(2)}) collective-permute-start(bf16[128,512]{1,0:T(8,128)(2,1)S(1)} %fusion), channel_id=1, source_target_pairs={{0,2},{1,3},{2,4},{3,5},{4,6},{5,7},{6,8},{7,9},{8,10},{9,11},{10,... | collective-permute-start | bytes 393224 | tf_op jit(solution)/shard_map/ppermute | solution.py:18
  73.8 7.2 %collective-permute-start = (bf16[128,512]{1,0:T(8,128)(2,1)S(1)}, bf16[128,512]{1,0:T(8,128)(2,1)S(1)}, u32[]{:S(2)}, u32[]{:S(2)}) collective-permute-start(bf16[128,512]{1,0:T(8,128)(2,1)S(1)} %fusion), channel_id=1, source_target_pairs={{0,1},{1,2},{2,3},{3,4},{4,5},{5,6},{6,7},{7,8},{8,9},{9,10},{10,1... | collective-permute-start | bytes 393224 | tf_op jit(solution)/shard_map/ppermute | solution.py:18
  81.0 1.9 %copy-start.4 = (bf16[512,512]{1,0:T(8,128)(2,1)S(1)}, bf16[512,512]{1,0:T(8,128)(2,1)}, u32[]{:S(2)}) copy-start(bf16[512,512]{1,0:T(8,128)(2,1)} %param.15) | copy-start | bytes 1572868

commit v11 on v8

--- a/solution.py
+++ b/solution.py
@@ -119,8 +119,13 @@
         "hrd,hdc->rc", back, w_latent.reshape(HEADS, HD, -1), preferred_element_type=jnp.float32
     ).astype(jnp.bfloat16)
     attention = jnp.transpose(back, (1, 0, 2)).reshape(rows, HEADS * HD)
-    earlier_one = passed_along(latent, "seq", 1)
-    earlier_two = passed_along(latent, "seq", 2)
+    peers = lax.axis_size("seq")
+    odd = lax.axis_index("seq") % 2 == 1
+    partner = lax.ppermute(latent, "seq", [(i, i ^ 1) for i in range(peers)])
+    pair = jnp.stack([jnp.where(odd, partner, latent), jnp.where(odd, latent, partner)])
+    prior = passed_along(pair, "seq", 2)
+    earlier_one = jnp.where(odd, partner, prior[1])
+    earlier_two = jnp.where(odd, prior[1], prior[0])
     taps = jnp.concatenate([latent, earlier_one, earlier_two], axis=1)
     state = jnp.dot(taps, w_temporal.reshape(-1, w_temporal.shape[2]), preferred_element_type=jnp.float32)
     act = lax.optimization_barrier(jax.nn.silu(state).astype(jnp.bfloat16))

time: 84.1 us -> 88.9 us (1.057)
  waiting for transfers between devices: 3.95 us -> 8.49 us
  other arithmetic: 0 us -> 1.74 us
  starting transfers between devices: 5.1 us -> 3.59 us
    ppermute x2 -> x1, waiting for transfers between devices: 3.95 us -> 7.5 us  [passed_along(): return lax.ppermute(shard, axis, pairs)]
    ppermute x2 -> x1, starting transfers between devices: 5.1 us -> 2.86 us  [passed_along(): return lax.ppermute(shard, axis, pairs)]
    select_n x0 -> x1, other arithmetic: none -> 0.99 us  [body(): earlier_one = jnp.where(odd, partner, prior[1])]
    ppermute x0 -> x1, waiting for transfers between devices: none -> 0.99 us  [body(): partner = lax.ppermute(latent, 'seq', [(i, i ^ 1) for i in range(peers)])]
  transfers between devices with their start and end apart: 2 -> 2, of which waited for: 2 -> 2; matrix products, arithmetic and copies ran while one was open for 2% -> 1% of each run, Pallas kernels for 0% -> 0%
where the time goes in v11:
time: 88.9 us; the launch traced here: 88.6 us
  blocking collectives  61 us (69%)
  Pallas kernels  8.55 us (10%)
  waiting for transfers between devices  8.49 us (10%)
  starting transfers between devices  3.59 us (4%)
  matrix products  3.21 us (4%)
  other arithmetic  1.74 us (2%)
  local copies, waits for them, and re-layouts  1.32 us (1%)
    all_to_all x1, blocking collectives, body(): lax.all_to_all(stacked, 'seq', split_axis=0, concat_axis=0, tiled=True)  42.5 us
    all_to_all x1, blocking collectives, body(): back = lax.all_to_all(out, 'seq', split_axis=0, concat_axis=0, tiled=True)  18.4 us
    ppermute x1, waiting for transfers between devices, passed_along(): return lax.ppermute(shard, axis, pairs)  7.5 us
    pallas_call x1, Pallas kernels, attend(): pl.pallas_call(_attn_kernel, out_shape=jax.ShapeDtypeStruct((span_blocks,...  6 us
    ppermute x1, starting transfers between devices, passed_along(): return lax.ppermute(shard, axis, pairs)  2.86 us
    pallas_call x1, Pallas kernels, pack(): pl.pallas_call(_pack_kernel, out_shape=jax.ShapeDtypeStruct((HEADS * copi...  2.56 us
    dot_general x1, matrix products, body(): jnp.dot(taps, w_temporal.reshape(-1, w_temporal.shape[2]), preferred_elem...  1.88 us
  transfers between devices with their start and end apart: 2, of which 2 were waited for; matrix products, arithmetic and copies ran while one was open for 1% of the time, Pallas kernels for 0%

profile of v11, /device:TPU:8, one launch (start us, length us, event | category | flops | bytes accessed | tf_op | source)
XLA Modules:
  0.0 88.6 jit_solution(1876830420437489747)
XLA Ops:
  0.6 0.0 copy-start
  0.6 2.6 %shard_map.95 = bf16[16,3,128,128]{3,2,1,0:T(8,128)(2,1)} custom-call(bf16[128,2048]{1,0:T(8,128)(2,1)} %q_ref.1, bf16[128,2048]{1,0:T(8,128)(2,1)} %k_ref.1, bf16[128,2048]{1,0:T(8,128)(2,1)} %v_ref.1), custom_call_target="tpu_custom_call" | custom-call | tf_op jit(solution)/shard_map/pallas_call | solution.py:90
  3.2 0.0 copy-start.1
  3.2 0.0 copy-start.2
  3.2 42.5 %all_to_all.10.q_ref.k_ref.v_ref = bf16[16,3,128,128]{3,2,1,0:T(8,128)(2,1)S(1)} all-to-all(bf16[16,3,128,128]{3,2,1,0:T(8,128)(2,1)} %shard_map.95), channel_id=1, replica_groups=mesh['groups'=2,'seq'=16] {'seq'}, dimensions={0} | all-to-all | bytes 3145728 | tf_op jit(solution)/shard_map/all_to_all | solution.py:105
  45.7 0.0 copy-done.1
  45.8 0.0 copy-done.2
  45.8 6.0 %shard_map.96 = bf16[16,128,128]{2,1,0:T(8,128)(2,1)S(1)} custom-call(s32[1]{0:T(128)} %constant.25.clone.1.share_ref, bf16[16,3,128,128]{3,2,1,0:T(8,128)(2,1)S(1)} %all_to_all.10.q_ref.k_ref.v_ref, bf16[16,3,128,128]{3,2,1,0:T(8,128)(2,1)S(1)} %all_to_all.10.q_ref.k_ref.v_ref, bf16[16,3,128,128]{3,2,1,0:T(8,128)(2,1)S(1)} %all_to_all.10.q_ref.k_ref.v_ref, ...), custom_call_target="tpu_custom_call" | custom-call | tf_op jit(solution)/shard_map/pallas_call | solution.py:55
  51.8 18.4 %all_to_all.11 = bf16[16,128,128]{2,1,0:T(8,128)(2,1)S(1)} all-to-all(bf16[16,128,128]{2,1,0:T(8,128)(2,1)S(1)} %shard_map.96), channel_id=1, replica_groups=mesh['groups'=2,'seq'=16] {'seq'}, dimensions={0} | all-to-all | bytes 1048576 | tf_op jit(solution)/shard_map/all_to_all | solution.py:113
  70.2 0.0 copy-done
  70.2 0.4 fusion
  70.6 0.7 collective-permute-start
  71.4 1.0 %collective-permute-done = bf16[128,512]{1,0:T(8,128)(2,1)S(1)} collective-permute-done((bf16[128,512]{1,0:T(8,128)(2,1)S(1)}, bf16[128,512]{1,0:T(8,128)(2,1)S(1)}, u32[]{:S(2)}, u32[]{:S(2)}) %collective-permute-start) | collective-permute-done | bytes 131104 | tf_op jit(solution)/shard_map/ppermute | solution.py:124
  72.4 0.7 pad_maximum_fusion
  73.1 2.9 %collective-permute-start.1 = (bf16[2,128,512]{2,1,0:T(8,128)(2,1)}, bf16[2,128,512]{2,1,0:T(8,128)(2,1)}, u32[]{:S(2)}, u32[]{:S(2)}) collective-permute-start(bf16[2,128,512]{2,1,0:T(8,128)(2,1)} %pad_maximum_fusion), channel_id=1, source_target_pairs={{0,2},{1,3},{2,4},{3,5},{4,6},{5,7},{6,8},{7,9},{8,10},{9,11},{10,... | collective-permute-start | bytes 786440 | tf_op jit(solution)/shard_map/ppermute | solution.py:18
  76.0 0.3 copy.10
  76.3 1.0 %copy.11 = bf16[128,2048]{1,0:T(8,128)(2,1)} copy(bf16[128,2048]{0,1:T(8,128)(2,1)S(1)} %bitcast.33) | data formatting | bytes 1048576
  77.3 7.5 %collective-permute-done.1 = bf16[2,128,512]{2,1,0:T(8,128)(2,1)} collective-permute-done((bf16[2,128,512]{2,1,0:T(8,128)(2,1)}, bf16[2,128,512]{2,1,0:T(8,128)(2,1)}, u32[]{:S(2)}, u32[]{:S(2)}) %collective-permute-start.1) | collective-permute-done | bytes 262176 | tf_op jit(solution)/shard_map/ppermute | solution.py:18
  84.8 1.0 %broadcast_select_fusion = (bf16[128,512]{1,0:T(8,128)(2,1)S(1)}, bf16[128,512]{1,0:T(8,128)(2,1)S(1)}) fusion(bf16[128,512]{1,0:T(8,128)(2,1)S(1)} %collective-permute-done, pred[]{:T(512)S(6)} %eq.6, bf16[2,128,512]{2,1,0:T(8,128)(2,1)} %collective-permute-done.1), kind=kLoop, calls=%fused_computation.16 | loop fusion | flops 131072 | bytes 655361 | tf_op jit(solution)/shard_map/jit(_where)/select_n | solution.py:127
  85.8 0.0 copy-start.3
  85.8 1.9 %multiply_convert_fusion = bf16[128,512]{1,0:T(8,128)(2,1)S(1)} fusion(bf16[1536,512]{1,0:T(8,128)(2,1)} %bitcast.34, bf16[128,512]{1,0:T(8,128)(2,1)S(1)} %get-tuple-element.5, bf16[128,512]{1,0:T(8,128)(2,1)S(1)} %get-tuple-element.4, bf16[128,512]{1,0:T(8,128)(2,1)S(1)} %fusion), kind=kOutput, calls=%fused_computation.10 | convolution fusion | flops 202833920 | bytes 2097152 | tf_op jit(solution)/shard_map/dot_general | solution.py:130
  87.7 0.0 copy-done.3
  87.7 0.9 %convolution_convert_fusion = bf16[128,512]{1,0:T(8,128)(2,1)} fusion(bf16[128,512]{1,0:T(8,128)(2,1)S(1)} %multiply_convert_fusion, bf16[512,512]{1,0:T(8,128)(2,1)S(1)} %copy-done.3), kind=kOutput, calls=%fused_computation.1 | convolution fusion | flops 67174400 | bytes 786432 | tf_op jit(solution)/shard_map/dot_general | solution.py:132
  (1 shorter events, 0.0 us)
Async XLA Ops:
  0.6 69.6 %copy-start = (bf16[2048,512]{1,0:T(8,128)(2,1)S(1)}, bf16[2048,512]{1,0:T(8,128)(2,1)}, u32[]{:S(2)}) copy-start(bf16[2048,512]{1,0:T(8,128)(2,1)} %param.13) | copy-start | bytes 6291460
  3.2 42.5 %copy-start.1 = (f32[128]{0:T(128)S(1)}, f32[128]{0:T(128)}, u32[]{:S(2)}) copy-start(f32[128]{0:T(128)} %param.11) | copy-start | bytes 1540
  3.2 42.5 %copy-start.2 = (f32[128]{0:T(128)S(1)}, f32[128]{0:T(128)}, u32[]{:S(2)}) copy-start(f32[128]{0:T(128)} %param.12) | copy-start | bytes 1540
  70.6 1.7 %collective-permute-start = (bf16[128,512]{1,0:T(8,128)(2,1)S(1)}, bf16[128,512]{1,0:T(8,128)(2,1)S(1)}, u32[]{:S(2)}, u32[]{:S(2)}) collective-permute-start(bf16[128,512]{1,0:T(8,128)(2,1)S(1)} %fusion), channel_id=1, source_target_pairs={{0,1},{1,0},{2,3},{3,2},{4,5},{5,4},{6,7},{7,6},{8,9},{9,8},{10,11... | collective-permute-start | bytes 393224 | tf_op jit(solution)/shard_map/ppermute | solution.py:124
  73.1 11.7 %collective-permute-start.1 = (bf16[2,128,512]{2,1,0:T(8,128)(2,1)}, bf16[2,128,512]{2,1,0:T(8,128)(2,1)}, u32[]{:S(2)}, u32[]{:S(2)}) collective-permute-start(bf16[2,128,512]{2,1,0:T(8,128)(2,1)} %pad_maximum_fusion), channel_id=1, source_target_pairs={{0,2},{1,3},{2,4},{3,5},{4,6},{5,7},{6,8},{7,9},{8,10},{9,11},{10,... | collective-permute-start | bytes 786440 | tf_op jit(solution)/shard_map/ppermute | solution.py:18
  85.8 1.9 %copy-start.3 = (bf16[512,512]{1,0:T(8,128)(2,1)S(1)}, bf16[512,512]{1,0:T(8,128)(2,1)}, u32[]{:S(2)}) copy-start(bf16[512,512]{1,0:T(8,128)(2,1)} %param.15) | copy-start | bytes 1572868

commit v12 on v6

--- a/solution.py
+++ b/solution.py
@@ -124,9 +124,9 @@
     state = jnp.dot(latent, w_temporal[0], preferred_element_type=jnp.float32)
     state = state + jnp.dot(earlier_one, w_temporal[1], preferred_element_type=jnp.float32)
     state = state + jnp.dot(earlier_two, w_temporal[2], preferred_element_type=jnp.float32)
-    act = lax.optimization_barrier(jax.nn.silu(state).astype(jnp.bfloat16))
-    decoded = jnp.dot(act, w_decode, preferred_element_type=jnp.float32)
-    return (attention, decoded.astype(jnp.bfloat16))
+    act = jax.nn.silu(state).astype(jnp.bfloat16)
+    decoded = jnp.dot(act, w_decode, preferred_element_type=jnp.float32).astype(jnp.bfloat16)
+    return (attention, decoded)
 
 
 def solution(mesh):

time: 85.2 us -> 85.1 us (level)
    dot_general x2 -> x1, matrix products: 2.21 us -> 2.15 us  [body(): jnp.dot(act, w_decode, preferred_element_type=jnp.float32)]
where the time goes in v12:
time: 85.1 us; the launch traced here: 84.5 us
  blocking collectives  61 us (72%)
  Pallas kernels  8.56 us (10%)
  matrix products  5.18 us (6%)
  starting transfers between devices  5.1 us (6%)
  waiting for transfers between devices  2.62 us (3%)
  local copies, waits for them, and re-layouts  1.31 us (2%)
    all_to_all x1, blocking collectives, body(): lax.all_to_all(stacked, 'seq', split_axis=0, concat_axis=0, tiled=True)  42.5 us
    all_to_all x1, blocking collectives, body(): back = lax.all_to_all(out, 'seq', split_axis=0, concat_axis=0, tiled=True)  18.4 us
    pallas_call x1, Pallas kernels, attend(): pl.pallas_call(_attn_kernel, out_shape=jax.ShapeDtypeStruct((span_blocks,...  5.99 us
    ppermute x2, starting transfers between devices, passed_along(): return lax.ppermute(shard, axis, pairs)  5.1 us
    ppermute x2, waiting for transfers between devices, passed_along(): return lax.ppermute(shard, axis, pairs)  2.62 us
    pallas_call x1, Pallas kernels, pack(): pl.pallas_call(_pack_kernel, out_shape=jax.ShapeDtypeStruct((HEADS * copi...  2.57 us
    dot_general x1, matrix products, body(): jnp.dot(act, w_decode, preferred_element_type=jnp.float32)  2.15 us
  transfers between devices with their start and end apart: 2, of which 1 were waited for; matrix products, arithmetic and copies ran while one was open for 5% of the time, Pallas kernels for 0%

profile of v12, /device:TPU:8, one launch (start us, length us, event | category | flops | bytes accessed | tf_op | source)
XLA Modules:
  0.0 84.5 jit_solution(14426934299438065571)
XLA Ops:
  0.6 0.0 copy-start
  0.6 2.6 %shard_map.95 = bf16[16,3,128,128]{3,2,1,0:T(8,128)(2,1)} custom-call(bf16[128,2048]{1,0:T(8,128)(2,1)} %q_ref.1, bf16[128,2048]{1,0:T(8,128)(2,1)} %k_ref.1, bf16[128,2048]{1,0:T(8,128)(2,1)} %v_ref.1), custom_call_target="tpu_custom_call" | custom-call | tf_op jit(solution)/shard_map/pallas_call | solution.py:90
  3.2 0.0 copy-start.1
  3.2 0.0 copy-start.2
  3.2 42.5 %all_to_all.10.q_ref.k_ref.v_ref = bf16[16,3,128,128]{3,2,1,0:T(8,128)(2,1)S(1)} all-to-all(bf16[16,3,128,128]{3,2,1,0:T(8,128)(2,1)} %shard_map.95), channel_id=1, replica_groups=mesh['groups'=2,'seq'=16] {'seq'}, dimensions={0} | all-to-all | bytes 3145728 | tf_op jit(solution)/shard_map/all_to_all | solution.py:105
  45.8 0.0 copy-done.1
  45.8 0.0 copy-done.2
  45.8 6.0 %shard_map.96 = bf16[16,128,128]{2,1,0:T(8,128)(2,1)S(1)} custom-call(s32[1]{0:T(128)} %constant.17.clone.1.share_ref, bf16[16,3,128,128]{3,2,1,0:T(8,128)(2,1)S(1)} %all_to_all.10.q_ref.k_ref.v_ref, bf16[16,3,128,128]{3,2,1,0:T(8,128)(2,1)S(1)} %all_to_all.10.q_ref.k_ref.v_ref, bf16[16,3,128,128]{3,2,1,0:T(8,128)(2,1)S(1)} %all_to_all.10.q_ref.k_ref.v_ref, ...), custom_call_target="tpu_custom_call" | custom-call | tf_op jit(solution)/shard_map/pallas_call | solution.py:55
  51.8 18.4 %all_to_all.11 = bf16[16,128,128]{2,1,0:T(8,128)(2,1)S(1)} all-to-all(bf16[16,128,128]{2,1,0:T(8,128)(2,1)S(1)} %shard_map.96), channel_id=1, replica_groups=mesh['groups'=2,'seq'=16] {'seq'}, dimensions={0} | all-to-all | bytes 1048576 | tf_op jit(solution)/shard_map/all_to_all | solution.py:113
  70.2 0.0 copy-done
  70.2 0.4 fusion
  70.6 3.2 %collective-permute-start.1 = (bf16[128,512]{1,0:T(8,128)(2,1)S(1)}, bf16[128,512]{1,0:T(8,128)(2,1)S(1)}, u32[]{:S(2)}, u32[]{:S(2)}) collective-permute-start(bf16[128,512]{1,0:T(8,128)(2,1)S(1)} %fusion), channel_id=1, source_target_pairs={{0,2},{1,3},{2,4},{3,5},{4,6},{5,7},{6,8},{7,9},{8,10},{9,11},{10,... | collective-permute-start | bytes 393224 | tf_op jit(solution)/shard_map/ppermute | solution.py:18
  73.8 1.9 %collective-permute-start = (bf16[128,512]{1,0:T(8,128)(2,1)S(1)}, bf16[128,512]{1,0:T(8,128)(2,1)S(1)}, u32[]{:S(2)}, u32[]{:S(2)}) collective-permute-start(bf16[128,512]{1,0:T(8,128)(2,1)S(1)} %fusion), channel_id=1, source_target_pairs={{0,1},{1,2},{2,3},{3,4},{4,5},{5,6},{6,7},{7,8},{8,9},{9,10},{10,1... | collective-permute-start | bytes 393224 | tf_op jit(solution)/shard_map/ppermute | solution.py:18
  75.8 0.3 copy.10
  76.1 1.0 %copy.11 = bf16[128,2048]{1,0:T(8,128)(2,1)} copy(bf16[128,2048]{0,1:T(8,128)(2,1)S(1)} %bitcast.32) | data formatting | bytes 1048576
  77.1 0.0 copy-start.3
  77.1 1.3 %fusion.3 = f32[128,512]{1,0:T(8,128)S(1)} fusion(bf16[128,512]{1,0:T(8,128)(2,1)S(1)} %fusion, bf16[3,512,512]{2,1,0:T(8,128)(2,1)} %param.14), kind=kOutput, calls=%fused_computation.7 | convolution fusion | flops 67108864 | bytes 917504 | tf_op jit(solution)/shard_map/dot_general | solution.py:124
  78.4 2.6 %collective-permute-done = bf16[128,512]{1,0:T(8,128)(2,1)S(1)} collective-permute-done((bf16[128,512]{1,0:T(8,128)(2,1)S(1)}, bf16[128,512]{1,0:T(8,128)(2,1)S(1)}, u32[]{:S(2)}, u32[]{:S(2)}) %collective-permute-start) | collective-permute-done | bytes 131104 | tf_op jit(solution)/shard_map/ppermute | solution.py:18
  81.0 1.3 %convolution_add_fusion.1 = f32[128,512]{1,0:T(8,128)S(1)} fusion(f32[128,512]{1,0:T(8,128)S(1)} %fusion.3, bf16[128,512]{1,0:T(8,128)(2,1)S(1)} %collective-permute-done, bf16[3,512,512]{2,1,0:T(8,128)(2,1)} %param.14), kind=kOutput, calls=%fused_computation.1 | convolution fusion | flops 67174400 | bytes 1179648 | tf_op jit(solution)/shard_map/dot_general | solution.py:125
  82.3 0.0 collective-permute-done.1
  82.3 0.0 copy-done.3
  82.3 2.1 %convolution_convert_fusion = bf16[128,512]{1,0:T(8,128)(2,1)} fusion(bf16[512,512]{1,0:T(8,128)(2,1)S(1)} %copy-done.3, f32[128,512]{1,0:T(8,128)S(1)} %convolution_add_fusion.1, bf16[128,512]{1,0:T(8,128)(2,1)S(1)} %collective-permute-done.1, bf16[3,512,512]{2,1,0:T(8,128)(2,1)} %param.14), kind=kOutput, calls=%fused_computation.3 | convolution fusion | flops 134676480 | bytes 1572864 | tf_op jit(solution)/shard_map/dot_general | solution.py:128
Async XLA Ops:
  0.6 69.6 %copy-start = (bf16[2048,512]{1,0:T(8,128)(2,1)S(1)}, bf16[2048,512]{1,0:T(8,128)(2,1)}, u32[]{:S(2)}) copy-start(bf16[2048,512]{1,0:T(8,128)(2,1)} %param.13) | copy-start | bytes 6291460
  3.2 42.5 %copy-start.1 = (f32[128]{0:T(128)S(1)}, f32[128]{0:T(128)}, u32[]{:S(2)}) copy-start(f32[128]{0:T(128)} %param.11) | copy-start | bytes 1540
  3.2 42.5 %copy-start.2 = (f32[128]{0:T(128)S(1)}, f32[128]{0:T(128)}, u32[]{:S(2)}) copy-start(f32[128]{0:T(128)} %param.12) | copy-start | bytes 1540
  70.6 11.7 %collective-permute-start.1 = (bf16[128,512]{1,0:T(8,128)(2,1)S(1)}, bf16[128,512]{1,0:T(8,128)(2,1)S(1)}, u32[]{:S(2)}, u32[]{:S(2)}) collective-permute-start(bf16[128,512]{1,0:T(8,128)(2,1)S(1)} %fusion), channel_id=1, source_target_pairs={{0,2},{1,3},{2,4},{3,5},{4,6},{5,7},{6,8},{7,9},{8,10},{9,11},{10,... | collective-permute-start | bytes 393224 | tf_op jit(solution)/shard_map/ppermute | solution.py:18
  73.8 7.2 %collective-permute-start = (bf16[128,512]{1,0:T(8,128)(2,1)S(1)}, bf16[128,512]{1,0:T(8,128)(2,1)S(1)}, u32[]{:S(2)}, u32[]{:S(2)}) collective-permute-start(bf16[128,512]{1,0:T(8,128)(2,1)S(1)} %fusion), channel_id=1, source_target_pairs={{0,1},{1,2},{2,3},{3,4},{4,5},{5,6},{6,7},{7,8},{8,9},{9,10},{10,1... | collective-permute-start | bytes 393224 | tf_op jit(solution)/shard_map/ppermute | solution.py:18
  77.1 5.2 %copy-start.3 = (bf16[512,512]{1,0:T(8,128)(2,1)S(1)}, bf16[512,512]{1,0:T(8,128)(2,1)}, u32[]{:S(2)}) copy-start(bf16[512,512]{1,0:T(8,128)(2,1)} %param.15) | copy-start | bytes 1572868

commit v13 on v8

--- a/solution.py
+++ b/solution.py
@@ -123,7 +123,7 @@
     earlier_two = passed_along(latent, "seq", 2)
     taps = jnp.concatenate([latent, earlier_one, earlier_two], axis=1)
     state = jnp.dot(taps, w_temporal.reshape(-1, w_temporal.shape[2]), preferred_element_type=jnp.float32)
-    act = lax.optimization_barrier(jax.nn.silu(state).astype(jnp.bfloat16))
+    act = jax.nn.silu(state).astype(jnp.bfloat16)
     decoded = jnp.dot(act, w_decode, preferred_element_type=jnp.float32).astype(jnp.bfloat16)
     return (attention, decoded)
 

time: 84.1 us -> 84.1 us (level)
    dot_general x1 -> x0, matrix products: 1.88 us -> none  [body(): jnp.dot(taps, w_temporal.reshape(-1, w_temporal.shape[2]), preferred_elem...]
    dot_general x1, matrix products: 0.89 us -> 2.76 us  [body(): jnp.dot(act, w_decode, preferred_element_type=jnp.float32)]
where the time goes in v13:
time: 84.1 us; the launch traced here: 83.8 us
  blocking collectives  61 us (73%)
  Pallas kernels  8.57 us (10%)
  starting transfers between devices  5.1 us (6%)
  waiting for transfers between devices  3.95 us (5%)
  matrix products  3.19 us (4%)
  local copies, waits for them, and re-layouts  1.31 us (2%)
    all_to_all x1, blocking collectives, body(): lax.all_to_all(stacked, 'seq', split_axis=0, concat_axis=0, tiled=True)  42.5 us
    all_to_all x1, blocking collectives, body(): back = lax.all_to_all(out, 'seq', split_axis=0, concat_axis=0, tiled=True)  18.4 us
    pallas_call x1, Pallas kernels, attend(): pl.pallas_call(_attn_kernel, out_shape=jax.ShapeDtypeStruct((span_blocks,...  6 us
    ppermute x2, starting transfers between devices, passed_along(): return lax.ppermute(shard, axis, pairs)  5.1 us
    ppermute x2, waiting for transfers between devices, passed_along(): return lax.ppermute(shard, axis, pairs)  3.95 us
    dot_general x1, matrix products, body(): jnp.dot(act, w_decode, preferred_element_type=jnp.float32)  2.76 us
    pallas_call x1, Pallas kernels, pack(): pl.pallas_call(_pack_kernel, out_shape=jax.ShapeDtypeStruct((HEADS * copi...  2.57 us
  transfers between devices with their start and end apart: 2, of which 2 were waited for; matrix products, arithmetic and copies ran while one was open for 2% of the time, Pallas kernels for 0%

profile of v13, /device:TPU:8, one launch (start us, length us, event | category | flops | bytes accessed | tf_op | source)
XLA Modules:
  0.0 83.8 jit_solution(8650205767137250680)
XLA Ops:
  0.6 0.0 copy-start
  0.6 2.6 %shard_map.95 = bf16[16,3,128,128]{3,2,1,0:T(8,128)(2,1)} custom-call(bf16[128,2048]{1,0:T(8,128)(2,1)} %q_ref.1, bf16[128,2048]{1,0:T(8,128)(2,1)} %k_ref.1, bf16[128,2048]{1,0:T(8,128)(2,1)} %v_ref.1), custom_call_target="tpu_custom_call" | custom-call | tf_op jit(solution)/shard_map/pallas_call | solution.py:90
  3.2 0.0 copy-start.1
  3.2 0.0 copy-start.2
  3.2 42.5 %all_to_all.10.q_ref.k_ref.v_ref = bf16[16,3,128,128]{3,2,1,0:T(8,128)(2,1)S(1)} all-to-all(bf16[16,3,128,128]{3,2,1,0:T(8,128)(2,1)} %shard_map.95), channel_id=1, replica_groups=mesh['groups'=2,'seq'=16] {'seq'}, dimensions={0} | all-to-all | bytes 3145728 | tf_op jit(solution)/shard_map/all_to_all | solution.py:105
  45.8 0.0 copy-done.1
  45.8 0.0 copy-done.2
  45.8 6.0 %shard_map.96 = bf16[16,128,128]{2,1,0:T(8,128)(2,1)S(1)} custom-call(s32[1]{0:T(128)} %constant.17.clone.1.share_ref, bf16[16,3,128,128]{3,2,1,0:T(8,128)(2,1)S(1)} %all_to_all.10.q_ref.k_ref.v_ref, bf16[16,3,128,128]{3,2,1,0:T(8,128)(2,1)S(1)} %all_to_all.10.q_ref.k_ref.v_ref, bf16[16,3,128,128]{3,2,1,0:T(8,128)(2,1)S(1)} %all_to_all.10.q_ref.k_ref.v_ref, ...), custom_call_target="tpu_custom_call" | custom-call | tf_op jit(solution)/shard_map/pallas_call | solution.py:55
  51.8 18.4 %all_to_all.11 = bf16[16,128,128]{2,1,0:T(8,128)(2,1)S(1)} all-to-all(bf16[16,128,128]{2,1,0:T(8,128)(2,1)S(1)} %shard_map.96), channel_id=1, replica_groups=mesh['groups'=2,'seq'=16] {'seq'}, dimensions={0} | all-to-all | bytes 1048576 | tf_op jit(solution)/shard_map/all_to_all | solution.py:113
  70.2 0.0 copy-done
  70.2 0.4 fusion
  70.7 3.2 %collective-permute-start.1 = (bf16[128,512]{1,0:T(8,128)(2,1)S(1)}, bf16[128,512]{1,0:T(8,128)(2,1)S(1)}, u32[]{:S(2)}, u32[]{:S(2)}) collective-permute-start(bf16[128,512]{1,0:T(8,128)(2,1)S(1)} %fusion), channel_id=1, source_target_pairs={{0,2},{1,3},{2,4},{3,5},{4,6},{5,7},{6,8},{7,9},{8,10},{9,11},{10,... | collective-permute-start | bytes 393224 | tf_op jit(solution)/shard_map/ppermute | solution.py:18
  73.8 1.9 %collective-permute-start = (bf16[128,512]{1,0:T(8,128)(2,1)S(1)}, bf16[128,512]{1,0:T(8,128)(2,1)S(1)}, u32[]{:S(2)}, u32[]{:S(2)}) collective-permute-start(bf16[128,512]{1,0:T(8,128)(2,1)S(1)} %fusion), channel_id=1, source_target_pairs={{0,1},{1,2},{2,3},{3,4},{4,5},{5,6},{6,7},{7,8},{8,9},{9,10},{10,1... | collective-permute-start | bytes 393224 | tf_op jit(solution)/shard_map/ppermute | solution.py:18
  75.8 0.3 copy.10
  76.1 1.0 %copy.11 = bf16[128,2048]{1,0:T(8,128)(2,1)} copy(bf16[128,2048]{0,1:T(8,128)(2,1)S(1)} %bitcast.18) | data formatting | bytes 1048576
  77.1 2.4 %collective-permute-done.1 = bf16[128,512]{1,0:T(8,128)(2,1)S(1)} collective-permute-done((bf16[128,512]{1,0:T(8,128)(2,1)S(1)}, bf16[128,512]{1,0:T(8,128)(2,1)S(1)}, u32[]{:S(2)}, u32[]{:S(2)}) %collective-permute-start.1) | collective-permute-done | bytes 131104 | tf_op jit(solution)/shard_map/ppermute | solution.py:18
  79.5 1.5 %collective-permute-done = bf16[128,512]{1,0:T(8,128)(2,1)S(1)} collective-permute-done((bf16[128,512]{1,0:T(8,128)(2,1)S(1)}, bf16[128,512]{1,0:T(8,128)(2,1)S(1)}, u32[]{:S(2)}, u32[]{:S(2)}) %collective-permute-start) | collective-permute-done | bytes 131104 | tf_op jit(solution)/shard_map/ppermute | solution.py:18
  81.0 2.8 %convolution_convert_fusion = bf16[128,512]{1,0:T(8,128)(2,1)} fusion(bf16[512,512]{1,0:T(8,128)(2,1)} %param.15, bf16[1536,512]{1,0:T(8,128)(2,1)} %bitcast.19, bf16[128,512]{1,0:T(8,128)(2,1)S(1)} %collective-permute-done.1, bf16[128,512]{1,0:T(8,128)(2,1)S(1)} %collective-permute-done, bf16[128,512]{1,0:T(8,128)(2,1)S(1)} %fusion), kind=kOutput, calls=%fused_computation.1 | convolution fusion | flops 270008320 | bytes 2621440 | tf_op jit(solution)/shard_map/dot_general | solution.py:127
Async XLA Ops:
  0.6 69.6 %copy-start = (bf16[2048,512]{1,0:T(8,128)(2,1)S(1)}, bf16[2048,512]{1,0:T(8,128)(2,1)}, u32[]{:S(2)}) copy-start(bf16[2048,512]{1,0:T(8,128)(2,1)} %param.13) | copy-start | bytes 6291460
  3.2 42.5 %copy-start.1 = (f32[128]{0:T(128)S(1)}, f32[128]{0:T(128)}, u32[]{:S(2)}) copy-start(f32[128]{0:T(128)} %param.11) | copy-start | bytes 1540
  3.2 42.5 %copy-start.2 = (f32[128]{0:T(128)S(1)}, f32[128]{0:T(128)}, u32[]{:S(2)}) copy-start(f32[128]{0:T(128)} %param.12) | copy-start | bytes 1540
  70.7 8.8 %collective-permute-start.1 = (bf16[128,512]{1,0:T(8,128)(2,1)S(1)}, bf16[128,512]{1,0:T(8,128)(2,1)S(1)}, u32[]{:S(2)}, u32[]{:S(2)}) collective-permute-start(bf16[128,512]{1,0:T(8,128)(2,1)S(1)} %fusion), channel_id=1, source_target_pairs={{0,2},{1,3},{2,4},{3,5},{4,6},{5,7},{6,8},{7,9},{8,10},{9,11},{10,... | collective-permute-start | bytes 393224 | tf_op jit(solution)/shard_map/ppermute | solution.py:18
  73.8 7.2 %collective-permute-start = (bf16[128,512]{1,0:T(8,128)(2,1)S(1)}, bf16[128,512]{1,0:T(8,128)(2,1)S(1)}, u32[]{:S(2)}, u32[]{:S(2)}) collective-permute-start(bf16[128,512]{1,0:T(8,128)(2,1)S(1)} %fusion), channel_id=1, source_target_pairs={{0,1},{1,2},{2,3},{3,4},{4,5},{5,6},{6,7},{7,8},{8,9},{9,10},{10,1... | collective-permute-start | bytes 393224 | tf_op jit(solution)/shard_map/ppermute | solution.py:18

commit v14 on v8

--- a/solution.py
+++ b/solution.py
@@ -39,7 +39,7 @@
     st = jnp.dot(kn_ref[...], qt, preferred_element_type=jnp.float32)
     c = math.log2(math.e) / math.sqrt(HD)
     m = jnp.max(st, axis=0, keepdims=True)
-    e = jnp.exp2(st * c - m * c)
+    e = jnp.exp2((st - m) * c)
     total = jnp.sum(e, axis=0, keepdims=True)
     out_t = jnp.dot(vt_ref[...], e.astype(jnp.bfloat16), preferred_element_type=jnp.float32)
     out = (out_t / total).T.astype(jnp.bfloat16)

time: 84.1 us -> 83.8 us (level)
  no operation moved by 1% of the time
where the time goes in v14:
time: 83.8 us; the launch traced here: 83.6 us
  blocking collectives  61 us (73%)
  Pallas kernels  8.29 us (10%)
  starting transfers between devices  5.1 us (6%)
  waiting for transfers between devices  3.96 us (5%)
  matrix products  3.21 us (4%)
  local copies, waits for them, and re-layouts  1.31 us (2%)
    all_to_all x1, blocking collectives, body(): lax.all_to_all(stacked, 'seq', split_axis=0, concat_axis=0, tiled=True)  42.5 us
    all_to_all x1, blocking collectives, body(): back = lax.all_to_all(out, 'seq', split_axis=0, concat_axis=0, tiled=True)  18.4 us
    pallas_call x1, Pallas kernels, attend(): pl.pallas_call(_attn_kernel, out_shape=jax.ShapeDtypeStruct((span_blocks,...  5.73 us
    ppermute x2, starting transfers between devices, passed_along(): return lax.ppermute(shard, axis, pairs)  5.1 us
    ppermute x2, waiting for transfers between devices, passed_along(): return lax.ppermute(shard, axis, pairs)  3.96 us
    pallas_call x1, Pallas kernels, pack(): pl.pallas_call(_pack_kernel, out_shape=jax.ShapeDtypeStruct((HEADS * copi...  2.57 us
    dot_general x1, matrix products, body(): jnp.dot(taps, w_temporal.reshape(-1, w_temporal.shape[2]), preferred_elem...  1.88 us
  transfers between devices with their start and end apart: 2, of which 2 were waited for; matrix products, arithmetic and copies ran while one was open for 2% of the time, Pallas kernels for 0%

profile of v14, /device:TPU:8, one launch (start us, length us, event | category | flops | bytes accessed | tf_op | source)
XLA Modules:
  0.0 83.6 jit_solution(9656068407322375000)
XLA Ops:
  0.6 0.0 copy-start
  0.6 2.6 %shard_map.95 = bf16[16,3,128,128]{3,2,1,0:T(8,128)(2,1)} custom-call(bf16[128,2048]{1,0:T(8,128)(2,1)} %q_ref.1, bf16[128,2048]{1,0:T(8,128)(2,1)} %k_ref.1, bf16[128,2048]{1,0:T(8,128)(2,1)} %v_ref.1), custom_call_target="tpu_custom_call" | custom-call | tf_op jit(solution)/shard_map/pallas_call | solution.py:90
  3.2 0.0 copy-start.1
  3.2 0.0 copy-start.2
  3.2 42.5 %all_to_all.10.q_ref.k_ref.v_ref = bf16[16,3,128,128]{3,2,1,0:T(8,128)(2,1)S(1)} all-to-all(bf16[16,3,128,128]{3,2,1,0:T(8,128)(2,1)} %shard_map.95), channel_id=1, replica_groups=mesh['groups'=2,'seq'=16] {'seq'}, dimensions={0} | all-to-all | bytes 3145728 | tf_op jit(solution)/shard_map/all_to_all | solution.py:105
  45.8 0.0 copy-done.1
  45.8 0.0 copy-done.2
  45.8 5.7 %shard_map.96 = bf16[16,128,128]{2,1,0:T(8,128)(2,1)S(1)} custom-call(s32[1]{0:T(128)} %constant.17.clone.1.share_ref, bf16[16,3,128,128]{3,2,1,0:T(8,128)(2,1)S(1)} %all_to_all.10.q_ref.k_ref.v_ref, bf16[16,3,128,128]{3,2,1,0:T(8,128)(2,1)S(1)} %all_to_all.10.q_ref.k_ref.v_ref, bf16[16,3,128,128]{3,2,1,0:T(8,128)(2,1)S(1)} %all_to_all.10.q_ref.k_ref.v_ref, ...), custom_call_target="tpu_custom_call" | custom-call | tf_op jit(solution)/shard_map/pallas_call | solution.py:55
  51.5 18.4 %all_to_all.11 = bf16[16,128,128]{2,1,0:T(8,128)(2,1)S(1)} all-to-all(bf16[16,128,128]{2,1,0:T(8,128)(2,1)S(1)} %shard_map.96), channel_id=1, replica_groups=mesh['groups'=2,'seq'=16] {'seq'}, dimensions={0} | all-to-all | bytes 1048576 | tf_op jit(solution)/shard_map/all_to_all | solution.py:113
  69.9 0.0 copy-done
  69.9 0.4 fusion
  70.4 3.2 %collective-permute-start.1 = (bf16[128,512]{1,0:T(8,128)(2,1)S(1)}, bf16[128,512]{1,0:T(8,128)(2,1)S(1)}, u32[]{:S(2)}, u32[]{:S(2)}) collective-permute-start(bf16[128,512]{1,0:T(8,128)(2,1)S(1)} %fusion), channel_id=1, source_target_pairs={{0,2},{1,3},{2,4},{3,5},{4,6},{5,7},{6,8},{7,9},{8,10},{9,11},{10,... | collective-permute-start | bytes 393224 | tf_op jit(solution)/shard_map/ppermute | solution.py:18
  73.6 1.9 %collective-permute-start = (bf16[128,512]{1,0:T(8,128)(2,1)S(1)}, bf16[128,512]{1,0:T(8,128)(2,1)S(1)}, u32[]{:S(2)}, u32[]{:S(2)}) collective-permute-start(bf16[128,512]{1,0:T(8,128)(2,1)S(1)} %fusion), channel_id=1, source_target_pairs={{0,1},{1,2},{2,3},{3,4},{4,5},{5,6},{6,7},{7,8},{8,9},{9,10},{10,1... | collective-permute-start | bytes 393224 | tf_op jit(solution)/shard_map/ppermute | solution.py:18
  75.5 0.3 copy.10
  75.8 1.0 %copy.11 = bf16[128,2048]{1,0:T(8,128)(2,1)} copy(bf16[128,2048]{0,1:T(8,128)(2,1)S(1)} %bitcast.19) | data formatting | bytes 1048576
  76.8 2.4 %collective-permute-done.1 = bf16[128,512]{1,0:T(8,128)(2,1)S(1)} collective-permute-done((bf16[128,512]{1,0:T(8,128)(2,1)S(1)}, bf16[128,512]{1,0:T(8,128)(2,1)S(1)}, u32[]{:S(2)}, u32[]{:S(2)}) %collective-permute-start.1) | collective-permute-done | bytes 131104 | tf_op jit(solution)/shard_map/ppermute | solution.py:18
  79.2 1.5 %collective-permute-done = bf16[128,512]{1,0:T(8,128)(2,1)S(1)} collective-permute-done((bf16[128,512]{1,0:T(8,128)(2,1)S(1)}, bf16[128,512]{1,0:T(8,128)(2,1)S(1)}, u32[]{:S(2)}, u32[]{:S(2)}) %collective-permute-start) | collective-permute-done | bytes 131104 | tf_op jit(solution)/shard_map/ppermute | solution.py:18
  80.8 0.0 copy-start.3
  80.8 1.9 %multiply_convert_fusion = bf16[128,512]{1,0:T(8,128)(2,1)S(1)} fusion(bf16[1536,512]{1,0:T(8,128)(2,1)} %bitcast.20, bf16[128,512]{1,0:T(8,128)(2,1)S(1)} %collective-permute-done.1, bf16[128,512]{1,0:T(8,128)(2,1)S(1)} %collective-permute-done, bf16[128,512]{1,0:T(8,128)(2,1)S(1)} %fusion), kind=kOutput, calls=%fused_computation.9 | convolution fusion | flops 202833920 | bytes 2097152 | tf_op jit(solution)/shard_map/dot_general | solution.py:125
  82.7 0.0 copy-done.3
  82.7 0.9 %convolution_convert_fusion = bf16[128,512]{1,0:T(8,128)(2,1)} fusion(bf16[128,512]{1,0:T(8,128)(2,1)S(1)} %multiply_convert_fusion, bf16[512,512]{1,0:T(8,128)(2,1)S(1)} %copy-done.3), kind=kOutput, calls=%fused_computation.1 | convolution fusion | flops 67174400 | bytes 786432 | tf_op jit(solution)/shard_map/dot_general | solution.py:127
Async XLA Ops:
  0.6 69.3 %copy-start = (bf16[2048,512]{1,0:T(8,128)(2,1)S(1)}, bf16[2048,512]{1,0:T(8,128)(2,1)}, u32[]{:S(2)}) copy-start(bf16[2048,512]{1,0:T(8,128)(2,1)} %param.13) | copy-start | bytes 6291460
  3.2 42.5 %copy-start.1 = (f32[128]{0:T(128)S(1)}, f32[128]{0:T(128)}, u32[]{:S(2)}) copy-start(f32[128]{0:T(128)} %param.11) | copy-start | bytes 1540
  3.2 42.5 %copy-start.2 = (f32[128]{0:T(128)S(1)}, f32[128]{0:T(128)}, u32[]{:S(2)}) copy-start(f32[128]{0:T(128)} %param.12) | copy-start | bytes 1540
  70.4 8.9 %collective-permute-start.1 = (bf16[128,512]{1,0:T(8,128)(2,1)S(1)}, bf16[128,512]{1,0:T(8,128)(2,1)S(1)}, u32[]{:S(2)}, u32[]{:S(2)}) collective-permute-start(bf16[128,512]{1,0:T(8,128)(2,1)S(1)} %fusion), channel_id=1, source_target_pairs={{0,2},{1,3},{2,4},{3,5},{4,6},{5,7},{6,8},{7,9},{8,10},{9,11},{10,... | collective-permute-start | bytes 393224 | tf_op jit(solution)/shard_map/ppermute | solution.py:18
  73.6 7.2 %collective-permute-start = (bf16[128,512]{1,0:T(8,128)(2,1)S(1)}, bf16[128,512]{1,0:T(8,128)(2,1)S(1)}, u32[]{:S(2)}, u32[]{:S(2)}) collective-permute-start(bf16[128,512]{1,0:T(8,128)(2,1)S(1)} %fusion), channel_id=1, source_target_pairs={{0,1},{1,2},{2,3},{3,4},{4,5},{5,6},{6,7},{7,8},{8,9},{9,10},{10,1... | collective-permute-start | bytes 393224 | tf_op jit(solution)/shard_map/ppermute | solution.py:18
  80.8 1.9 %copy-start.3 = (bf16[512,512]{1,0:T(8,128)(2,1)S(1)}, bf16[512,512]{1,0:T(8,128)(2,1)}, u32[]{:S(2)}) copy-start(bf16[512,512]{1,0:T(8,128)(2,1)} %param.15) | copy-start | bytes 1572868

commit v15 on v14

--- a/solution.py
+++ b/solution.py
@@ -35,7 +35,9 @@
 
     q = q_ref[...]
     q = q.reshape(q.shape[0] * q.shape[1], HD)
-    qt = _norm(q, gq_ref[...]).T
+    qt = q.T.astype(jnp.float32)
+    qt = qt * lax.rsqrt(jnp.mean(qt * qt, axis=0, keepdims=True) + EPS) * gq_ref[...].T
+    qt = qt.astype(jnp.bfloat16)
     st = jnp.dot(kn_ref[...], qt, preferred_element_type=jnp.float32)
     c = math.log2(math.e) / math.sqrt(HD)
     m = jnp.max(st, axis=0, keepdims=True)

time: 83.8 us -> 83.7 us (level)
  no operation moved by 1% of the time
where the time goes in v15:
time: 83.7 us; the launch traced here: 83.4 us
  blocking collectives  61 us (73%)
  Pallas kernels  8.17 us (10%)
  starting transfers between devices  5.09 us (6%)
  waiting for transfers between devices  3.96 us (5%)
  matrix products  3.22 us (4%)
  local copies, waits for them, and re-layouts  1.31 us (2%)
    all_to_all x1, blocking collectives, body(): lax.all_to_all(stacked, 'seq', split_axis=0, concat_axis=0, tiled=True)  42.5 us
    all_to_all x1, blocking collectives, body(): back = lax.all_to_all(out, 'seq', split_axis=0, concat_axis=0, tiled=True)  18.4 us
    pallas_call x1, Pallas kernels, attend(): pl.pallas_call(_attn_kernel, out_shape=jax.ShapeDtypeStruct((span_blocks,...  5.6 us
    ppermute x2, starting transfers between devices, passed_along(): return lax.ppermute(shard, axis, pairs)  5.09 us
    ppermute x2, waiting for transfers between devices, passed_along(): return lax.ppermute(shard, axis, pairs)  3.96 us
    pallas_call x1, Pallas kernels, pack(): pl.pallas_call(_pack_kernel, out_shape=jax.ShapeDtypeStruct((HEADS * copi...  2.57 us
    dot_general x1, matrix products, body(): jnp.dot(taps, w_temporal.reshape(-1, w_temporal.shape[2]), preferred_elem...  1.88 us
  transfers between devices with their start and end apart: 2, of which 2 were waited for; matrix products, arithmetic and copies ran while one was open for 2% of the time, Pallas kernels for 0%

profile of v15, /device:TPU:8, one launch (start us, length us, event | category | flops | bytes accessed | tf_op | source)
XLA Modules:
  0.0 83.4 jit_solution(8463528961305951416)
XLA Ops:
  0.6 0.0 copy-start
  0.6 2.6 %shard_map.95 = bf16[16,3,128,128]{3,2,1,0:T(8,128)(2,1)} custom-call(bf16[128,2048]{1,0:T(8,128)(2,1)} %q_ref.1, bf16[128,2048]{1,0:T(8,128)(2,1)} %k_ref.1, bf16[128,2048]{1,0:T(8,128)(2,1)} %v_ref.1), custom_call_target="tpu_custom_call" | custom-call | tf_op jit(solution)/shard_map/pallas_call | solution.py:92
  3.2 0.0 copy-start.1
  3.2 0.0 copy-start.2
  3.2 42.5 %all_to_all.10.q_ref.k_ref.v_ref = bf16[16,3,128,128]{3,2,1,0:T(8,128)(2,1)S(1)} all-to-all(bf16[16,3,128,128]{3,2,1,0:T(8,128)(2,1)} %shard_map.95), channel_id=1, replica_groups=mesh['groups'=2,'seq'=16] {'seq'}, dimensions={0} | all-to-all | bytes 3145728 | tf_op jit(solution)/shard_map/all_to_all | solution.py:107
  45.8 0.0 copy-done.1
  45.8 0.0 copy-done.2
  45.8 5.6 %shard_map.96 = bf16[16,128,128]{2,1,0:T(8,128)(2,1)S(1)} custom-call(s32[1]{0:T(128)} %constant.17.clone.1.share_ref, bf16[16,3,128,128]{3,2,1,0:T(8,128)(2,1)S(1)} %all_to_all.10.q_ref.k_ref.v_ref, bf16[16,3,128,128]{3,2,1,0:T(8,128)(2,1)S(1)} %all_to_all.10.q_ref.k_ref.v_ref, bf16[16,3,128,128]{3,2,1,0:T(8,128)(2,1)S(1)} %all_to_all.10.q_ref.k_ref.v_ref, ...), custom_call_target="tpu_custom_call" | custom-call | tf_op jit(solution)/shard_map/pallas_call | solution.py:57
  51.4 18.4 %all_to_all.11 = bf16[16,128,128]{2,1,0:T(8,128)(2,1)S(1)} all-to-all(bf16[16,128,128]{2,1,0:T(8,128)(2,1)S(1)} %shard_map.96), channel_id=1, replica_groups=mesh['groups'=2,'seq'=16] {'seq'}, dimensions={0} | all-to-all | bytes 1048576 | tf_op jit(solution)/shard_map/all_to_all | solution.py:115
  69.8 0.0 copy-done
  69.8 0.4 fusion
  70.3 3.2 %collective-permute-start.1 = (bf16[128,512]{1,0:T(8,128)(2,1)S(1)}, bf16[128,512]{1,0:T(8,128)(2,1)S(1)}, u32[]{:S(2)}, u32[]{:S(2)}) collective-permute-start(bf16[128,512]{1,0:T(8,128)(2,1)S(1)} %fusion), channel_id=1, source_target_pairs={{0,2},{1,3},{2,4},{3,5},{4,6},{5,7},{6,8},{7,9},{8,10},{9,11},{10,... | collective-permute-start | bytes 393224 | tf_op jit(solution)/shard_map/ppermute | solution.py:18
  73.4 1.9 %collective-permute-start = (bf16[128,512]{1,0:T(8,128)(2,1)S(1)}, bf16[128,512]{1,0:T(8,128)(2,1)S(1)}, u32[]{:S(2)}, u32[]{:S(2)}) collective-permute-start(bf16[128,512]{1,0:T(8,128)(2,1)S(1)} %fusion), channel_id=1, source_target_pairs={{0,1},{1,2},{2,3},{3,4},{4,5},{5,6},{6,7},{7,8},{8,9},{9,10},{10,1... | collective-permute-start | bytes 393224 | tf_op jit(solution)/shard_map/ppermute | solution.py:18
  75.4 0.3 copy.10
  75.7 1.0 %copy.11 = bf16[128,2048]{1,0:T(8,128)(2,1)} copy(bf16[128,2048]{0,1:T(8,128)(2,1)S(1)} %bitcast.19) | data formatting | bytes 1048576
  76.7 2.4 %collective-permute-done.1 = bf16[128,512]{1,0:T(8,128)(2,1)S(1)} collective-permute-done((bf16[128,512]{1,0:T(8,128)(2,1)S(1)}, bf16[128,512]{1,0:T(8,128)(2,1)S(1)}, u32[]{:S(2)}, u32[]{:S(2)}) %collective-permute-start.1) | collective-permute-done | bytes 131104 | tf_op jit(solution)/shard_map/ppermute | solution.py:18
  79.1 1.5 %collective-permute-done = bf16[128,512]{1,0:T(8,128)(2,1)S(1)} collective-permute-done((bf16[128,512]{1,0:T(8,128)(2,1)S(1)}, bf16[128,512]{1,0:T(8,128)(2,1)S(1)}, u32[]{:S(2)}, u32[]{:S(2)}) %collective-permute-start) | collective-permute-done | bytes 131104 | tf_op jit(solution)/shard_map/ppermute | solution.py:18
  80.6 0.0 copy-start.3
  80.6 1.9 %multiply_convert_fusion = bf16[128,512]{1,0:T(8,128)(2,1)S(1)} fusion(bf16[1536,512]{1,0:T(8,128)(2,1)} %bitcast.20, bf16[128,512]{1,0:T(8,128)(2,1)S(1)} %collective-permute-done.1, bf16[128,512]{1,0:T(8,128)(2,1)S(1)} %collective-permute-done, bf16[128,512]{1,0:T(8,128)(2,1)S(1)} %fusion), kind=kOutput, calls=%fused_computation.9 | convolution fusion | flops 202833920 | bytes 2097152 | tf_op jit(solution)/shard_map/dot_general | solution.py:127
  82.5 0.0 copy-done.3
  82.5 0.9 %convolution_convert_fusion = bf16[128,512]{1,0:T(8,128)(2,1)} fusion(bf16[128,512]{1,0:T(8,128)(2,1)S(1)} %multiply_convert_fusion, bf16[512,512]{1,0:T(8,128)(2,1)S(1)} %copy-done.3), kind=kOutput, calls=%fused_computation.1 | convolution fusion | flops 67174400 | bytes 786432 | tf_op jit(solution)/shard_map/dot_general | solution.py:129
Async XLA Ops:
  0.6 69.2 %copy-start = (bf16[2048,512]{1,0:T(8,128)(2,1)S(1)}, bf16[2048,512]{1,0:T(8,128)(2,1)}, u32[]{:S(2)}) copy-start(bf16[2048,512]{1,0:T(8,128)(2,1)} %param.13) | copy-start | bytes 6291460
  3.2 42.5 %copy-start.1 = (f32[128]{0:T(128)S(1)}, f32[128]{0:T(128)}, u32[]{:S(2)}) copy-start(f32[128]{0:T(128)} %param.11) | copy-start | bytes 1540
  3.2 42.5 %copy-start.2 = (f32[128]{0:T(128)S(1)}, f32[128]{0:T(128)}, u32[]{:S(2)}) copy-start(f32[128]{0:T(128)} %param.12) | copy-start | bytes 1540
  70.3 8.8 %collective-permute-start.1 = (bf16[128,512]{1,0:T(8,128)(2,1)S(1)}, bf16[128,512]{1,0:T(8,128)(2,1)S(1)}, u32[]{:S(2)}, u32[]{:S(2)}) collective-permute-start(bf16[128,512]{1,0:T(8,128)(2,1)S(1)} %fusion), channel_id=1, source_target_pairs={{0,2},{1,3},{2,4},{3,5},{4,6},{5,7},{6,8},{7,9},{8,10},{9,11},{10,... | collective-permute-start | bytes 393224 | tf_op jit(solution)/shard_map/ppermute | solution.py:18
  73.4 7.2 %collective-permute-start = (bf16[128,512]{1,0:T(8,128)(2,1)S(1)}, bf16[128,512]{1,0:T(8,128)(2,1)S(1)}, u32[]{:S(2)}, u32[]{:S(2)}) collective-permute-start(bf16[128,512]{1,0:T(8,128)(2,1)S(1)} %fusion), channel_id=1, source_target_pairs={{0,1},{1,2},{2,3},{3,4},{4,5},{5,6},{6,7},{7,8},{8,9},{9,10},{10,1... | collective-permute-start | bytes 393224 | tf_op jit(solution)/shard_map/ppermute | solution.py:18
  80.6 1.9 %copy-start.3 = (bf16[512,512]{1,0:T(8,128)(2,1)S(1)}, bf16[512,512]{1,0:T(8,128)(2,1)}, u32[]{:S(2)}) copy-start(bf16[512,512]{1,0:T(8,128)(2,1)} %param.15) | copy-start | bytes 1572868

commit v16 on v15

--- a/solution.py
+++ b/solution.py
@@ -120,7 +120,7 @@
     latent = jnp.einsum(
         "hrd,hdc->rc", back, w_latent.reshape(HEADS, HD, -1), preferred_element_type=jnp.float32
     ).astype(jnp.bfloat16)
-    attention = jnp.transpose(back, (1, 0, 2)).reshape(rows, HEADS * HD)
+    attention = jnp.concatenate([back[h] for h in range(HEADS)], axis=1)
     earlier_one = passed_along(latent, "seq", 1)
     earlier_two = passed_along(latent, "seq", 2)
     taps = jnp.concatenate([latent, earlier_one, earlier_two], axis=1)

time: 83.7 us -> 83 us (level)
  matrix products: 3.22 us -> 1.74 us
  waiting for transfers between devices: 3.96 us -> 4.95 us
    dot_general x1, matrix products: 1.88 us -> 0.42 us  [body(): jnp.dot(taps, w_temporal.reshape(-1, w_temporal.shape[2]), preferred_elem...]
    ppermute x2, waiting for transfers between devices: 3.96 us -> 4.95 us  [passed_along(): return lax.ppermute(shard, axis, pairs)]
  transfers between devices with their start and end apart: 2 -> 2, of which waited for: 2 -> 2; matrix products, arithmetic and copies ran while one was open for 2% -> 0% of each run, Pallas kernels for 0% -> 0%
where the time goes in v16:
time: 83 us; the launch traced here: 82.7 us
  blocking collectives  61 us (73%)
  Pallas kernels  8.16 us (10%)
  starting transfers between devices  5.24 us (6%)
  waiting for transfers between devices  4.95 us (6%)
  matrix products  1.74 us (2%)
  local copies, waits for them, and re-layouts  0.85 us (1%)
    all_to_all x1, blocking collectives, body(): lax.all_to_all(stacked, 'seq', split_axis=0, concat_axis=0, tiled=True)  42.5 us
    all_to_all x1, blocking collectives, body(): back = lax.all_to_all(out, 'seq', split_axis=0, concat_axis=0, tiled=True)  18.4 us
    pallas_call x1, Pallas kernels, attend(): pl.pallas_call(_attn_kernel, out_shape=jax.ShapeDtypeStruct((span_blocks,...  5.61 us
    ppermute x2, starting transfers between devices, passed_along(): return lax.ppermute(shard, axis, pairs)  5.24 us
    ppermute x2, waiting for transfers between devices, passed_along(): return lax.ppermute(shard, axis, pairs)  4.95 us
    pallas_call x1, Pallas kernels, pack(): pl.pallas_call(_pack_kernel, out_shape=jax.ShapeDtypeStruct((HEADS * copi...  2.56 us
  transfers between devices with their start and end apart: 2, of which 2 were waited for; matrix products, arithmetic and copies ran while one was open for 0% of the time, Pallas kernels for 0%

profile of v16, /device:TPU:8, one launch (start us, length us, event | category | flops | bytes accessed | tf_op | source)
XLA Modules:
  0.0 82.7 jit_solution(17957320887778403336)
XLA Ops:
  0.6 0.0 copy-start
  0.6 2.6 %shard_map.95 = bf16[16,3,128,128]{3,2,1,0:T(8,128)(2,1)} custom-call(bf16[128,2048]{1,0:T(8,128)(2,1)} %q_ref.1, bf16[128,2048]{1,0:T(8,128)(2,1)} %k_ref.1, bf16[128,2048]{1,0:T(8,128)(2,1)} %v_ref.1), custom_call_target="tpu_custom_call" | custom-call | tf_op jit(solution)/shard_map/pallas_call | solution.py:92
  3.2 0.0 copy-start.1
  3.2 0.0 copy-start.2
  3.2 42.5 %all_to_all.10.q_ref.k_ref.v_ref = bf16[16,3,128,128]{3,2,1,0:T(8,128)(2,1)S(1)} all-to-all(bf16[16,3,128,128]{3,2,1,0:T(8,128)(2,1)} %shard_map.95), channel_id=1, replica_groups=mesh['groups'=2,'seq'=16] {'seq'}, dimensions={0} | all-to-all | bytes 3145728 | tf_op jit(solution)/shard_map/all_to_all | solution.py:107
  45.7 0.0 copy-done.1
  45.8 0.0 copy-done.2
  45.8 5.6 %shard_map.96 = bf16[16,128,128]{2,1,0:T(8,128)(2,1)S(1)} custom-call(s32[1]{0:T(128)} %constant.17.clone.1.share_ref, bf16[16,3,128,128]{3,2,1,0:T(8,128)(2,1)S(1)} %all_to_all.10.q_ref.k_ref.v_ref, bf16[16,3,128,128]{3,2,1,0:T(8,128)(2,1)S(1)} %all_to_all.10.q_ref.k_ref.v_ref, bf16[16,3,128,128]{3,2,1,0:T(8,128)(2,1)S(1)} %all_to_all.10.q_ref.k_ref.v_ref, ...), custom_call_target="tpu_custom_call" | custom-call | tf_op jit(solution)/shard_map/pallas_call | solution.py:57
  51.4 18.4 %all_to_all.11 = bf16[16,128,128]{2,1,0:T(8,128)(2,1)S(1)} all-to-all(bf16[16,128,128]{2,1,0:T(8,128)(2,1)S(1)} %shard_map.96), channel_id=1, replica_groups=mesh['groups'=2,'seq'=16] {'seq'}, dimensions={0} | all-to-all | bytes 1048576 | tf_op jit(solution)/shard_map/all_to_all | solution.py:115
  69.8 0.0 copy-done
  69.8 0.0 copy-start.5
  69.8 0.4 fusion
  70.2 3.3 %collective-permute-start.1 = (bf16[128,512]{1,0:T(8,128)(2,1)S(1)}, bf16[128,512]{1,0:T(8,128)(2,1)S(1)}, u32[]{:S(2)}, u32[]{:S(2)}) collective-permute-start(bf16[128,512]{1,0:T(8,128)(2,1)S(1)} %fusion), channel_id=1, source_target_pairs={{0,2},{1,3},{2,4},{3,5},{4,6},{5,7},{6,8},{7,9},{8,10},{9,11},{10,... | collective-permute-start | bytes 393224 | tf_op jit(solution)/shard_map/ppermute | solution.py:18
  73.6 1.9 %collective-permute-start = (bf16[128,512]{1,0:T(8,128)(2,1)S(1)}, bf16[128,512]{1,0:T(8,128)(2,1)S(1)}, u32[]{:S(2)}, u32[]{:S(2)}) collective-permute-start(bf16[128,512]{1,0:T(8,128)(2,1)S(1)} %fusion), channel_id=1, source_target_pairs={{0,1},{1,2},{2,3},{3,4},{4,5},{5,6},{6,7},{7,8},{8,9},{9,10},{10,1... | collective-permute-start | bytes 393224 | tf_op jit(solution)/shard_map/ppermute | solution.py:18
  75.8 0.0 copy-start.4
  75.8 3.3 %collective-permute-done.1 = bf16[128,512]{1,0:T(8,128)(2,1)S(1)} collective-permute-done((bf16[128,512]{1,0:T(8,128)(2,1)S(1)}, bf16[128,512]{1,0:T(8,128)(2,1)S(1)}, u32[]{:S(2)}, u32[]{:S(2)}) %collective-permute-start.1) | collective-permute-done | bytes 131104 | tf_op jit(solution)/shard_map/ppermute | solution.py:18
  79.1 1.6 %collective-permute-done = bf16[128,512]{1,0:T(8,128)(2,1)S(1)} collective-permute-done((bf16[128,512]{1,0:T(8,128)(2,1)S(1)}, bf16[128,512]{1,0:T(8,128)(2,1)S(1)}, u32[]{:S(2)}, u32[]{:S(2)}) %collective-permute-start) | collective-permute-done | bytes 131104 | tf_op jit(solution)/shard_map/ppermute | solution.py:18
  80.8 0.0 copy-done.5
  80.8 0.0 copy-start.3
  80.8 0.4 multiply_convert_fusion
  81.2 0.0 copy-done.4
  81.2 0.6 copy-done.3
  81.8 0.9 %convolution_convert_fusion = bf16[128,512]{1,0:T(8,128)(2,1)} fusion(bf16[128,512]{1,0:T(8,128)(2,1)S(1)} %multiply_convert_fusion, bf16[512,512]{1,0:T(8,128)(2,1)S(1)} %copy-done.3), kind=kOutput, calls=%fused_computation.1 | convolution fusion | flops 67174400 | bytes 786432 | tf_op jit(solution)/shard_map/dot_general | solution.py:129
  (16 shorter events, 0.2 us)
Async XLA Ops:
  0.6 69.2 %copy-start = (bf16[2048,512]{1,0:T(8,128)(2,1)S(1)}, bf16[2048,512]{1,0:T(8,128)(2,1)}, u32[]{:S(2)}) copy-start(bf16[2048,512]{1,0:T(8,128)(2,1)} %param.13) | copy-start | bytes 6291460
  3.2 42.5 %copy-start.1 = (f32[128]{0:T(128)S(1)}, f32[128]{0:T(128)}, u32[]{:S(2)}) copy-start(f32[128]{0:T(128)} %param.11) | copy-start | bytes 1540
  3.2 42.5 %copy-start.2 = (f32[128]{0:T(128)S(1)}, f32[128]{0:T(128)}, u32[]{:S(2)}) copy-start(f32[128]{0:T(128)} %param.12) | copy-start | bytes 1540
  69.8 11.0 %copy-start.5 = (bf16[3,512,512]{2,1,0:T(8,128)(2,1)S(1)}, bf16[3,512,512]{2,1,0:T(8,128)(2,1)}, u32[]{:S(2)}) copy-start(bf16[3,512,512]{2,1,0:T(8,128)(2,1)} %param.14) | copy-start | bytes 4718596
  70.2 8.9 %collective-permute-start.1 = (bf16[128,512]{1,0:T(8,128)(2,1)S(1)}, bf16[128,512]{1,0:T(8,128)(2,1)S(1)}, u32[]{:S(2)}, u32[]{:S(2)}) collective-permute-start(bf16[128,512]{1,0:T(8,128)(2,1)S(1)} %fusion), channel_id=1, source_target_pairs={{0,2},{1,3},{2,4},{3,5},{4,6},{5,7},{6,8},{7,9},{8,10},{9,11},{10,... | collective-permute-start | bytes 393224 | tf_op jit(solution)/shard_map/ppermute | solution.py:18
  73.6 7.2 %collective-permute-start = (bf16[128,512]{1,0:T(8,128)(2,1)S(1)}, bf16[128,512]{1,0:T(8,128)(2,1)S(1)}, u32[]{:S(2)}, u32[]{:S(2)}) collective-permute-start(bf16[128,512]{1,0:T(8,128)(2,1)S(1)} %fusion), channel_id=1, source_target_pairs={{0,1},{1,2},{2,3},{3,4},{4,5},{5,6},{6,7},{7,8},{8,9},{9,10},{10,1... | collective-permute-start | bytes 393224 | tf_op jit(solution)/shard_map/ppermute | solution.py:18
  75.8 5.4 %copy-start.4 = (bf16[128,2048]{1,0:T(8,128)(2,1)}, bf16[128,2048]{1,0:T(8,128)(2,1)S(1)}, u32[]{:S(2)}) copy-start(bf16[128,2048]{1,0:T(8,128)(2,1)S(1)} %constant_dynamic-update-slice_fusion) | copy-start | bytes 1572868
  80.8 1.0 %copy-start.3 = (bf16[512,512]{1,0:T(8,128)(2,1)S(1)}, bf16[512,512]{1,0:T(8,128)(2,1)}, u32[]{:S(2)}) copy-start(bf16[512,512]{1,0:T(8,128)(2,1)} %param.15) | copy-start | bytes 1572868

commit v17 on v16

--- a/solution.py
+++ b/solution.py
@@ -123,8 +123,9 @@
     attention = jnp.concatenate([back[h] for h in range(HEADS)], axis=1)
     earlier_one = passed_along(latent, "seq", 1)
     earlier_two = passed_along(latent, "seq", 2)
-    taps = jnp.concatenate([latent, earlier_one, earlier_two], axis=1)
-    state = jnp.dot(taps, w_temporal.reshape(-1, w_temporal.shape[2]), preferred_element_type=jnp.float32)
+    state = jnp.dot(latent, w_temporal[0], preferred_element_type=jnp.float32)
+    state = state + jnp.dot(earlier_one, w_temporal[1], preferred_element_type=jnp.float32)
+    state = state + jnp.dot(earlier_two, w_temporal[2], preferred_element_type=jnp.float32)
     act = lax.optimization_barrier(jax.nn.silu(state).astype(jnp.bfloat16))
     decoded = jnp.dot(act, w_decode, preferred_element_type=jnp.float32).astype(jnp.bfloat16)
     return (attention, decoded)

time: 83 us -> 82.5 us (level)
  transfers between devices with their start and end apart: 2 -> 2, of which waited for: 2 -> 1; matrix products, arithmetic and copies ran while one was open for 0% -> 1% of each run, Pallas kernels for 0% -> 0%
where the time goes in v17:
time: 82.5 us; the launch traced here: 82.2 us
  blocking collectives  61 us (74%)
  Pallas kernels  8.16 us (10%)
  starting transfers between devices  5.24 us (6%)
  waiting for transfers between devices  4.7 us (6%)
  matrix products  2.06 us (2%)
    all_to_all x1, blocking collectives, body(): lax.all_to_all(stacked, 'seq', split_axis=0, concat_axis=0, tiled=True)  42.5 us
    all_to_all x1, blocking collectives, body(): back = lax.all_to_all(out, 'seq', split_axis=0, concat_axis=0, tiled=True)  18.4 us
    pallas_call x1, Pallas kernels, attend(): pl.pallas_call(_attn_kernel, out_shape=jax.ShapeDtypeStruct((span_blocks,...  5.61 us
    ppermute x2, starting transfers between devices, passed_along(): return lax.ppermute(shard, axis, pairs)  5.24 us
    ppermute x2, waiting for transfers between devices, passed_along(): return lax.ppermute(shard, axis, pairs)  4.7 us
    pallas_call x1, Pallas kernels, pack(): pl.pallas_call(_pack_kernel, out_shape=jax.ShapeDtypeStruct((HEADS * copi...  2.56 us
  transfers between devices with their start and end apart: 2, of which 1 were waited for; matrix products, arithmetic and copies ran while one was open for 1% of the time, Pallas kernels for 0%

profile of v17, /device:TPU:8, one launch (start us, length us, event | category | flops | bytes accessed | tf_op | source)
XLA Modules:
  0.0 82.2 jit_solution(346125680196406653)
XLA Ops:
  0.6 0.0 copy-start
  0.6 2.6 %shard_map.95 = bf16[16,3,128,128]{3,2,1,0:T(8,128)(2,1)} custom-call(bf16[128,2048]{1,0:T(8,128)(2,1)} %q_ref.1, bf16[128,2048]{1,0:T(8,128)(2,1)} %k_ref.1, bf16[128,2048]{1,0:T(8,128)(2,1)} %v_ref.1), custom_call_target="tpu_custom_call" | custom-call | tf_op jit(solution)/shard_map/pallas_call | solution.py:92
  3.2 0.0 copy-start.1
  3.2 0.0 copy-start.2
  3.2 42.5 %all_to_all.10.q_ref.k_ref.v_ref = bf16[16,3,128,128]{3,2,1,0:T(8,128)(2,1)S(1)} all-to-all(bf16[16,3,128,128]{3,2,1,0:T(8,128)(2,1)} %shard_map.95), channel_id=1, replica_groups=mesh['groups'=2,'seq'=16] {'seq'}, dimensions={0} | all-to-all | bytes 3145728 | tf_op jit(solution)/shard_map/all_to_all | solution.py:107
  45.7 0.0 copy-done.1
  45.8 0.0 copy-done.2
  45.8 5.6 %shard_map.96 = bf16[16,128,128]{2,1,0:T(8,128)(2,1)S(1)} custom-call(s32[1]{0:T(128)} %constant.17.clone.1.share_ref, bf16[16,3,128,128]{3,2,1,0:T(8,128)(2,1)S(1)} %all_to_all.10.q_ref.k_ref.v_ref, bf16[16,3,128,128]{3,2,1,0:T(8,128)(2,1)S(1)} %all_to_all.10.q_ref.k_ref.v_ref, bf16[16,3,128,128]{3,2,1,0:T(8,128)(2,1)S(1)} %all_to_all.10.q_ref.k_ref.v_ref, ...), custom_call_target="tpu_custom_call" | custom-call | tf_op jit(solution)/shard_map/pallas_call | solution.py:57
  51.4 18.4 %all_to_all.11 = bf16[16,128,128]{2,1,0:T(8,128)(2,1)S(1)} all-to-all(bf16[16,128,128]{2,1,0:T(8,128)(2,1)S(1)} %shard_map.96), channel_id=1, replica_groups=mesh['groups'=2,'seq'=16] {'seq'}, dimensions={0} | all-to-all | bytes 1048576 | tf_op jit(solution)/shard_map/all_to_all | solution.py:115
  69.8 0.0 copy-done
  69.8 0.0 copy-start.3
  69.8 0.4 fusion
  70.2 3.3 %collective-permute-start.1 = (bf16[128,512]{1,0:T(8,128)(2,1)S(1)}, bf16[128,512]{1,0:T(8,128)(2,1)S(1)}, u32[]{:S(2)}, u32[]{:S(2)}) collective-permute-start(bf16[128,512]{1,0:T(8,128)(2,1)S(1)} %fusion), channel_id=1, source_target_pairs={{0,2},{1,3},{2,4},{3,5},{4,6},{5,7},{6,8},{7,9},{8,10},{9,11},{10,... | collective-permute-start | bytes 393224 | tf_op jit(solution)/shard_map/ppermute | solution.py:18
  73.6 1.9 %collective-permute-start = (bf16[128,512]{1,0:T(8,128)(2,1)S(1)}, bf16[128,512]{1,0:T(8,128)(2,1)S(1)}, u32[]{:S(2)}, u32[]{:S(2)}) collective-permute-start(bf16[128,512]{1,0:T(8,128)(2,1)S(1)} %fusion), channel_id=1, source_target_pairs={{0,1},{1,2},{2,3},{3,4},{4,5},{5,6},{6,7},{7,8},{8,9},{9,10},{10,1... | collective-permute-start | bytes 393224 | tf_op jit(solution)/shard_map/ppermute | solution.py:18
  75.5 0.0 copy-done.3
  75.5 0.2 fusion.3
  76.0 0.0 copy-start.5
  76.0 0.0 copy-start.4
  76.1 4.7 %collective-permute-done = bf16[128,512]{1,0:T(8,128)(2,1)S(1)} collective-permute-done((bf16[128,512]{1,0:T(8,128)(2,1)S(1)}, bf16[128,512]{1,0:T(8,128)(2,1)S(1)}, u32[]{:S(2)}, u32[]{:S(2)}) %collective-permute-start) | collective-permute-done | bytes 131104 | tf_op jit(solution)/shard_map/ppermute | solution.py:18
  80.8 0.2 convolution_add_fusion.1
  81.0 0.0 collective-permute-done.1
  81.0 0.3 multiply_convert_fusion
  81.3 0.0 copy-done.5
  81.3 0.0 copy-done.4
  81.3 0.9 %convolution_convert_fusion = bf16[128,512]{1,0:T(8,128)(2,1)} fusion(bf16[128,512]{1,0:T(8,128)(2,1)S(1)} %multiply_convert_fusion, bf16[512,512]{1,0:T(8,128)(2,1)S(1)} %copy-done.4), kind=kOutput, calls=%fused_computation.3 | convolution fusion | flops 67174400 | bytes 786432 | tf_op jit(solution)/shard_map/dot_general | solution.py:130
  (16 shorter events, 0.2 us)
Async XLA Ops:
  0.6 69.2 %copy-start = (bf16[2048,512]{1,0:T(8,128)(2,1)S(1)}, bf16[2048,512]{1,0:T(8,128)(2,1)}, u32[]{:S(2)}) copy-start(bf16[2048,512]{1,0:T(8,128)(2,1)} %param.13) | copy-start | bytes 6291460
  3.2 42.5 %copy-start.1 = (f32[128]{0:T(128)S(1)}, f32[128]{0:T(128)}, u32[]{:S(2)}) copy-start(f32[128]{0:T(128)} %param.11) | copy-start | bytes 1540
  3.2 42.5 %copy-start.2 = (f32[128]{0:T(128)S(1)}, f32[128]{0:T(128)}, u32[]{:S(2)}) copy-start(f32[128]{0:T(128)} %param.12) | copy-start | bytes 1540
  69.8 5.7 %copy-start.3 = (bf16[3,512,512]{2,1,0:T(8,128)(2,1)S(1)}, bf16[3,512,512]{2,1,0:T(8,128)(2,1)}, u32[]{:S(2)}) copy-start(bf16[3,512,512]{2,1,0:T(8,128)(2,1)} %param.14) | copy-start | bytes 4718596
  70.2 10.8 %collective-permute-start.1 = (bf16[128,512]{1,0:T(8,128)(2,1)S(1)}, bf16[128,512]{1,0:T(8,128)(2,1)S(1)}, u32[]{:S(2)}, u32[]{:S(2)}) collective-permute-start(bf16[128,512]{1,0:T(8,128)(2,1)S(1)} %fusion), channel_id=1, source_target_pairs={{0,2},{1,3},{2,4},{3,5},{4,6},{5,7},{6,8},{7,9},{8,10},{9,11},{10,... | collective-permute-start | bytes 393224 | tf_op jit(solution)/shard_map/ppermute | solution.py:18
  73.6 7.2 %collective-permute-start = (bf16[128,512]{1,0:T(8,128)(2,1)S(1)}, bf16[128,512]{1,0:T(8,128)(2,1)S(1)}, u32[]{:S(2)}, u32[]{:S(2)}) collective-permute-start(bf16[128,512]{1,0:T(8,128)(2,1)S(1)} %fusion), channel_id=1, source_target_pairs={{0,1},{1,2},{2,3},{3,4},{4,5},{5,6},{6,7},{7,8},{8,9},{9,10},{10,1... | collective-permute-start | bytes 393224 | tf_op jit(solution)/shard_map/ppermute | solution.py:18
  76.0 5.3 %copy-start.5 = (bf16[128,2048]{1,0:T(8,128)(2,1)}, bf16[128,2048]{1,0:T(8,128)(2,1)S(1)}, u32[]{:S(2)}) copy-start(bf16[128,2048]{1,0:T(8,128)(2,1)S(1)} %constant_dynamic-update-slice_fusion) | copy-start | bytes 1572868
  76.0 5.3 %copy-start.4 = (bf16[512,512]{1,0:T(8,128)(2,1)S(1)}, bf16[512,512]{1,0:T(8,128)(2,1)}, u32[]{:S(2)}) copy-start(bf16[512,512]{1,0:T(8,128)(2,1)} %param.15) | copy-start | bytes 1572868
